TPU v7x, 512 devices: a whole 4x8x8 slice. The times are simulated.
512 devices in a mesh: ctx: 64 (over x, y, core), head: 8 (over z).
Axes of the slice: x: 4, y: 8, z: 8, core: 2. Of those that a mesh axis runs over, the one named last changes fastest.
Arguments:
- query_rows: bfloat16 [65536, 1024], P(('ctx', 'head')), may hold values from -6 to 6
- key_rows: bfloat16 [65536, 1024], P(('ctx', 'head')), may hold values from -6 to 6
- value_rows: bfloat16 [65536, 2048], P(('ctx', 'head')), may hold values from -6 to 6
- gate_rows: bfloat16 [65536, 2048], P(('ctx', 'head')), may hold values from -6 to 6
- log_decay: bfloat16 [65536, 16], P(('ctx', 'head')), may hold values from -0.8 to 0, as said below
- write_strength: bfloat16 [65536, 16], P(('ctx', 'head')), may hold values from 0 to 1, as said below
- conv_query: bfloat16 [4, 1024], P(None, 'head'), may hold values from -3 to 3
- conv_key: bfloat16 [4, 1024], P(None, 'head'), may hold values from -3 to 3
- conv_value: bfloat16 [4, 2048], P(None, 'head'), may hold values from -3 to 3
- norm_gain: float32 [128], replicated, may hold values from 0.1 to 1.9
Outputs:
- layer_out: bfloat16 [65536, 2048], P(('ctx', 'head'))
Inputs may be any that keep to these rules, and one draw needn't show every extreme that they name: log_decay holds natural logarithms of decay factors. write_strength lies strictly between 0 and 1.
All inputs are finite; a program needn't handle non-finite values.
Results may differ from a plain program's by a relative error of at most 0.001.
Values may be sent and summed in bfloat16 or wider, within the bound.
A program may use at most 128 MiB of HBM per device.

v0:
```python
import jax
import jax.numpy as jnp
from jax import lax
from jax.sharding import PartitionSpec as P

DK = 128
DV = 128
HK = 8
HV = 16
BLOCK = 64


HIGHEST_PRECISION = lax.Precision.HIGHEST
EPSILON = 1e-06


def passed_along(value, axis, steps):
    count = lax.axis_size(axis)
    leading, last = (max(0, -steps), min(count, count - steps))
    return lax.ppermute(value, axis, [(source, source + steps) for source in range(leading, last)])


def forward_substitution(coupling, targets):
    return lax.linalg.triangular_solve(
        coupling,
        targets,
        left_side=True,
        lower=True,
        transpose_a=False,
        conjugate_a=False,
        unit_diagonal=True,
    )


def causal_conv(inputs, earlier_rows, weights):
    kernel_width = weights.shape[0]
    count_rows = inputs.shape[0]
    joined = jnp.concatenate([earlier_rows, inputs], axis=0)
    result = joined[kernel_width - 1 :] * weights[kernel_width - 1]
    for offset in range(1, kernel_width):
        result = (
            result
            + joined[kernel_width - 1 - offset : kernel_width - 1 - offset + count_rows]
            * weights[kernel_width - 1 - offset]
        )
    return jax.nn.silu(result)


def unit_heads(mixed, heads):
    shaped = mixed.reshape(mixed.shape[0], heads, -1)
    return shaped / jnp.sqrt(jnp.sum(shaped * shaped, axis=-1, keepdims=True) + EPSILON)


def into_blocks(array, block_len):
    count_rows, heads, inner_dim = array.shape
    return array.reshape(count_rows // block_len, block_len, heads, inner_dim).transpose(0, 2, 1, 3)


def block_scalars(array, block_len):
    count_rows, heads = array.shape
    return (
        array.astype(jnp.float32)
        .reshape(count_rows // block_len, block_len, heads)
        .transpose(0, 2, 1)
    )


def block_terms(queries, keys, values, log_gate, strength):
    block_len = queries.shape[2]
    key_dim = keys.shape[-1]
    cumulative = jnp.cumsum(log_gate, axis=-1)
    rows_index = jnp.arange(block_len)[:, None]
    cols_index = jnp.arange(block_len)[None, :]
    causal = rows_index >= cols_index
    strictly = rows_index > cols_index
    spread = jnp.where(causal, cumulative[..., :, None] - cumulative[..., None, :], 0.0)
    decays = jnp.where(causal, jnp.exp(spread), 0.0)
    key_key = jnp.einsum("nhid,nhjd->nhij", keys, keys, precision=HIGHEST_PRECISION)
    coupling = jnp.where(strictly, strength[..., None] * decays * key_key, 0.0)
    targets = jnp.concatenate(
        [(strength * jnp.exp(cumulative))[..., None] * keys, strength[..., None] * values], axis=-1
    )
    solved = forward_substitution(coupling, targets)
    key_part = solved[..., :key_dim]
    value_part = solved[..., key_dim:]
    query_key = jnp.einsum("nhid,nhjd->nhij", queries, keys, precision=HIGHEST_PRECISION)
    within = query_key * decays
    query_decay = jnp.exp(cumulative)[..., None] * queries
    closing_logarithm = cumulative[..., -1:]
    key_decay = jnp.exp(closing_logarithm - cumulative)[..., None] * keys
    end_decay = jnp.exp(closing_logarithm[..., 0])
    return (key_part, value_part, within, query_decay, key_decay, end_decay)


def block_apply(memory, pieces):
    key_part, value_part, within, query_decay, key_decay, end_decay = pieces
    corrected = value_part - jnp.einsum(
        "hcd,hde->hce", key_part, memory, precision=HIGHEST_PRECISION
    )
    result = jnp.einsum("hcd,hde->hce", query_decay, memory, precision=HIGHEST_PRECISION)
    result = result + jnp.einsum("hij,hje->hie", within, corrected, precision=HIGHEST_PRECISION)
    memory = end_decay[:, None, None] * memory + jnp.einsum(
        "hcd,hce->hde", key_decay, corrected, precision=HIGHEST_PRECISION
    )
    return (memory, result)


def gated_norm(outputs, gate, gain):
    meansq = jnp.mean(outputs * outputs, axis=-1, keepdims=True)
    scaled = outputs / jnp.sqrt(meansq + EPSILON) * gain * jax.nn.silu(gate)
    return scaled.astype(jnp.bfloat16).reshape(outputs.shape[0], -1)


def compose_maps(later_map, earlier_map):
    return jnp.einsum("hij,hjk->hik", later_map, earlier_map, precision=HIGHEST_PRECISION)


def on_device(
    query_rows,
    key_rows,
    value_rows,
    gate_rows,
    log_decay,
    write_strength,
    conv_query,
    conv_key,
    conv_value,
    norm_gain,
):
    device_query, local_key, local_value, local_gate, local_decay, local_strength = (
        lax.all_to_all(query_rows, "head", split_axis=1, concat_axis=0, tiled=True),
        lax.all_to_all(key_rows, "head", split_axis=1, concat_axis=0, tiled=True),
        lax.all_to_all(value_rows, "head", split_axis=1, concat_axis=0, tiled=True),
        lax.all_to_all(gate_rows, "head", split_axis=1, concat_axis=0, tiled=True),
        lax.all_to_all(log_decay, "head", split_axis=1, concat_axis=0, tiled=True),
        lax.all_to_all(write_strength, "head", split_axis=1, concat_axis=0, tiled=True),
    )
    joined = jnp.concatenate([device_query, local_key, local_value], axis=1)
    kernel_width = conv_query.shape[0]
    count_rows = joined.shape[0]
    tail_rows = passed_along(joined[count_rows - (kernel_width - 1) :], "ctx", 1)
    weights_all = jnp.concatenate([conv_query, conv_key, conv_value], axis=1).astype(jnp.float32)
    mixed = causal_conv(joined.astype(jnp.float32), tail_rows.astype(jnp.float32), weights_all)
    key_width = device_query.shape[1]
    head_keys = key_width // DK
    per_key = HV // HK
    query_heads = jnp.repeat(
        unit_heads(mixed[:, :key_width], head_keys) * DK ** (-0.5), per_key, axis=1
    )
    key_heads = jnp.repeat(
        unit_heads(mixed[:, key_width : 2 * key_width], head_keys), per_key, axis=1
    )
    value_heads = mixed[:, 2 * key_width :].reshape(count_rows, -1, DV)
    terms = block_terms(
        into_blocks(query_heads, BLOCK),
        into_blocks(key_heads, BLOCK),
        into_blocks(value_heads, BLOCK),
        block_scalars(local_decay, BLOCK),
        block_scalars(local_strength, BLOCK),
    )
    key_part, value_part, within, query_decay, key_decay, end_decay = terms
    heads_here = key_part.shape[1]
    identity_mat = jnp.broadcast_to(jnp.eye(DK, dtype=jnp.float32), (heads_here, DK, DK))
    trans_blocks = end_decay[..., None, None] * identity_mat - jnp.einsum(
        "nhcd,nhce->nhde", key_decay, key_part, precision=HIGHEST_PRECISION
    )
    bias_blocks = jnp.einsum("nhcd,nhce->nhde", key_decay, value_part, precision=HIGHEST_PRECISION)
    blank_state = jnp.zeros((heads_here, DK, DV), jnp.float32)

    def merge_transitions(carry, pieces):
        trans_all, bias_all = carry
        trans_one, bias_one = pieces
        return (
            (compose_maps(trans_one, trans_all), compose_maps(trans_one, bias_all) + bias_one),
            None,
        )

    block_trans, block_bias = lax.scan(
        merge_transitions, (identity_mat, blank_state), (trans_blocks, bias_blocks)
    )[0]

    def advance(iteration, initial):
        ending = compose_maps(block_trans, initial) + block_bias
        return passed_along(ending, "ctx", 1)

    initial = lax.fori_loop(0, lax.axis_size("ctx") - 1, advance, blank_state)
    produced = lax.scan(block_apply, initial, terms)[1]
    outputs = produced.transpose(0, 2, 1, 3).reshape(count_rows, heads_here, DV)
    gate = local_gate.astype(jnp.float32).reshape(count_rows, heads_here, DV)
    normed = gated_norm(outputs, gate, norm_gain)
    return lax.all_to_all(normed, "head", split_axis=0, concat_axis=1, tiled=True)


def solution(mesh):
    in_specs = (
        P(("ctx", "head"), None),
        P(("ctx", "head"), None),
        P(("ctx", "head"), None),
        P(("ctx", "head"), None),
        P(("ctx", "head"), None),
        P(("ctx", "head"), None),
        P(None, "head"),
        P(None, "head"),
        P(None, "head"),
        P(),
    )
    out_specs = P(("ctx", "head"), None)
    return jax.shard_map(
        on_device, mesh=mesh, in_specs=in_specs, out_specs=out_specs, check_vma=False
    )
```

profile of v0, /device:TPU:6, one launch (start us, length us, event | category | flops | bytes accessed | tf_op | source)
XLA Modules:
  0.0 957.7 jit_solution(8045039109217462826)
XLA Ops:
  0.0 18.1 %all_to_all.112 = bf16[128,8,2]{0,2,1:T(2,128)(2,1)S(1)} all-to-all(bf16[128,8,2]{0,2,1:T(2,128)(2,1)} %bitcast.157), channel_id=1, replica_groups=mesh['ctx'=64,'head'=8] {'head'}, dimensions={1} | all-to-all | bytes 8192 | tf_op jit(solution)/shard_map/all_to_all | solution.py:135
  34.2 8.6 all-to-all-done.1
  47.2 9.3 all-to-all-done.2
  62.7 10.6 %all-to-all-done.3 = bf16[128,8,256]{0,2,1:T(8,128)(2,1)S(1)} async-done(((bf16[128,8,256]{0,2,1:T(8,128)(2,1)}), bf16[128,8,256]{0,2,1:T(8,128)(2,1)S(1)}, u32[]{:S(2)}, u32[]{:S(2)}) %all-to-all-start.3) | async-done | bytes 524320 | tf_op jit(solution)/shard_map/all_to_all | solution.py:133
  94.2 158.0 %custom-call.3 = f32[16,2,1,64,64]{3,4,2,1,0:T(8,128)} custom-call(f32[16,2,1,64,64]{4,3,2,1,0:T(8,128)S(1)} %fusion.42), custom_call_target="InvertDiagBlocksLowerTriangular" | custom-call | tf_op jit(solution)/shard_map/triangular_solve | solution.py:24
  268.8 40.0 %while.37 = (s32[]{:T(128)}, f32[2,128,128]{2,1,0:T(8,128)S(1)}, f32[2,128,128]{2,1,0:T(8,128)S(1)}, f32[16,2,128,128]{3,2,1,0:T(8,128)}, f32[16,2,128,128]{3,2,1,0:T(8,128)}, /*index=5*/s32[]{:T(128)}, s32[]{:T(128)}) while((s32[]{:T(128)}, f32[2,128,128]{2,1,0:T(8,128)S(1)}, f32[2,128,128]{2,1,0:T(8,128)S(1)}, ...), condition=%wide.region_3.4_spmd.clone, body=%wide.region_2.3_spmd.clone.sunk | while | flops 100728832 | bytes 1443415 | solution.py:178
  312.8 546.3 %while.35 = (s32[]{:T(128)}, f32[2,128,128]{2,1,0:T(8,128)S(1)}, f32[2,128,128]{2,1,0:T(8,128)S(1)}, f32[2,128,128]{2,1,0:T(8,128)S(1)}, s32[]{:T(128)}) while((s32[]{:T(128)}, f32[2,128,128]{2,1,0:T(8,128)S(1)}, f32[2,128,128]{2,1,0:T(8,128)S(1)}, f32[2,128,128]{2,1,0:T(8,128)S(1)}, s32[]{:T(128)}) %tuple.70), condition=%wide.region_5.6_spmd, body=%wide.region_4.5_spmd.sunk | while | flops 50364416 | bytes 1048677 | solution.py:186
  315.1 6.5 collective-permute-done
  323.7 6.5 collective-permute-done
  332.4 6.5 collective-permute-done
  341.1 6.5 collective-permute-done
  349.8 6.5 collective-permute-done
  358.4 6.5 collective-permute-done
  367.1 6.5 collective-permute-done
  375.8 6.5 collective-permute-done
  384.4 6.5 collective-permute-done
  393.1 6.5 collective-permute-done
  401.8 6.5 collective-permute-done
  410.4 6.5 collective-permute-done
  419.1 6.5 collective-permute-done
  427.8 6.5 collective-permute-done
  436.5 6.5 collective-permute-done
  445.1 6.5 collective-permute-done
  453.8 6.5 collective-permute-done
  462.5 6.5 collective-permute-done
  471.1 6.5 collective-permute-done
  479.8 6.5 collective-permute-done
  488.5 6.5 collective-permute-done
  497.2 6.5 collective-permute-done
  505.8 6.5 collective-permute-done
  514.5 6.5 collective-permute-done
  523.2 6.5 collective-permute-done
  531.8 6.5 collective-permute-done
  540.5 6.5 collective-permute-done
  549.2 6.5 collective-permute-done
  557.9 6.5 collective-permute-done
  566.5 6.5 collective-permute-done
  575.2 6.5 collective-permute-done
  583.9 6.5 collective-permute-done
  592.5 6.5 collective-permute-done
  601.2 6.5 collective-permute-done
  609.9 6.5 collective-permute-done
  618.5 6.5 collective-permute-done
  627.2 6.5 collective-permute-done
  635.9 6.5 collective-permute-done
  644.6 6.5 collective-permute-done
  653.2 6.5 collective-permute-done
  661.9 6.5 collective-permute-done
  670.6 6.5 collective-permute-done
  679.2 6.5 collective-permute-done
  687.9 6.5 collective-permute-done
  696.6 6.5 collective-permute-done
  705.3 6.5 collective-permute-done
  713.9 6.5 collective-permute-done
  731.3 6.5 collective-permute-done
  739.9 6.5 collective-permute-done
  757.3 6.5 collective-permute-done
  783.3 6.5 collective-permute-done
  809.3 6.5 collective-permute-done
  826.6 6.5 collective-permute-done
  835.3 6.5 collective-permute-done
  852.7 6.5 collective-permute-done
  859.1 72.6 %while.36 = (s32[]{:T(128)}, f32[2,128,128]{2,1,0:T(8,128)S(1)}, f32[16,2,64,128]{3,2,1,0:T(8,128)S(1)}, f32[16,2]{1,0:T(8,128)S(1)}, f32[16,2,64,128]{3,2,1,0:T...) while((s32[]{:T(128)}, f32[2,128,128]{2,1,0:T(8,128)S(1)}, ...), condition=%wide.region_8.9_spmd, body=%wide.region_7.8_spmd.sunk | while | flops 88178688 | bytes 1248385 | solution.py:187
  936.2 20.2 %all_to_all.113 = bf16[8,128,256]{2,1,0:T(8,128)(2,1)S(1)} all-to-all(bf16[8,128,256]{2,1,0:T(8,128)(2,1)S(1)} %fusion.48), channel_id=1, replica_groups=mesh['ctx'=64,'head'=8] {'head'}, dimensions={0} | all-to-all | bytes 1048576 | tf_op jit(solution)/shard_map/all_to_all | solution.py:191
  (370 shorter events, 374.1 us)
Async XLA Ops:
  18.1 10.8 %all-to-all-start.4 = ((bf16[128,8,2]{0,2,1:T(2,128)(2,1)}), bf16[128,8,2]{0,2,1:T(2,128)(2,1)S(1)}, u32[]{:S(2)}, u32[]{:S(2)}) async-start(bf16[128,8,2]{0,2,1:T(2,128)(2,1)} %bitcast.158), calls=%async_computation.4 | async-start | bytes 8192 | tf_op jit(solution)/shard_map/all_to_all | solution.py:136
  28.9 13.8 %all-to-all-start.1 = ((bf16[128,8,128]{0,2,1:T(8,128)(2,1)}), bf16[128,8,128]{0,2,1:T(8,128)(2,1)S(1)}, u32[]{:S(2)}, u32[]{:S(2)}) async-start(bf16[128,8,128]{0,2,1:T(8,128)(2,1)} %bitcast.10), calls=%async_computation.1 | async-start | bytes 524288 | tf_op jit(solution)/shard_map/all_to_all | solution.py:131
  42.7 13.8 %all-to-all-start.2 = ((bf16[128,8,128]{0,2,1:T(8,128)(2,1)}), bf16[128,8,128]{0,2,1:T(8,128)(2,1)S(1)}, u32[]{:S(2)}, u32[]{:S(2)}) async-start(bf16[128,8,128]{0,2,1:T(8,128)(2,1)} %bitcast.13), calls=%async_computation.2 | async-start | bytes 524288 | tf_op jit(solution)/shard_map/all_to_all | solution.py:132
  56.6 16.7 %all-to-all-start.3 = ((bf16[128,8,256]{0,2,1:T(8,128)(2,1)}), bf16[128,8,256]{0,2,1:T(8,128)(2,1)S(1)}, u32[]{:S(2)}, u32[]{:S(2)}) async-start(bf16[128,8,256]{0,2,1:T(8,128)(2,1)} %bitcast.16), calls=%async_computation.3 | async-start | bytes 1048576 | tf_op jit(solution)/shard_map/all_to_all | solution.py:133
  73.3 861.4 %all-to-all-start.5 = ((bf16[128,8,256]{2,0,1:T(8,128)(2,1)}), bf16[128,8,256]{2,0,1:T(8,128)(2,1)}, u32[]{:S(2)}, u32[]{:S(2)}) async-start(bf16[128,8,256]{2,0,1:T(8,128)(2,1)} %copy.137), calls=%async_computation.5 | async-start | bytes 1048576 | tf_op jit(solution)/shard_map/all_to_all | solution.py:134
  313.1 8.4 collective-permute-start
  321.8 8.4 collective-permute-start
  330.5 8.4 collective-permute-start
  339.1 8.4 collective-permute-start
  347.8 8.4 collective-permute-start
  356.5 8.4 collective-permute-start
  365.2 8.4 collective-permute-start
  373.8 8.4 collective-permute-start
  382.5 8.4 collective-permute-start
  391.2 8.4 collective-permute-start
  399.8 8.4 collective-permute-start
  408.5 8.4 collective-permute-start
  417.2 8.4 collective-permute-start
  425.9 8.4 collective-permute-start
  434.5 8.4 collective-permute-start
  443.2 8.4 collective-permute-start
  451.9 8.4 collective-permute-start
  460.5 8.4 collective-permute-start
  469.2 8.4 collective-permute-start
  477.9 8.4 collective-permute-start
  486.6 8.4 collective-permute-start
  495.2 8.4 collective-permute-start
  503.9 8.4 collective-permute-start
  512.6 8.4 collective-permute-start
  521.2 8.4 collective-permute-start
  529.9 8.4 collective-permute-start
  538.6 8.4 collective-permute-start
  547.2 8.4 collective-permute-start
  555.9 8.4 collective-permute-start
  564.6 8.4 collective-permute-start
  573.3 8.4 collective-permute-start
  581.9 8.4 collective-permute-start
  590.6 8.4 collective-permute-start
  599.3 8.4 collective-permute-start
  607.9 8.4 collective-permute-start
  616.6 8.4 collective-permute-start
  625.3 8.4 collective-permute-start
  634.0 8.4 collective-permute-start
  642.6 8.4 collective-permute-start
  651.3 8.4 collective-permute-start
  660.0 8.4 collective-permute-start
  668.6 8.4 collective-permute-start
  677.3 8.4 collective-permute-start
  686.0 8.4 collective-permute-start
  694.7 8.4 collective-permute-start
  703.3 8.4 collective-permute-start
  712.0 8.4 collective-permute-start
  729.3 8.4 collective-permute-start
  738.0 8.4 collective-permute-start
  746.7 8.4 collective-permute-start
  755.3 8.4 collective-permute-start
  764.0 8.4 collective-permute-start
  781.4 8.4 collective-permute-start
  790.0 8.4 collective-permute-start
  807.4 8.4 collective-permute-start
  824.7 8.4 collective-permute-start
  833.4 8.4 collective-permute-start
  842.1 8.4 collective-permute-start
  850.7 8.4 collective-permute-start
  (15 other events, 1021.9 us)
where the time goes:
time: 964 us; the launch traced here: 958 us
  waiting for transfers between devices  446 us (46%)
  other arithmetic  171 us (18%)
  matrix products  144 us (15%)
  starting transfers between devices  141 us (15%)
  blocking collectives  38.2 us (4%)
  local copies, waits for them, and re-layouts  14.2 us (1%)
    ppermute x64, waiting for transfers between devices, passed_along(): lax.ppermute(value, axis, [(source, source + steps) for source in range(l...  412 us
    another operation x3, other arithmetic, forward_substitution(): lax.linalg.triangular_solve(coupling, targets, left_side=True, lower=True...  158 us
    ppermute x64, starting transfers between devices, passed_along(): lax.ppermute(value, axis, [(source, source + steps) for source in range(l...  123 us
    dot_general x95, matrix products, compose_maps(): jnp.einsum('hij,hjk->hik', later_map, earlier_map, precision=HIGHEST_PREC...  55.4 us
    all_to_all x1, blocking collectives, on_device(): lax.all_to_all(normed, 'head', split_axis=0, concat_axis=1, tiled=True)  20.2 us
    dot_general x16, matrix products, block_apply(): jnp.einsum('hcd,hce->hde', key_decay, corrected, precision=HIGHEST_PRECIS...  20 us
  transfers between devices with their start and end apart: 69, of which 68 were waited for; matrix products, arithmetic and copies ran while one was open for 34% of the time, Pallas kernels for 0%

commit v1 on v0

--- a/solution.py
+++ b/solution.py
@@ -20,16 +20,31 @@
     return lax.ppermute(value, axis, [(source, source + steps) for source in range(leading, last)])
 
 
+def matmul(spec, left, right):
+    return jnp.einsum(spec, left, right, precision=HIGHEST_PRECISION)
+
+
+def unit_lower_inverse(strict):
+    size = strict.shape[-1]
+    rows_index = jnp.arange(size)[:, None]
+    cols_index = jnp.arange(size)[None, :]
+    inverse = jnp.broadcast_to(jnp.eye(size, dtype=strict.dtype), strict.shape)
+    width = 1
+    while width < size:
+        pick = (
+            (rows_index // (2 * width) == cols_index // (2 * width))
+            & ((rows_index // width) % 2 == 1)
+            & ((cols_index // width) % 2 == 0)
+        )
+        lower = jnp.where(pick, strict, 0.0)
+        step = matmul("...ij,...jk->...ik", inverse, matmul("...ij,...jk->...ik", lower, inverse))
+        inverse = inverse - lax.optimization_barrier(step)
+        width *= 2
+    return inverse
+
+
 def forward_substitution(coupling, targets):
-    return lax.linalg.triangular_solve(
-        coupling,
-        targets,
-        left_side=True,
-        lower=True,
-        transpose_a=False,
-        conjugate_a=False,
-        unit_diagonal=True,
-    )
+    return matmul("...ij,...jf->...if", unit_lower_inverse(coupling), targets)
 
 
 def causal_conv(inputs, earlier_rows, weights):
@@ -161,30 +176,44 @@
     key_part, value_part, within, query_decay, key_decay, end_decay = terms
     heads_here = key_part.shape[1]
     identity_mat = jnp.broadcast_to(jnp.eye(DK, dtype=jnp.float32), (heads_here, DK, DK))
-    trans_blocks = end_decay[..., None, None] * identity_mat - jnp.einsum(
-        "nhcd,nhce->nhde", key_decay, key_part, precision=HIGHEST_PRECISION
-    )
-    bias_blocks = jnp.einsum("nhcd,nhce->nhde", key_decay, value_part, precision=HIGHEST_PRECISION)
-    blank_state = jnp.zeros((heads_here, DK, DV), jnp.float32)
-
-    def merge_transitions(carry, pieces):
-        trans_all, bias_all = carry
-        trans_one, bias_one = pieces
-        return (
-            (compose_maps(trans_one, trans_all), compose_maps(trans_one, bias_all) + bias_one),
-            None,
-        )
-
-    block_trans, block_bias = lax.scan(
-        merge_transitions, (identity_mat, blank_state), (trans_blocks, bias_blocks)
-    )[0]
-
-    def advance(iteration, initial):
-        ending = compose_maps(block_trans, initial) + block_bias
-        return passed_along(ending, "ctx", 1)
-
-    initial = lax.fori_loop(0, lax.axis_size("ctx") - 1, advance, blank_state)
-    produced = lax.scan(block_apply, initial, terms)[1]
+    trans = end_decay[..., None, None] * identity_mat - matmul(
+        "nhcd,nhce->nhde", key_decay, key_part
+    )
+    bias = matmul("nhcd,nhce->nhde", key_decay, value_part)
+    blocks_here = trans.shape[0]
+    span = 1
+    while span < blocks_here:
+        earlier_trans = jnp.concatenate(
+            [jnp.broadcast_to(identity_mat, (span,) + identity_mat.shape), trans[:-span]], axis=0
+        )
+        earlier_bias = jnp.concatenate([jnp.zeros_like(bias[:span]), bias[:-span]], axis=0)
+        trans, bias = (
+            matmul("nhij,nhjk->nhik", trans, earlier_trans),
+            matmul("nhij,nhjk->nhik", trans, earlier_bias) + bias,
+        )
+        span *= 2
+    total_trans, total_bias = trans[-1], bias[-1]
+    place = lax.axis_index("ctx")
+    count = lax.axis_size("ctx")
+    span = 1
+    while span < count:
+        if 2 * span < count:
+            arrived = passed_along(jnp.stack([total_trans, total_bias]), "ctx", span)
+            total_trans, total_bias = (
+                jnp.where(place >= span, compose_maps(total_trans, arrived[0]), total_trans),
+                compose_maps(total_trans, arrived[1]) + total_bias,
+            )
+        else:
+            total_bias = compose_maps(total_trans, passed_along(total_bias, "ctx", span)) + total_bias
+        span *= 2
+    initial = passed_along(total_bias, "ctx", 1)
+    earlier_trans = jnp.concatenate([identity_mat[None], trans[:-1]], axis=0)
+    earlier_bias = jnp.concatenate([jnp.zeros_like(bias[:1]), bias[:-1]], axis=0)
+    starts = matmul("nhij,hjk->nhik", earlier_trans, initial) + earlier_bias
+    corrected = value_part - matmul("nhcd,nhde->nhce", key_part, starts)
+    produced = matmul("nhcd,nhde->nhce", query_decay, starts) + matmul(
+        "nhij,nhje->nhie", within, corrected
+    )
     outputs = produced.transpose(0, 2, 1, 3).reshape(count_rows, heads_here, DV)
     gate = local_gate.astype(jnp.float32).reshape(count_rows, heads_here, DV)
     normed = gated_norm(outputs, gate, norm_gain)

time: 964 us -> 278 us (0.29)
  the two profiles are of different devices: /device:TPU:6 before, /device:TPU:21 now
where the time goes in v1:
time: 278 us; the launch traced here: 274 us
  waiting for transfers between devices  75.6 us (27%)
  starting transfers between devices  67.6 us (24%)
  matrix products  67.1 us (24%)
  blocking collectives  24.6 us (9%)
  local copies, waits for them, and re-layouts  22 us (8%)
  other arithmetic  15.5 us (6%)
    dot_general x27, matrix products, matmul(): return jnp.einsum(spec, left, right, precision=HIGHEST_PRECISION)  50.5 us
    ppermute x8, starting transfers between devices, passed_along(): lax.ppermute(value, axis, [(source, source + steps) for source in range(l...  39.7 us
    ppermute x8, waiting for transfers between devices, passed_along(): lax.ppermute(value, axis, [(source, source + steps) for source in range(l...  38.6 us
    all_to_all x1, blocking collectives, on_device(): lax.all_to_all(normed, 'head', split_axis=0, concat_axis=1, tiled=True)  24.6 us
    dot_general x11, matrix products, compose_maps(): jnp.einsum('hij,hjk->hik', later_map, earlier_map, precision=HIGHEST_PREC...  12.2 us
    all_to_all x1, waiting for transfers between devices, on_device(): lax.all_to_all(value_rows, 'head', split_axis=1, concat_axis=0, tiled=True)  10.9 us
    all_to_all x1, starting transfers between devices, on_device(): lax.all_to_all(write_strength, 'head', split_axis=1, concat_axis=0, tiled...  10.2 us
    unnamed x23, local copies, waits for them, and re-layouts  9.52 us
  transfers between devices with their start and end apart: 14, of which 10 were waited for; matrix products, arithmetic and copies ran while one was open for 10% of the time, Pallas kernels for 0%

profile of v1, /device:TPU:21, one launch (start us, length us, event | category | flops | bytes accessed | tf_op | source)
XLA Modules:
  0.0 273.7 jit_solution(15192412606114932465)
XLA Ops:
  0.0 10.2 %all-to-all-start.4 = ((bf16[128,8,2]{0,2,1:T(2,128)(2,1)}), bf16[128,8,2]{0,2,1:T(2,128)(2,1)S(1)}, u32[]{:S(2)}, u32[]{:S(2)}) async-start(bf16[128,8,2]{0,2,1:T(2,128)(2,1)} %bitcast.177), calls=%async_computation.4 | async-start | bytes 8192 | tf_op jit(solution)/shard_map/all_to_all | solution.py:151
  10.5 6.1 %all-to-all-done.4 = bf16[128,8,2]{0,2,1:T(2,128)(2,1)S(1)} async-done(((bf16[128,8,2]{0,2,1:T(2,128)(2,1)}), bf16[128,8,2]{0,2,1:T(2,128)(2,1)S(1)}, u32[]{:S(2)}, u32[]{:S(2)}) %all-to-all-start.4) | async-done | bytes 4128 | tf_op jit(solution)/shard_map/all_to_all | solution.py:151
  16.6 3.3 %all-to-all-start = ((bf16[128,8,2]{0,2,1:T(2,128)(2,1)}), bf16[128,8,2]{0,2,1:T(2,128)(2,1)S(1)}, u32[]{:S(2)}, u32[]{:S(2)}) async-start(bf16[128,8,2]{0,2,1:T(2,128)(2,1)} %bitcast.178), calls=%async_computation | async-start | bytes 8192 | tf_op jit(solution)/shard_map/all_to_all | solution.py:150
  20.0 1.8 copy.120
  21.8 4.5 %all-to-all-done = bf16[128,8,2]{0,2,1:T(2,128)(2,1)S(1)} async-done(((bf16[128,8,2]{0,2,1:T(2,128)(2,1)}), bf16[128,8,2]{0,2,1:T(2,128)(2,1)S(1)}, u32[]{:S(2)}, u32[]{:S(2)}) %all-to-all-start) | async-done | bytes 4128 | tf_op jit(solution)/shard_map/all_to_all | solution.py:150
  26.3 3.4 %all-to-all-start.2 = ((bf16[128,8,128]{0,2,1:T(8,128)(2,1)}), bf16[128,8,128]{0,2,1:T(8,128)(2,1)S(1)}, u32[]{:S(2)}, u32[]{:S(2)}) async-start(bf16[128,8,128]{0,2,1:T(8,128)(2,1)} %bitcast.6), calls=%async_computation.2 | async-start | bytes 524288 | tf_op jit(solution)/shard_map/all_to_all | solution.py:147
  29.7 1.8 copy.118
  31.7 7.4 %all-to-all-done.2 = bf16[128,8,128]{0,2,1:T(8,128)(2,1)S(1)} async-done(((bf16[128,8,128]{0,2,1:T(8,128)(2,1)}), bf16[128,8,128]{0,2,1:T(8,128)(2,1)S(1)}, u32[]{:S(2)}, u32[]{:S(2)}) %all-to-all-start.2) | async-done | bytes 262176 | tf_op jit(solution)/shard_map/all_to_all | solution.py:147
  39.1 3.4 %all-to-all-start.1 = ((bf16[128,8,128]{0,2,1:T(8,128)(2,1)}), bf16[128,8,128]{0,2,1:T(8,128)(2,1)S(1)}, u32[]{:S(2)}, u32[]{:S(2)}) async-start(bf16[128,8,128]{0,2,1:T(8,128)(2,1)} %bitcast.3), calls=%async_computation.1 | async-start | bytes 524288 | tf_op jit(solution)/shard_map/all_to_all | solution.py:146
  43.7 8.0 %all-to-all-done.1 = bf16[128,8,128]{0,2,1:T(8,128)(2,1)S(1)} async-done(((bf16[128,8,128]{0,2,1:T(8,128)(2,1)}), bf16[128,8,128]{0,2,1:T(8,128)(2,1)S(1)}, u32[]{:S(2)}, u32[]{:S(2)}) %all-to-all-start.1) | async-done | bytes 262176 | tf_op jit(solution)/shard_map/all_to_all | solution.py:146
  51.8 3.5 %all-to-all-start.3 = ((bf16[128,8,256]{0,2,1:T(8,128)(2,1)}), bf16[128,8,256]{0,2,1:T(8,128)(2,1)S(1)}, u32[]{:S(2)}, u32[]{:S(2)}) async-start(bf16[128,8,256]{0,2,1:T(8,128)(2,1)} %bitcast.9), calls=%async_computation.3 | async-start | bytes 1048576 | tf_op jit(solution)/shard_map/all_to_all | solution.py:148
  56.5 10.9 %all-to-all-done.3 = bf16[128,8,256]{0,2,1:T(8,128)(2,1)S(1)} async-done(((bf16[128,8,256]{0,2,1:T(8,128)(2,1)}), bf16[128,8,256]{0,2,1:T(8,128)(2,1)S(1)}, u32[]{:S(2)}, u32[]{:S(2)}) %all-to-all-start.3) | async-done | bytes 524320 | tf_op jit(solution)/shard_map/all_to_all | solution.py:148
  67.7 1.7 pad_maximum_fusion.7
  69.4 9.6 %collective-permute-start = (bf16[3,512]{1,0:T(4,128)(2,1)S(1)}, bf16[3,512]{1,0:T(4,128)(2,1)S(1)}, u32[]{:S(2)}, u32[]{:S(2)}) collective-permute-start(bf16[3,512]{1,0:T(4,128)(2,1)S(1)} %slice.145), channel_id=1, source_target_pairs={{0,8},{8,16},{16,24},{24,32},{32,40},{40,48},{48,56},{56,64},{64,7... | collective-permute-start | bytes 9224 | tf_op jit(solution)/shard_map/ppermute | solution.py:20
  79.7 5.0 %divide_multiply_fusion = f32[1024,512]{1,0:T(8,128)S(1)} fusion(f32[1024,512]{1,0:T(8,128)} %get-tuple-element.10, f32[3,512]{1,0:T(4,128)S(1)} %convert_element_type.63, f32[512]{0:T(512)S(1)} %bitcast.174, f32[512]{0:T(512)S(1)} %bitcast.175, f32[512]{0:T(512)S(1)} %bitcast.176, f32[512]{0:T(512)S(1)} %bitcast.173), kind=kLoop, calls=%fused_computation.43 | loop fusion | flops 7340032 | bytes 4208640 | tf_op jit(solution)/shard_map/jit(silu)/mul | solution.py:61
  85.2 1.5 reshape_reshape.2
  86.7 1.6 bitcast_multiply_fusion.1
  89.8 1.9 fusion.52
  93.8 1.2 fusion.66
  95.0 1.3 fusion.76
  96.5 1.3 fusion.64
  97.7 1.2 fusion.139
  99.1 1.5 fusion.62
  101.9 1.3 fusion.60
  104.6 1.2 fusion.58
  105.8 1.2 fusion.142
  107.0 2.0 fusion.10
  109.0 4.2 %fusion.48 = f32[16,2,128,128]{3,2,1,0:T(8,128)S(1)} fusion(f32[16,2,64,256]{3,2,1,0:T(8,128)S(1)} %fusion.10, f32[16,64,128]{2,1,0:T(8,128)S(1)} %bitcast.147, f32[16,2,64]{2,1,0:T(2,128)S(1)} %copy.125), kind=kOutput, calls=%fused_computation.48 | convolution fusion | flops 402915328 | bytes 3686400 | tf_op jit(solution)/shard_map/nhcd,nhce->nhde/dot_general | solution.py:24
  113.4 4.0 %multiply_subtract_fusion = f32[16,2,128,128]{3,2,1,0:T(8,128)S(1)} fusion(f32[128,128]{1,0:T(8,128)S(1)} %fusion.108, f32[16,2]{1,0:T(8,128)S(1)} %copy.124, f32[16,2,64,256]{3,2,1,0:T(8,128)S(1)} %fusion.10, f32[16,64,128]{2,1,0:T(8,128)S(1)} %bitcast.148, f32[16,2,64]{2,1,0:T(2,128)S(1)} %copy.125), kind=kOutput, calls=%fused_computation.42 | convolution fusion | flops 403963904 | bytes 3760128 | tf_op jit(solution)/shard_map/nhcd,nhce->nhde/dot_general | solution.py:24
  117.6 2.3 fusion.36
  120.2 2.3 fusion
  122.6 2.3 fusion.39
  125.1 2.4 fusion.15
  127.7 2.2 fusion.42
  130.1 2.3 fusion.19
  132.5 2.1 fusion.45
  134.6 1.3 copy-done.2
  136.1 2.3 fusion.23
  138.4 1.3 copy-done.1
  139.7 4.1 %collective-permute-start.1 = (f32[2,2,128,128]{3,2,1,0:T(8,128)S(1)}, f32[2,2,128,128]{3,2,1,0:T(8,128)}, u32[]{:S(2)}, u32[]{:S(2)}) collective-permute-start(f32[2,2,128,128]{3,2,1,0:T(8,128)S(1)} %pad_maximum_fusion.8), channel_id=1, source_target_pairs={{0,8},{8,16},{16,24},{24,32},{32,40},{40,48},{48,56},{56,64},{64,7... | collective-permute-start | bytes 786440 | tf_op jit(solution)/shard_map/ppermute | solution.py:20
  143.9 3.3 %collective-permute-done.1 = f32[2,2,128,128]{3,2,1,0:T(8,128)} collective-permute-done((f32[2,2,128,128]{3,2,1,0:T(8,128)S(1)}, f32[2,2,128,128]{3,2,1,0:T(8,128)}, u32[]{:S(2)}, u32[]{:S(2)}) %collective-permute-start.1) | collective-permute-done | bytes 262176 | tf_op jit(solution)/shard_map/ppermute | solution.py:20
  147.1 1.3 convolution_add_fusion.6
  148.5 1.3 convolution_select_fusion.4
  149.8 5.6 %collective-permute-start.2 = (f32[2,2,128,128]{3,2,1,0:T(8,128)S(1)}, f32[2,2,128,128]{3,2,1,0:T(8,128)}, u32[]{:S(2)}, u32[]{:S(2)}) collective-permute-start(f32[2,2,128,128]{3,2,1,0:T(8,128)S(1)} %pad_maximum_fusion.9), channel_id=1, source_target_pairs={{0,16},{8,24},{16,32},{24,40},{32,48},{40,56},{48,64},{56,72},{64,... | collective-permute-start | bytes 786440 | tf_op jit(solution)/shard_map/ppermute | solution.py:20
  155.4 5.5 %collective-permute-done.2 = f32[2,2,128,128]{3,2,1,0:T(8,128)} collective-permute-done((f32[2,2,128,128]{3,2,1,0:T(8,128)S(1)}, f32[2,2,128,128]{3,2,1,0:T(8,128)}, u32[]{:S(2)}, u32[]{:S(2)}) %collective-permute-start.2) | collective-permute-done | bytes 262176 | tf_op jit(solution)/shard_map/ppermute | solution.py:20
  163.4 2.6 collective-permute-start.3
  166.0 11.9 %collective-permute-done.3 = f32[2,2,128,128]{3,2,1,0:T(8,128)} collective-permute-done((f32[2,2,128,128]{3,2,1,0:T(8,128)S(1)}, f32[2,2,128,128]{3,2,1,0:T(8,128)}, u32[]{:S(2)}, u32[]{:S(2)}) %collective-permute-start.3) | collective-permute-done | bytes 262176 | tf_op jit(solution)/shard_map/ppermute | solution.py:20
  180.9 1.9 collective-permute-start.4
  182.9 13.1 %collective-permute-done.4 = f32[2,2,128,128]{3,2,1,0:T(8,128)} collective-permute-done((f32[2,2,128,128]{3,2,1,0:T(8,128)}, f32[2,2,128,128]{3,2,1,0:T(8,128)}, u32[]{:S(2)}, u32[]{:S(2)}) %collective-permute-start.4) | collective-permute-done | bytes 262176 | tf_op jit(solution)/shard_map/ppermute | solution.py:20
  199.1 2.0 collective-permute-start.5
  201.1 2.0 copy.138
  203.2 2.1 copy.139
  205.2 4.2 %all-to-all-start.5 = ((bf16[128,8,256]{2,0,1:T(8,128)(2,1)}), bf16[128,8,256]{2,0,1:T(8,128)(2,1)}, u32[]{:S(2)}, u32[]{:S(2)}) async-start(bf16[128,8,256]{2,0,1:T(8,128)(2,1)} %copy.139), calls=%async_computation.5 | async-start | bytes 1048576 | tf_op jit(solution)/shard_map/all_to_all | solution.py:149
  211.3 1.3 collective-permute-start.6
  213.8 4.7 %collective-permute-done.6 = f32[2,128,128]{2,1,0:T(8,128)S(1)} collective-permute-done((f32[2,128,128]{2,1,0:T(8,128)S(1)}, f32[2,128,128]{2,1,0:T(8,128)S(1)}, u32[]{:S(2)}, u32[]{:S(2)}) %collective-permute-start.6) | collective-permute-done | bytes 131104 | tf_op jit(solution)/shard_map/ppermute | solution.py:20
  218.8 12.5 %collective-permute-start.7 = (f32[2,128,128]{2,1,0:T(8,128)S(1)}, f32[2,128,128]{2,1,0:T(8,128)S(1)}, u32[]{:S(2)}, u32[]{:S(2)}) collective-permute-start(f32[2,128,128]{2,1,0:T(8,128)S(1)} %convolution_add_fusion.1), channel_id=1, source_target_pairs={{0,8},{8,16},{16,24},{24,32},{32,40},{40,48},{48,56},{56,64},{64,7... | collective-permute-start | bytes 393224 | tf_op jit(solution)/shard_map/ppermute | solution.py:20
  231.4 2.6 convolution_multiply_fusion
  234.0 1.5 slice-done
  236.1 1.8 bitcast_add_fusion
  237.9 2.1 fusion.70
  240.0 2.0 convolution_subtract_fusion
  242.0 1.5 multiply_reduce_fusion
  246.0 1.6 fusion.72
  247.6 24.6 %all_to_all.112 = bf16[8,128,256]{2,1,0:T(8,128)(2,1)S(1)} all-to-all(bf16[8,128,256]{2,1,0:T(8,128)(2,1)S(1)} %fusion.72), channel_id=1, replica_groups=mesh['ctx'=64,'head'=8] {'head'}, dimensions={0} | all-to-all | bytes 1048576 | tf_op jit(solution)/shard_map/all_to_all | solution.py:220
  (119 shorter events, 28.5 us)
Async XLA Ops:
  0.0 209.4 %copy-start = (f32[128]{0:T(128)S(1)}, f32[128]{0:T(128)}, u32[]{:S(2)}) copy-start(f32[128]{0:T(128)} %param.19) | copy-start | bytes 1540
  0.0 42.5 %copy-start.4 = (bf16[128,2048]{1,0:T(8,128)(2,1)S(1)}, bf16[128,2048]{1,0:T(8,128)(2,1)}, u32[]{:S(2)}) copy-start(bf16[128,2048]{1,0:T(8,128)(2,1)} %param.12) | copy-start | bytes 1572868
  0.0 16.6 %all-to-all-start.4 = ((bf16[128,8,2]{0,2,1:T(2,128)(2,1)}), bf16[128,8,2]{0,2,1:T(2,128)(2,1)S(1)}, u32[]{:S(2)}, u32[]{:S(2)}) async-start(bf16[128,8,2]{0,2,1:T(2,128)(2,1)} %bitcast.177), calls=%async_computation.4 | async-start | bytes 8192 | tf_op jit(solution)/shard_map/all_to_all | solution.py:151
  16.6 9.7 %all-to-all-start = ((bf16[128,8,2]{0,2,1:T(2,128)(2,1)}), bf16[128,8,2]{0,2,1:T(2,128)(2,1)S(1)}, u32[]{:S(2)}, u32[]{:S(2)}) async-start(bf16[128,8,2]{0,2,1:T(2,128)(2,1)} %bitcast.178), calls=%async_computation | async-start | bytes 8192 | tf_op jit(solution)/shard_map/all_to_all | solution.py:150
  20.0 35.3 %copy-start.6 = (bf16[4,256]{1,0:T(4,128)(2,1)S(1)}, bf16[4,256]{1,0:T(4,128)(2,1)}, u32[]{:S(2)}) copy-start(bf16[4,256]{1,0:T(4,128)(2,1)} %param.18) | copy-start | bytes 6148
  20.0 35.3 %copy-start.7 = (bf16[4,128]{1,0:T(4,128)(2,1)S(1)}, bf16[4,128]{1,0:T(4,128)(2,1)}, u32[]{:S(2)}) copy-start(bf16[4,128]{1,0:T(4,128)(2,1)} %param.17) | copy-start | bytes 3076
  20.0 35.3 %copy-start.8 = (bf16[4,128]{1,0:T(4,128)(2,1)S(1)}, bf16[4,128]{1,0:T(4,128)(2,1)}, u32[]{:S(2)}) copy-start(bf16[4,128]{1,0:T(4,128)(2,1)} %param.16) | copy-start | bytes 3076
  26.3 12.8 %all-to-all-start.2 = ((bf16[128,8,128]{0,2,1:T(8,128)(2,1)}), bf16[128,8,128]{0,2,1:T(8,128)(2,1)S(1)}, u32[]{:S(2)}, u32[]{:S(2)}) async-start(bf16[128,8,128]{0,2,1:T(8,128)(2,1)} %bitcast.6), calls=%async_computation.2 | async-start | bytes 524288 | tf_op jit(solution)/shard_map/all_to_all | solution.py:147
  39.1 12.7 %all-to-all-start.1 = ((bf16[128,8,128]{0,2,1:T(8,128)(2,1)}), bf16[128,8,128]{0,2,1:T(8,128)(2,1)S(1)}, u32[]{:S(2)}, u32[]{:S(2)}) async-start(bf16[128,8,128]{0,2,1:T(8,128)(2,1)} %bitcast.3), calls=%async_computation.1 | async-start | bytes 524288 | tf_op jit(solution)/shard_map/all_to_all | solution.py:146
  51.8 15.7 %all-to-all-start.3 = ((bf16[128,8,256]{0,2,1:T(8,128)(2,1)}), bf16[128,8,256]{0,2,1:T(8,128)(2,1)S(1)}, u32[]{:S(2)}, u32[]{:S(2)}) async-start(bf16[128,8,256]{0,2,1:T(8,128)(2,1)} %bitcast.9), calls=%async_computation.3 | async-start | bytes 1048576 | tf_op jit(solution)/shard_map/all_to_all | solution.py:148
  69.4 10.3 %collective-permute-start = (bf16[3,512]{1,0:T(4,128)(2,1)S(1)}, bf16[3,512]{1,0:T(4,128)(2,1)S(1)}, u32[]{:S(2)}, u32[]{:S(2)}) collective-permute-start(bf16[3,512]{1,0:T(4,128)(2,1)S(1)} %slice.145), channel_id=1, source_target_pairs={{0,8},{8,16},{16,24},{24,32},{32,40},{40,48},{48,56},{56,64},{64,7... | collective-permute-start | bytes 9224 | tf_op jit(solution)/shard_map/ppermute | solution.py:20
  79.5 10.2 %copy-start.5 = (f32[16,2,64]{2,1,0:T(2,128)}, f32[16,2,64]{2,1,0:T(2,128)S(1)}, u32[]{:S(2)}) copy-start(f32[16,2,64]{2,1,0:T(2,128)S(1)} %copy.128) | copy-start | bytes 24580
  134.6 1.4 copy-start.2
  138.4 1.3 copy-start.1
  139.7 7.4 %collective-permute-start.1 = (f32[2,2,128,128]{3,2,1,0:T(8,128)S(1)}, f32[2,2,128,128]{3,2,1,0:T(8,128)}, u32[]{:S(2)}, u32[]{:S(2)}) collective-permute-start(f32[2,2,128,128]{3,2,1,0:T(8,128)S(1)} %pad_maximum_fusion.8), channel_id=1, source_target_pairs={{0,8},{8,16},{16,24},{24,32},{32,40},{40,48},{48,56},{56,64},{64,7... | collective-permute-start | bytes 786440 | tf_op jit(solution)/shard_map/ppermute | solution.py:20
  149.8 11.2 %collective-permute-start.2 = (f32[2,2,128,128]{3,2,1,0:T(8,128)S(1)}, f32[2,2,128,128]{3,2,1,0:T(8,128)}, u32[]{:S(2)}, u32[]{:S(2)}) collective-permute-start(f32[2,2,128,128]{3,2,1,0:T(8,128)S(1)} %pad_maximum_fusion.9), channel_id=1, source_target_pairs={{0,16},{8,24},{16,32},{24,40},{32,48},{40,56},{48,64},{56,72},{64,... | collective-permute-start | bytes 786440 | tf_op jit(solution)/shard_map/ppermute | solution.py:20
  163.4 14.5 %collective-permute-start.3 = (f32[2,2,128,128]{3,2,1,0:T(8,128)S(1)}, f32[2,2,128,128]{3,2,1,0:T(8,128)}, u32[]{:S(2)}, u32[]{:S(2)}) collective-permute-start(f32[2,2,128,128]{3,2,1,0:T(8,128)S(1)} %pad_maximum_fusion.10), channel_id=1, source_target_pairs={{0,32},{8,40},{16,48},{24,56},{32,64},{40,72},{48,80},{56,88},{64,... | collective-permute-start | bytes 786440 | tf_op jit(solution)/shard_map/ppermute | solution.py:20
  180.9 15.0 %collective-permute-start.4 = (f32[2,2,128,128]{3,2,1,0:T(8,128)}, f32[2,2,128,128]{3,2,1,0:T(8,128)}, u32[]{:S(2)}, u32[]{:S(2)}) collective-permute-start(f32[2,2,128,128]{3,2,1,0:T(8,128)} %pad_maximum_fusion.11), channel_id=1, source_target_pairs={{0,64},{8,72},{16,80},{24,88},{32,96},{40,104},{48,112},{56,120},{... | collective-permute-start | bytes 786440 | tf_op jit(solution)/shard_map/ppermute | solution.py:20
  199.1 32.3 %copy-start.3 = (f32[1024,128]{1,0:T(8,128)S(1)}, f32[1024,128]{1,0:T(8,128)}, u32[]{:S(2)}) copy-start(f32[1024,128]{1,0:T(8,128)} %get-tuple-element.7) | copy-start | bytes 1572868
  199.1 11.1 %collective-permute-start.5 = (f32[2,2,128,128]{3,2,1,0:T(8,128)}, f32[2,2,128,128]{3,2,1,0:T(8,128)}, u32[]{:S(2)}, u32[]{:S(2)}) collective-permute-start(f32[2,2,128,128]{3,2,1,0:T(8,128)} %pad_maximum_fusion.12), channel_id=1, source_target_pairs={{0,128},{8,136},{16,144},{24,152},{32,160},{40,168},{48,176},{56,1... | collective-permute-start | bytes 786440 | tf_op jit(solution)/shard_map/ppermute | solution.py:20
  205.2 40.8 %all-to-all-start.5 = ((bf16[128,8,256]{2,0,1:T(8,128)(2,1)}), bf16[128,8,256]{2,0,1:T(8,128)(2,1)}, u32[]{:S(2)}, u32[]{:S(2)}) async-start(bf16[128,8,256]{2,0,1:T(8,128)(2,1)} %copy.139), calls=%async_computation.5 | async-start | bytes 1048576 | tf_op jit(solution)/shard_map/all_to_all | solution.py:149
  211.3 7.2 %collective-permute-start.6 = (f32[2,128,128]{2,1,0:T(8,128)S(1)}, f32[2,128,128]{2,1,0:T(8,128)S(1)}, u32[]{:S(2)}, u32[]{:S(2)}) collective-permute-start(f32[2,128,128]{2,1,0:T(8,128)S(1)} %convolution_add_fusion.2), channel_id=1, source_target_pairs={{0,256},{8,264},{16,272},{24,280},{32,288},{40,296},{48,304},{56,3... | collective-permute-start | bytes 393224 | tf_op jit(solution)/shard_map/ppermute | solution.py:20
  218.8 15.2 %collective-permute-start.7 = (f32[2,128,128]{2,1,0:T(8,128)S(1)}, f32[2,128,128]{2,1,0:T(8,128)S(1)}, u32[]{:S(2)}, u32[]{:S(2)}) collective-permute-start(f32[2,128,128]{2,1,0:T(8,128)S(1)} %convolution_add_fusion.1), channel_id=1, source_target_pairs={{0,8},{8,16},{16,24},{24,32},{32,40},{40,48},{48,56},{56,64},{64,7... | collective-permute-start | bytes 393224 | tf_op jit(solution)/shard_map/ppermute | solution.py:20
  234.0 1.5 slice-start
  234.0 2.1 slice-start.1

commit v2 on v1

--- a/solution.py
+++ b/solution.py
@@ -50,6 +50,111 @@
 def causal_conv(inputs, earlier_rows, weights):
     kernel_width = weights.shape[0]
     count_rows = inputs.shape[0]
+    joined = jnp.concatenate([earlier_rows, inputs], axis=0)
+    result = joined[kernel_width - 1 :] * weights[kernel_width - 1]
+    for offset in range(1, kernel_width):
+        result = (
+            result
+            + joined[kernel_width - 1 - offset : kernel_width - 1 - offset + count_rows]
+            * weights[kernel_width - 1 - offset]
+        )
+    return jax.nn.silu(result)
+
+
+def unit_heads(mixed, heads):
+    shaped = mixed.reshape(mixed.shape[0], heads, -1)
+    return shaped / jnp.sqrt(jnp.sum(shaped * shaped, axis=-1, keepdims=True) + EPSILON)
+
+
+def into_blocks(array, block_len):
+    count_rows, heads, inner_dim = array.shape
+    return array.reshape(count_rows // block_len, block_len, heads, inner_dim).transpose(0, 2, 1, 3)
+
+
+def block_scalars(array, block_len):
+    count_rows, heads = array.shape
+    return (
+        array.astype(jnp.float32)
+        .reshape(count_rows // block_len, block_len, heads)
+        .transpose(0, 2, 1)
+    )
+
+
+def block_terms(queries, keys, values, log_gate, strength):
+    block_len = queries.shape[2]
+    key_dim = keys.shape[-1]
+    cumulative = jnp.cumsum(log_gate, axis=-1)
+    rows_index = jnp.arange(block_len)[:, None]
+    cols_index = jnp.arange(block_len)[None, :]
+    causal = rows_index >= cols_index
+    strictly = rows_index > cols_index
+    spread = jnp.where(causal, cumulative[..., :, None] - cumulative[..., None, :], 0.0)
+    decays = jnp.where(causal, jnp.exp(spread), 0.0)
+    key_key = jnp.einsum("nhid,nhjd->nhij", keys, keys, precision=HIGHEST_PRECISION)
+    coupling = jnp.where(strictly, strength[..., None] * decays * key_key, 0.0)
+    targets = jnp.concatenate(
+        [(strength * jnp.exp(cumulative))[..., None] * keys, strength[..., None] * values], axis=-1
+    )
+    solved = forward_substitution(coupling, targets)
+    key_part = solved[..., :key_dim]
+    value_part = solved[..., key_dim:]
+    query_key = jnp.einsum("nhid,nhjd->nhij", queries, keys, precision=HIGHEST_PRECISION)
+    within = query_key * decays
+    query_decay = jnp.exp(cumulative)[..., None] * queries
+    closing_logarithm = cumulative[..., -1:]
+    key_decay = jnp.exp(closing_logarithm - cumulative)[..., None] * keys
+    end_decay = jnp.exp(closing_logarithm[..., 0])
+    return (key_part, value_part, within, query_decay, key_decay, end_decay)
+
+
+def block_apply(memory, pieces):
+    key_part, value_part, within, query_decay, key_decay, end_decay = pieces
+    corrected = value_part - jnp.einsum(
+        "hcd,hde->hce", key_part, memory, precision=HIGHEST_PRECISION
+    )
+    result = jnp.einsum("hcd,hde->hce", query_decay, memory, precision=HIGHEST_PRECISION)
+    result = result + jnp.einsum("hij,hje->hie", within, corrected, precision=HIGHEST_PRECISION)
+    memory = end_decay[:, None, None] * memory + jnp.einsum(
+        "hcd,hce->hde", key_decay, corrected, precision=HIGHEST_PRECISION
+    )
+    return (memory, result)
+
+
+def gated_norm(outputs, gate, gain):
+    meansq = jnp.mean(outputs * outputs, axis=-1, keepdims=True)
+    scaled = outputs / jnp.sqrt(meansq + EPSILON) * gain * jax.nn.silu(gate)
+    return scaled.astype(jnp.bfloat16).reshape(outputs.shape[0], -1)
+
+
+def compose_maps(later_map, earlier_map):
+    return jnp.einsum("hij,hjk->hik", later_map, earlier_map, precision=HIGHEST_PRECISION)
+
+
+def on_device(
+    query_rows,
+    key_rows,
+    value_rows,
+    gate_rows,
+    log_decay,
+    write_strength,
+    conv_query,
+    conv_key,
+    conv_value,
+    norm_gain,
+):
+    parts = lax.axis_size("head")
+    pieces = (query_rows, key_rows, value_rows, log_decay, write_strength)
+    widths = [piece.shape[1] // parts for piece in pieces]
+    packed = jnp.concatenate(
+        [piece.reshape(piece.shape[0], parts, -1) for piece in pieces], axis=2
+    )
+    moved = lax.all_to_all(packed, "head", split_axis=1, concat_axis=0, tiled=True)
+    moved = moved.reshape(moved.shape[0], -1)
+    offsets = [sum(widths[:index]) for index in range(len(widths) + 1)]
+    device_query, local_key, local_value, local_decay, local_strength = (
+        moved[:, offsets[index] : offsets[index + 1]] for index in range(len(widths))
+    )
+    local_gate = lax.all_to_all(gate_rows, "head", split_axis=1, concat_axis=0, tiled=True)
     joined = jnp.concatenate([earlier_rows, inputs], axis=0)
     result = joined[kernel_width - 1 :] * weights[kernel_width - 1]
     for offset in range(1, kernel_width):
@@ -192,28 +297,32 @@
             matmul("nhij,nhjk->nhik", trans, earlier_bias) + bias,
         )
         span *= 2
+    earlier_trans = jnp.concatenate([identity_mat[None], trans[:-1]], axis=0)
+    earlier_bias = jnp.concatenate([jnp.zeros_like(bias[:1]), bias[:-1]], axis=0)
+    corrected = value_part - matmul("nhcd,nhde->nhce", key_part, earlier_bias)
+    local_result = matmul("nhcd,nhde->nhce", query_decay, earlier_bias) + matmul(
+        "nhij,nhje->nhie", within, corrected
+    )
+    reach = query_decay - matmul("nhij,nhjd->nhid", within, key_part)
+    carry_map = matmul("nhcd,nhde->nhce", reach, earlier_trans)
     total_trans, total_bias = trans[-1], bias[-1]
     place = lax.axis_index("ctx")
     count = lax.axis_size("ctx")
     span = 1
-    while span < count:
-        if 2 * span < count:
-            arrived = passed_along(jnp.stack([total_trans, total_bias]), "ctx", span)
-            total_trans, total_bias = (
-                jnp.where(place >= span, compose_maps(total_trans, arrived[0]), total_trans),
-                compose_maps(total_trans, arrived[1]) + total_bias,
-            )
-        else:
-            total_bias = compose_maps(total_trans, passed_along(total_bias, "ctx", span)) + total_bias
+    while 2 * span < count:
+        arrived = passed_along(jnp.stack([total_trans, total_bias]), "ctx", span)
+        total_trans, total_bias = (
+            jnp.where(place >= span, compose_maps(total_trans, arrived[0]), total_trans),
+            compose_maps(total_trans, arrived[1]) + total_bias,
+        )
         span *= 2
-    initial = passed_along(total_bias, "ctx", 1)
-    earlier_trans = jnp.concatenate([identity_mat[None], trans[:-1]], axis=0)
-    earlier_bias = jnp.concatenate([jnp.zeros_like(bias[:1]), bias[:-1]], axis=0)
-    starts = matmul("nhij,hjk->nhik", earlier_trans, initial) + earlier_bias
-    corrected = value_part - matmul("nhcd,nhde->nhce", key_part, starts)
-    produced = matmul("nhcd,nhde->nhce", query_decay, starts) + matmul(
-        "nhij,nhje->nhie", within, corrected
-    )
+    initial = jnp.zeros_like(total_bias)
+    if count > 1:
+        near = passed_along(jnp.stack([total_trans, total_bias]), "ctx", 1)
+        initial = near[1]
+        if span + 1 < count:
+            initial = compose_maps(near[0], passed_along(total_bias, "ctx", span + 1)) + initial
+    produced = local_result + matmul("nhcd,hde->nhce", carry_map, initial)
     outputs = produced.transpose(0, 2, 1, 3).reshape(count_rows, heads_here, DV)
     gate = local_gate.astype(jnp.float32).reshape(count_rows, heads_here, DV)
     normed = gated_norm(outputs, gate, norm_gain)

time: 278 us -> 267 us (0.960)
  the two profiles are of different devices: /device:TPU:21 before, /device:TPU:57 now
where the time goes in v2:
time: 267 us; the launch traced here: 263 us
  starting transfers between devices  83.7 us (31%)
  matrix products  61.1 us (23%)
  waiting for transfers between devices  56.4 us (21%)
  blocking collectives  24.5 us (9%)
  local copies, waits for them, and re-layouts  22.3 us (8%)
  other arithmetic  13.5 us (5%)
    ppermute x8, starting transfers between devices, passed_along(): lax.ppermute(value, axis, [(source, source + steps) for source in range(l...  55.6 us
    dot_general x29, matrix products, matmul(): return jnp.einsum(spec, left, right, precision=HIGHEST_PRECISION)  52.7 us
    all_to_all x1, blocking collectives, on_device(): lax.all_to_all(normed, 'head', split_axis=0, concat_axis=1, tiled=True)  24.5 us
    ppermute x8, waiting for transfers between devices, passed_along(): lax.ppermute(value, axis, [(source, source + steps) for source in range(l...  19.5 us
    unnamed x23, local copies, waits for them, and re-layouts  12.4 us
    all_to_all x1, waiting for transfers between devices, on_device(): lax.all_to_all(value_rows, 'head', split_axis=1, concat_axis=0, tiled=True)  10.9 us
    all_to_all x1, starting transfers between devices, on_device(): lax.all_to_all(write_strength, 'head', split_axis=1, concat_axis=0, tiled...  10.2 us
    all_to_all x1, waiting for transfers between devices, on_device(): lax.all_to_all(query_rows, 'head', split_axis=1, concat_axis=0, tiled=True)  8.05 us
  transfers between devices with their start and end apart: 14, of which 11 were waited for; matrix products, arithmetic and copies ran while one was open for 11% of the time, Pallas kernels for 0%

profile of v2, /device:TPU:57, one launch (start us, length us, event | category | flops | bytes accessed | tf_op | source)
XLA Modules:
  0.0 262.8 jit_solution(6496869524590255096)
XLA Ops:
  0.0 10.2 %all-to-all-start.4 = ((bf16[128,8,2]{0,2,1:T(2,128)(2,1)}), bf16[128,8,2]{0,2,1:T(2,128)(2,1)S(1)}, u32[]{:S(2)}, u32[]{:S(2)}) async-start(bf16[128,8,2]{0,2,1:T(2,128)(2,1)} %bitcast.191), calls=%async_computation.4 | async-start | bytes 8192 | tf_op jit(solution)/shard_map/all_to_all | solution.py:256
  10.5 6.1 %all-to-all-done.4 = bf16[128,8,2]{0,2,1:T(2,128)(2,1)S(1)} async-done(((bf16[128,8,2]{0,2,1:T(2,128)(2,1)}), bf16[128,8,2]{0,2,1:T(2,128)(2,1)S(1)}, u32[]{:S(2)}, u32[]{:S(2)}) %all-to-all-start.4) | async-done | bytes 4128 | tf_op jit(solution)/shard_map/all_to_all | solution.py:256
  16.6 3.3 %all-to-all-start = ((bf16[128,8,2]{0,2,1:T(2,128)(2,1)}), bf16[128,8,2]{0,2,1:T(2,128)(2,1)S(1)}, u32[]{:S(2)}, u32[]{:S(2)}) async-start(bf16[128,8,2]{0,2,1:T(2,128)(2,1)} %bitcast.192), calls=%async_computation | async-start | bytes 8192 | tf_op jit(solution)/shard_map/all_to_all | solution.py:255
  20.0 1.8 copy.119
  21.8 4.5 %all-to-all-done = bf16[128,8,2]{0,2,1:T(2,128)(2,1)S(1)} async-done(((bf16[128,8,2]{0,2,1:T(2,128)(2,1)}), bf16[128,8,2]{0,2,1:T(2,128)(2,1)S(1)}, u32[]{:S(2)}, u32[]{:S(2)}) %all-to-all-start) | async-done | bytes 4128 | tf_op jit(solution)/shard_map/all_to_all | solution.py:255
  26.3 3.4 %all-to-all-start.2 = ((bf16[128,8,128]{0,2,1:T(8,128)(2,1)}), bf16[128,8,128]{0,2,1:T(8,128)(2,1)S(1)}, u32[]{:S(2)}, u32[]{:S(2)}) async-start(bf16[128,8,128]{0,2,1:T(8,128)(2,1)} %bitcast.6), calls=%async_computation.2 | async-start | bytes 524288 | tf_op jit(solution)/shard_map/all_to_all | solution.py:252
  29.7 1.8 copy.117
  31.7 7.4 %all-to-all-done.2 = bf16[128,8,128]{0,2,1:T(8,128)(2,1)S(1)} async-done(((bf16[128,8,128]{0,2,1:T(8,128)(2,1)}), bf16[128,8,128]{0,2,1:T(8,128)(2,1)S(1)}, u32[]{:S(2)}, u32[]{:S(2)}) %all-to-all-start.2) | async-done | bytes 262176 | tf_op jit(solution)/shard_map/all_to_all | solution.py:252
  39.1 3.4 %all-to-all-start.1 = ((bf16[128,8,128]{0,2,1:T(8,128)(2,1)}), bf16[128,8,128]{0,2,1:T(8,128)(2,1)S(1)}, u32[]{:S(2)}, u32[]{:S(2)}) async-start(bf16[128,8,128]{0,2,1:T(8,128)(2,1)} %bitcast.3), calls=%async_computation.1 | async-start | bytes 524288 | tf_op jit(solution)/shard_map/all_to_all | solution.py:251
  43.7 8.0 %all-to-all-done.1 = bf16[128,8,128]{0,2,1:T(8,128)(2,1)S(1)} async-done(((bf16[128,8,128]{0,2,1:T(8,128)(2,1)}), bf16[128,8,128]{0,2,1:T(8,128)(2,1)S(1)}, u32[]{:S(2)}, u32[]{:S(2)}) %all-to-all-start.1) | async-done | bytes 262176 | tf_op jit(solution)/shard_map/all_to_all | solution.py:251
  51.8 3.5 %all-to-all-start.3 = ((bf16[128,8,256]{0,2,1:T(8,128)(2,1)}), bf16[128,8,256]{0,2,1:T(8,128)(2,1)S(1)}, u32[]{:S(2)}, u32[]{:S(2)}) async-start(bf16[128,8,256]{0,2,1:T(8,128)(2,1)} %bitcast.9), calls=%async_computation.3 | async-start | bytes 1048576 | tf_op jit(solution)/shard_map/all_to_all | solution.py:253
  56.5 10.9 %all-to-all-done.3 = bf16[128,8,256]{0,2,1:T(8,128)(2,1)S(1)} async-done(((bf16[128,8,256]{0,2,1:T(8,128)(2,1)}), bf16[128,8,256]{0,2,1:T(8,128)(2,1)S(1)}, u32[]{:S(2)}, u32[]{:S(2)}) %all-to-all-start.3) | async-done | bytes 524320 | tf_op jit(solution)/shard_map/all_to_all | solution.py:253
  67.7 1.7 pad_maximum_fusion.5
  69.3 8.7 %collective-permute-start = (bf16[3,512]{1,0:T(4,128)(2,1)S(1)}, bf16[3,512]{1,0:T(4,128)(2,1)S(1)}, u32[]{:S(2)}, u32[]{:S(2)}) collective-permute-start(bf16[3,512]{1,0:T(4,128)(2,1)S(1)} %slice.153), channel_id=1, source_target_pairs={{0,8},{8,16},{16,24},{24,32},{32,40},{40,48},{48,56},{56,64},{64,7... | collective-permute-start | bytes 9224 | tf_op jit(solution)/shard_map/ppermute | solution.py:20
  78.8 5.0 %divide_multiply_fusion = f32[1024,512]{1,0:T(8,128)S(1)} fusion(f32[1024,512]{1,0:T(8,128)} %get-tuple-element.10, f32[3,512]{1,0:T(4,128)S(1)} %convert_element_type.63, f32[512]{0:T(512)S(1)} %bitcast.188, f32[512]{0:T(512)S(1)} %bitcast.189, f32[512]{0:T(512)S(1)} %bitcast.190, f32[512]{0:T(512)S(1)} %bitcast.187), kind=kLoop, calls=%fused_computation.42 | loop fusion | flops 7340032 | bytes 4208640 | tf_op jit(solution)/shard_map/jit(silu)/mul | solution.py:61
  84.3 1.5 reshape_reshape.2
  85.8 1.6 bitcast_multiply_fusion.1
  88.0 1.8 fusion.74
  92.0 1.2 fusion.90
  93.2 1.2 fusion.99
  94.6 1.2 fusion.88
  95.8 1.2 fusion.163
  97.2 1.5 fusion.86
  100.1 1.2 fusion.84
  101.3 1.2 fusion.165
  102.6 1.2 fusion.82
  103.9 1.2 fusion.166
  105.1 2.0 fusion.10
  107.0 4.0 %fusion.52 = f32[16,2,128,128]{3,2,1,0:T(8,128)S(1)} fusion(f32[16,2,64,256]{3,2,1,0:T(8,128)S(1)} %fusion.10, f32[16,64,128]{2,1,0:T(8,128)S(1)} %bitcast.159, f32[16,2,64]{2,1,0:T(2,128)S(1)} %copy.124), kind=kOutput, calls=%fused_computation.51 | convolution fusion | flops 402915328 | bytes 3686400 | tf_op jit(solution)/shard_map/nhcd,nhce->nhde/dot_general | solution.py:24
  111.3 4.0 %multiply_subtract_fusion = f32[16,2,128,128]{3,2,1,0:T(8,128)S(1)} fusion(f32[128,128]{1,0:T(8,128)S(1)} %fusion.130, f32[16,2]{1,0:T(8,128)S(1)} %copy.123, f32[16,2,64,256]{3,2,1,0:T(8,128)S(1)} %fusion.10, f32[16,64,128]{2,1,0:T(8,128)S(1)} %bitcast.160, f32[16,2,64]{2,1,0:T(2,128)S(1)} %copy.124), kind=kOutput, calls=%fused_computation.41 | convolution fusion | flops 403963904 | bytes 3760128 | tf_op jit(solution)/shard_map/nhcd,nhce->nhde/dot_general | solution.py:24
  115.5 2.3 fusion.40
  118.0 2.3 fusion
  120.5 2.3 fusion.43
  123.0 2.7 %fusion.15 = f32[16,2,128,128]{3,2,1,0:T(8,128)S(1)} fusion(f32[16,2,128,128]{3,2,1,0:T(8,128)S(1)} %fusion, f32[14,2,128,128]{3,2,1,0:T(8,128)S(1)} %slice.167, f32[2,2,128,128]{3,2,1,0:T(8,128)S(1)} %broadcast_in_dim_broadcast_in_dim.16), kind=kOutput, calls=%fused_computation.20 | convolution fusion | flops 805830656 | bytes 6291456 | tf_op jit(solution)/shard_map/nhij,nhjk->nhik/dot_general | solution.py:24
  125.8 2.2 fusion.46
  128.2 2.3 fusion.19
  130.6 2.1 fusion.49
  132.8 1.3 copy-done.3
  134.1 2.3 fusion.23
  136.4 1.3 copy-done.1
  138.5 6.3 %collective-permute-start.1 = (f32[2,2,128,128]{3,2,1,0:T(8,128)}, f32[2,2,128,128]{3,2,1,0:T(8,128)}, u32[]{:S(2)}, u32[]{:S(2)}) collective-permute-start(f32[2,2,128,128]{3,2,1,0:T(8,128)} %pad_maximum_fusion.6), channel_id=1, source_target_pairs={{0,8},{8,16},{16,24},{24,32},{32,40},{40,48},{48,56},{56,64},{64,7... | collective-permute-start | bytes 786440 | tf_op jit(solution)/shard_map/ppermute | solution.py:20
  144.8 2.0 copy.138
  146.8 2.1 copy.139
  148.9 4.3 %all-to-all-start.5 = ((bf16[128,8,256]{2,0,1:T(8,128)(2,1)}), bf16[128,8,256]{2,0,1:T(8,128)(2,1)}, u32[]{:S(2)}, u32[]{:S(2)}) async-start(bf16[128,8,256]{2,0,1:T(8,128)(2,1)} %copy.139), calls=%async_computation.5 | async-start | bytes 1048576 | tf_op jit(solution)/shard_map/all_to_all | solution.py:254
  153.3 1.6 copy-done.4
  155.1 1.4 copy-done.2
  158.8 1.9 collective-permute-start.2
  160.8 1.8 convolution_multiply_fusion
  162.5 4.7 %collective-permute-done.2 = f32[2,2,128,128]{3,2,1,0:T(8,128)S(1)} collective-permute-done((f32[2,2,128,128]{3,2,1,0:T(8,128)S(1)}, f32[2,2,128,128]{3,2,1,0:T(8,128)S(1)}, u32[]{:S(2)}, u32[]{:S(2)}) %collective-permute-start.2) | collective-permute-done | bytes 262176 | tf_op jit(solution)/shard_map/ppermute | solution.py:20
  167.8 3.9 %collective-permute-start.3 = (f32[2,2,128,128]{3,2,1,0:T(8,128)S(1)}, f32[2,2,128,128]{3,2,1,0:T(8,128)S(1)}, u32[]{:S(2)}, u32[]{:S(2)}) collective-permute-start(f32[2,2,128,128]{3,2,1,0:T(8,128)S(1)} %pad_maximum_fusion.8), channel_id=1, source_target_pairs={{0,32},{8,40},{16,48},{24,56},{32,64},{40,72},{48,80},{56,88},{64,... | collective-permute-start | bytes 786440 | tf_op jit(solution)/shard_map/ppermute | solution.py:20
  171.7 1.3 multiply_subtract_fusion.1
  173.0 5.8 %collective-permute-done.3 = f32[2,2,128,128]{3,2,1,0:T(8,128)S(1)} collective-permute-done((f32[2,2,128,128]{3,2,1,0:T(8,128)S(1)}, f32[2,2,128,128]{3,2,1,0:T(8,128)S(1)}, u32[]{:S(2)}, u32[]{:S(2)}) %collective-permute-start.3) | collective-permute-done | bytes 262176 | tf_op jit(solution)/shard_map/ppermute | solution.py:20
  179.4 7.4 %collective-permute-start.4 = (f32[2,2,128,128]{3,2,1,0:T(8,128)S(1)}, f32[2,2,128,128]{3,2,1,0:T(8,128)S(1)}, u32[]{:S(2)}, u32[]{:S(2)}) collective-permute-start(f32[2,2,128,128]{3,2,1,0:T(8,128)S(1)} %pad_maximum_fusion.9), channel_id=1, source_target_pairs={{0,64},{8,72},{16,80},{24,88},{32,96},{40,104},{48,112},{56,120},{... | collective-permute-start | bytes 786440 | tf_op jit(solution)/shard_map/ppermute | solution.py:20
  186.7 2.1 fusion.71
  188.8 5.0 %collective-permute-done.4 = f32[2,2,128,128]{3,2,1,0:T(8,128)S(1)} collective-permute-done((f32[2,2,128,128]{3,2,1,0:T(8,128)S(1)}, f32[2,2,128,128]{3,2,1,0:T(8,128)S(1)}, u32[]{:S(2)}, u32[]{:S(2)}) %collective-permute-start.4) | collective-permute-done | bytes 262176 | tf_op jit(solution)/shard_map/ppermute | solution.py:20
  194.5 3.0 %collective-permute-start.5 = (f32[2,2,128,128]{3,2,1,0:T(8,128)S(1)}, f32[2,2,128,128]{3,2,1,0:T(8,128)S(1)}, u32[]{:S(2)}, u32[]{:S(2)}) collective-permute-start(f32[2,2,128,128]{3,2,1,0:T(8,128)S(1)} %pad_maximum_fusion.10), channel_id=1, source_target_pairs={{0,128},{8,136},{16,144},{24,152},{32,160},{40,168},{48,176},{56,1... | collective-permute-start | bytes 786440 | tf_op jit(solution)/shard_map/ppermute | solution.py:20
  197.5 1.2 fusion.167
  198.7 2.4 collective-permute-done.5
  201.4 22.3 %collective-permute-start.7 = (f32[2,128,128]{2,1,0:T(8,128)S(1)}, f32[2,128,128]{2,1,0:T(8,128)S(1)}, u32[]{:S(2)}, u32[]{:S(2)}) collective-permute-start(f32[2,128,128]{2,1,0:T(8,128)S(1)} %convolution_add_fusion.1), channel_id=1, source_target_pairs={{0,264},{8,272},{16,280},{24,288},{32,296},{40,304},{48,312},{56,3... | collective-permute-start | bytes 393224 | tf_op jit(solution)/shard_map/ppermute | solution.py:20
  224.0 2.1 collective-permute-start.6
  226.2 2.0 fusion.1
  230.5 2.2 multiply_reduce_fusion
  235.3 1.6 fusion.94
  236.8 24.5 %all_to_all.112 = bf16[8,128,256]{2,1,0:T(8,128)(2,1)S(1)} all-to-all(bf16[8,128,256]{2,1,0:T(8,128)(2,1)S(1)} %fusion.94), channel_id=1, replica_groups=mesh['ctx'=64,'head'=8] {'head'}, dimensions={0} | all-to-all | bytes 1048576 | tf_op jit(solution)/shard_map/all_to_all | solution.py:329
  (121 shorter events, 21.8 us)
Async XLA Ops:
  0.0 153.2 %copy-start = (f32[128]{0:T(128)S(1)}, f32[128]{0:T(128)}, u32[]{:S(2)}) copy-start(f32[128]{0:T(128)} %param.19) | copy-start | bytes 1540
  0.0 42.5 %copy-start.5 = (bf16[128,2048]{1,0:T(8,128)(2,1)S(1)}, bf16[128,2048]{1,0:T(8,128)(2,1)}, u32[]{:S(2)}) copy-start(bf16[128,2048]{1,0:T(8,128)(2,1)} %param.12) | copy-start | bytes 1572868
  0.0 16.6 %all-to-all-start.4 = ((bf16[128,8,2]{0,2,1:T(2,128)(2,1)}), bf16[128,8,2]{0,2,1:T(2,128)(2,1)S(1)}, u32[]{:S(2)}, u32[]{:S(2)}) async-start(bf16[128,8,2]{0,2,1:T(2,128)(2,1)} %bitcast.191), calls=%async_computation.4 | async-start | bytes 8192 | tf_op jit(solution)/shard_map/all_to_all | solution.py:256
  16.6 9.7 %all-to-all-start = ((bf16[128,8,2]{0,2,1:T(2,128)(2,1)}), bf16[128,8,2]{0,2,1:T(2,128)(2,1)S(1)}, u32[]{:S(2)}, u32[]{:S(2)}) async-start(bf16[128,8,2]{0,2,1:T(2,128)(2,1)} %bitcast.192), calls=%async_computation | async-start | bytes 8192 | tf_op jit(solution)/shard_map/all_to_all | solution.py:255
  20.0 35.3 %copy-start.6 = (bf16[4,256]{1,0:T(4,128)(2,1)S(1)}, bf16[4,256]{1,0:T(4,128)(2,1)}, u32[]{:S(2)}) copy-start(bf16[4,256]{1,0:T(4,128)(2,1)} %param.18) | copy-start | bytes 6148
  20.0 35.3 %copy-start.7 = (bf16[4,128]{1,0:T(4,128)(2,1)S(1)}, bf16[4,128]{1,0:T(4,128)(2,1)}, u32[]{:S(2)}) copy-start(bf16[4,128]{1,0:T(4,128)(2,1)} %param.17) | copy-start | bytes 3076
  20.0 35.3 %copy-start.8 = (bf16[4,128]{1,0:T(4,128)(2,1)S(1)}, bf16[4,128]{1,0:T(4,128)(2,1)}, u32[]{:S(2)}) copy-start(bf16[4,128]{1,0:T(4,128)(2,1)} %param.16) | copy-start | bytes 3076
  26.3 12.8 %all-to-all-start.2 = ((bf16[128,8,128]{0,2,1:T(8,128)(2,1)}), bf16[128,8,128]{0,2,1:T(8,128)(2,1)S(1)}, u32[]{:S(2)}, u32[]{:S(2)}) async-start(bf16[128,8,128]{0,2,1:T(8,128)(2,1)} %bitcast.6), calls=%async_computation.2 | async-start | bytes 524288 | tf_op jit(solution)/shard_map/all_to_all | solution.py:252
  39.1 12.7 %all-to-all-start.1 = ((bf16[128,8,128]{0,2,1:T(8,128)(2,1)}), bf16[128,8,128]{0,2,1:T(8,128)(2,1)S(1)}, u32[]{:S(2)}, u32[]{:S(2)}) async-start(bf16[128,8,128]{0,2,1:T(8,128)(2,1)} %bitcast.3), calls=%async_computation.1 | async-start | bytes 524288 | tf_op jit(solution)/shard_map/all_to_all | solution.py:251
  51.8 15.7 %all-to-all-start.3 = ((bf16[128,8,256]{0,2,1:T(8,128)(2,1)}), bf16[128,8,256]{0,2,1:T(8,128)(2,1)S(1)}, u32[]{:S(2)}, u32[]{:S(2)}) async-start(bf16[128,8,256]{0,2,1:T(8,128)(2,1)} %bitcast.9), calls=%async_computation.3 | async-start | bytes 1048576 | tf_op jit(solution)/shard_map/all_to_all | solution.py:253
  69.3 9.4 %collective-permute-start = (bf16[3,512]{1,0:T(4,128)(2,1)S(1)}, bf16[3,512]{1,0:T(4,128)(2,1)S(1)}, u32[]{:S(2)}, u32[]{:S(2)}) collective-permute-start(bf16[3,512]{1,0:T(4,128)(2,1)S(1)} %slice.153), channel_id=1, source_target_pairs={{0,8},{8,16},{16,24},{24,32},{32,40},{40,48},{48,56},{56,64},{64,7... | collective-permute-start | bytes 9224 | tf_op jit(solution)/shard_map/ppermute | solution.py:20
  132.7 1.3 copy-start.3
  136.4 1.4 copy-start.1
  138.5 16.6 %collective-permute-start.1 = (f32[2,2,128,128]{3,2,1,0:T(8,128)}, f32[2,2,128,128]{3,2,1,0:T(8,128)}, u32[]{:S(2)}, u32[]{:S(2)}) collective-permute-start(f32[2,2,128,128]{3,2,1,0:T(8,128)} %pad_maximum_fusion.6), channel_id=1, source_target_pairs={{0,8},{8,16},{16,24},{24,32},{32,40},{40,48},{48,56},{56,64},{64,7... | collective-permute-start | bytes 786440 | tf_op jit(solution)/shard_map/ppermute | solution.py:20
  148.9 86.3 %all-to-all-start.5 = ((bf16[128,8,256]{2,0,1:T(8,128)(2,1)}), bf16[128,8,256]{2,0,1:T(8,128)(2,1)}, u32[]{:S(2)}, u32[]{:S(2)}) async-start(bf16[128,8,256]{2,0,1:T(8,128)(2,1)} %copy.139), calls=%async_computation.5 | async-start | bytes 1048576 | tf_op jit(solution)/shard_map/all_to_all | solution.py:254
  153.3 1.6 copy-start.4
  154.8 1.6 copy-start.2
  158.8 8.4 %collective-permute-start.2 = (f32[2,2,128,128]{3,2,1,0:T(8,128)S(1)}, f32[2,2,128,128]{3,2,1,0:T(8,128)S(1)}, u32[]{:S(2)}, u32[]{:S(2)}) collective-permute-start(f32[2,2,128,128]{3,2,1,0:T(8,128)S(1)} %pad_maximum_fusion.7), channel_id=1, source_target_pairs={{0,16},{8,24},{16,32},{24,40},{32,48},{40,56},{48,64},{56,72},{64,... | collective-permute-start | bytes 786440 | tf_op jit(solution)/shard_map/ppermute | solution.py:20
  167.8 11.0 %collective-permute-start.3 = (f32[2,2,128,128]{3,2,1,0:T(8,128)S(1)}, f32[2,2,128,128]{3,2,1,0:T(8,128)S(1)}, u32[]{:S(2)}, u32[]{:S(2)}) collective-permute-start(f32[2,2,128,128]{3,2,1,0:T(8,128)S(1)} %pad_maximum_fusion.8), channel_id=1, source_target_pairs={{0,32},{8,40},{16,48},{24,56},{32,64},{40,72},{48,80},{56,88},{64,... | collective-permute-start | bytes 786440 | tf_op jit(solution)/shard_map/ppermute | solution.py:20
  179.4 14.5 %collective-permute-start.4 = (f32[2,2,128,128]{3,2,1,0:T(8,128)S(1)}, f32[2,2,128,128]{3,2,1,0:T(8,128)S(1)}, u32[]{:S(2)}, u32[]{:S(2)}) collective-permute-start(f32[2,2,128,128]{3,2,1,0:T(8,128)S(1)} %pad_maximum_fusion.9), channel_id=1, source_target_pairs={{0,64},{8,72},{16,80},{24,88},{32,96},{40,104},{48,112},{56,120},{... | collective-permute-start | bytes 786440 | tf_op jit(solution)/shard_map/ppermute | solution.py:20
  194.5 31.7 %slice-start = ((f32[16,2,128,128]{3,2,1,0:T(8,128)}), f32[15,2,128,128]{3,2,1,0:T(8,128)S(1)}, s32[]{:S(2)}) async-start(f32[16,2,128,128]{3,2,1,0:T(8,128)} %copy-done.1), calls=%async_computation.7 | async-start | bytes 3932160 | tf_op jit(solution)/shard_map/slice | solution.py:300
  194.5 6.7 %collective-permute-start.5 = (f32[2,2,128,128]{3,2,1,0:T(8,128)S(1)}, f32[2,2,128,128]{3,2,1,0:T(8,128)S(1)}, u32[]{:S(2)}, u32[]{:S(2)}) collective-permute-start(f32[2,2,128,128]{3,2,1,0:T(8,128)S(1)} %pad_maximum_fusion.10), channel_id=1, source_target_pairs={{0,128},{8,136},{16,144},{24,152},{32,160},{40,168},{48,176},{56,1... | collective-permute-start | bytes 786440 | tf_op jit(solution)/shard_map/ppermute | solution.py:20
  201.4 26.8 %collective-permute-start.7 = (f32[2,128,128]{2,1,0:T(8,128)S(1)}, f32[2,128,128]{2,1,0:T(8,128)S(1)}, u32[]{:S(2)}, u32[]{:S(2)}) collective-permute-start(f32[2,128,128]{2,1,0:T(8,128)S(1)} %convolution_add_fusion.1), channel_id=1, source_target_pairs={{0,264},{8,272},{16,280},{24,288},{32,296},{40,304},{48,312},{56,3... | collective-permute-start | bytes 393224 | tf_op jit(solution)/shard_map/ppermute | solution.py:20
  224.0 5.2 %collective-permute-start.6 = (f32[2,2,128,128]{3,2,1,0:T(8,128)S(1)}, f32[2,2,128,128]{3,2,1,0:T(8,128)S(1)}, u32[]{:S(2)}, u32[]{:S(2)}) collective-permute-start(f32[2,2,128,128]{3,2,1,0:T(8,128)S(1)} %pad_maximum_fusion.11), channel_id=1, source_target_pairs={{0,8},{8,16},{16,24},{24,32},{32,40},{40,48},{48,56},{56,64},{64,7... | collective-permute-start | bytes 786440 | tf_op jit(solution)/shard_map/ppermute | solution.py:20

commit v3 on v2

--- a/solution.py
+++ b/solution.py
@@ -1,6 +1,10 @@
+import functools
+
 import jax
 import jax.numpy as jnp
 from jax import lax
+from jax.experimental import pallas as pl
+from jax.experimental.pallas import tpu as pltpu
 from jax.sharding import PartitionSpec as P
 
 DK = 128
@@ -128,6 +132,133 @@
 
 def compose_maps(later_map, earlier_map):
     return jnp.einsum("hij,hjk->hik", later_map, earlier_map, precision=HIGHEST_PRECISION)
+
+
+MESH_IDS = pl.DeviceIdType.MESH
+
+
+def scan_spans(count):
+    spans = []
+    span = 1
+    while 2 * span < count:
+        spans.append(span)
+        span *= 2
+    return spans, span + 1
+
+
+def kernel_dot(left, right):
+    return jnp.dot(left, right, preferred_element_type=jnp.float32, precision=HIGHEST_PRECISION)
+
+
+def ctx_scan_kernel(count, maps_ref, out_ref, current, slots, near_slot, far_slot, send_sems, recv_sems):
+    place = lax.axis_index("ctx")
+    group = lax.axis_index("head")
+    heads = maps_ref.shape[1]
+    spans, far = scan_spans(count)
+    offsets = sorted(set(spans + [1] + ([far] if far < count else [])))
+    barrier = pltpu.get_barrier_semaphore()
+    partners = jnp.int32(0)
+    for offset in offsets:
+        for target in (place + offset, place - offset):
+            valid = jnp.logical_and(target >= 0, target < count)
+
+            @pl.when(valid)
+            def _():
+                pl.semaphore_signal(barrier, inc=1, device_id=(target, group), device_id_type=MESH_IDS)
+
+            partners = partners + valid.astype(jnp.int32)
+    pl.semaphore_wait(barrier, partners)
+
+    source = maps_ref
+    for index, span in enumerate(spans):
+        sending = place + span < count
+        receiving = place >= span
+        copy_out = pltpu.make_async_remote_copy(
+            src_ref=source,
+            dst_ref=slots.at[index],
+            send_sem=send_sems.at[index],
+            recv_sem=recv_sems.at[index],
+            device_id=(place + span, group),
+            device_id_type=MESH_IDS,
+        )
+        pl.when(sending)(copy_out.start)
+        pl.when(receiving)(copy_out.wait_recv)
+        dest = current.at[index % 2]
+
+        def composed(source=source, dest=dest, index=index):
+            for head in range(heads):
+                trans_here = source[0, head]
+                dest[0, head] = kernel_dot(trans_here, slots[index, 0, head])
+                dest[1, head] = kernel_dot(trans_here, slots[index, 1, head]) + source[1, head]
+
+        def kept(source=source, dest=dest):
+            dest[...] = source[...]
+
+        pl.when(receiving)(composed)
+        pl.when(jnp.logical_not(receiving))(kept)
+        pl.when(sending)(copy_out.wait_send)
+        source = dest
+
+    last = len(spans)
+    near_copy = pltpu.make_async_remote_copy(
+        src_ref=source,
+        dst_ref=near_slot,
+        send_sem=send_sems.at[last],
+        recv_sem=recv_sems.at[last],
+        device_id=(place + 1, group),
+        device_id_type=MESH_IDS,
+    )
+    pl.when(place + 1 < count)(near_copy.start)
+    if far < count:
+        far_copy = pltpu.make_async_remote_copy(
+            src_ref=source.at[1],
+            dst_ref=far_slot,
+            send_sem=send_sems.at[last + 1],
+            recv_sem=recv_sems.at[last + 1],
+            device_id=(place + far, group),
+            device_id_type=MESH_IDS,
+        )
+        pl.when(place + far < count)(far_copy.start)
+    pl.when(place >= 1)(near_copy.wait_recv)
+    out_ref[...] = jnp.zeros_like(out_ref)
+
+    def from_near():
+        out_ref[...] = near_slot[1]
+
+    pl.when(place >= 1)(from_near)
+    if far < count:
+        pl.when(place >= far)(far_copy.wait_recv)
+
+        def from_far():
+            for head in range(heads):
+                out_ref[head] = out_ref[head] + kernel_dot(near_slot[0, head], far_slot[head])
+
+        pl.when(place >= far)(from_far)
+        pl.when(place + far < count)(far_copy.wait_send)
+    pl.when(place + 1 < count)(near_copy.wait_send)
+
+
+def ctx_scan(maps):
+    count = lax.axis_size("ctx")
+    if count == 1:
+        return jnp.zeros_like(maps[1])
+    spans, far = scan_spans(count)
+    side = maps.shape[1:]
+    return pl.pallas_call(
+        functools.partial(ctx_scan_kernel, count),
+        out_shape=jax.ShapeDtypeStruct(side, jnp.float32),
+        in_specs=[pl.BlockSpec(memory_space=pltpu.VMEM)],
+        out_specs=pl.BlockSpec(memory_space=pltpu.VMEM),
+        scratch_shapes=[
+            pltpu.VMEM((2,) + maps.shape, jnp.float32),
+            pltpu.VMEM((max(len(spans), 1),) + maps.shape, jnp.float32),
+            pltpu.VMEM(maps.shape, jnp.float32),
+            pltpu.VMEM(side, jnp.float32),
+            pltpu.SemaphoreType.DMA((len(spans) + 2,)),
+            pltpu.SemaphoreType.DMA((len(spans) + 2,)),
+        ],
+        compiler_params=pltpu.CompilerParams(collective_id=0, has_side_effects=True),
+    )(maps)
 
 
 def on_device(
@@ -233,6 +364,133 @@
 
 def compose_maps(later_map, earlier_map):
     return jnp.einsum("hij,hjk->hik", later_map, earlier_map, precision=HIGHEST_PRECISION)
+
+
+MESH_IDS = pl.DeviceIdType.MESH
+
+
+def scan_spans(count):
+    spans = []
+    span = 1
+    while 2 * span < count:
+        spans.append(span)
+        span *= 2
+    return spans, span + 1
+
+
+def kernel_dot(left, right):
+    return jnp.dot(left, right, preferred_element_type=jnp.float32, precision=HIGHEST_PRECISION)
+
+
+def ctx_scan_kernel(count, maps_ref, out_ref, current, slots, near_slot, far_slot, send_sems, recv_sems):
+    place = lax.axis_index("ctx")
+    group = lax.axis_index("head")
+    heads = maps_ref.shape[1]
+    spans, far = scan_spans(count)
+    offsets = sorted(set(spans + [1] + ([far] if far < count else [])))
+    barrier = pltpu.get_barrier_semaphore()
+    partners = jnp.int32(0)
+    for offset in offsets:
+        for target in (place + offset, place - offset):
+            valid = jnp.logical_and(target >= 0, target < count)
+
+            @pl.when(valid)
+            def _():
+                pl.semaphore_signal(barrier, inc=1, device_id=(target, group), device_id_type=MESH_IDS)
+
+            partners = partners + valid.astype(jnp.int32)
+    pl.semaphore_wait(barrier, partners)
+
+    source = maps_ref
+    for index, span in enumerate(spans):
+        sending = place + span < count
+        receiving = place >= span
+        copy_out = pltpu.make_async_remote_copy(
+            src_ref=source,
+            dst_ref=slots.at[index],
+            send_sem=send_sems.at[index],
+            recv_sem=recv_sems.at[index],
+            device_id=(place + span, group),
+            device_id_type=MESH_IDS,
+        )
+        pl.when(sending)(copy_out.start)
+        pl.when(receiving)(copy_out.wait_recv)
+        dest = current.at[index % 2]
+
+        def composed(source=source, dest=dest, index=index):
+            for head in range(heads):
+                trans_here = source[0, head]
+                dest[0, head] = kernel_dot(trans_here, slots[index, 0, head])
+                dest[1, head] = kernel_dot(trans_here, slots[index, 1, head]) + source[1, head]
+
+        def kept(source=source, dest=dest):
+            dest[...] = source[...]
+
+        pl.when(receiving)(composed)
+        pl.when(jnp.logical_not(receiving))(kept)
+        pl.when(sending)(copy_out.wait_send)
+        source = dest
+
+    last = len(spans)
+    near_copy = pltpu.make_async_remote_copy(
+        src_ref=source,
+        dst_ref=near_slot,
+        send_sem=send_sems.at[last],
+        recv_sem=recv_sems.at[last],
+        device_id=(place + 1, group),
+        device_id_type=MESH_IDS,
+    )
+    pl.when(place + 1 < count)(near_copy.start)
+    if far < count:
+        far_copy = pltpu.make_async_remote_copy(
+            src_ref=source.at[1],
+            dst_ref=far_slot,
+            send_sem=send_sems.at[last + 1],
+            recv_sem=recv_sems.at[last + 1],
+            device_id=(place + far, group),
+            device_id_type=MESH_IDS,
+        )
+        pl.when(place + far < count)(far_copy.start)
+    pl.when(place >= 1)(near_copy.wait_recv)
+    out_ref[...] = jnp.zeros_like(out_ref)
+
+    def from_near():
+        out_ref[...] = near_slot[1]
+
+    pl.when(place >= 1)(from_near)
+    if far < count:
+        pl.when(place >= far)(far_copy.wait_recv)
+
+        def from_far():
+            for head in range(heads):
+                out_ref[head] = out_ref[head] + kernel_dot(near_slot[0, head], far_slot[head])
+
+        pl.when(place >= far)(from_far)
+        pl.when(place + far < count)(far_copy.wait_send)
+    pl.when(place + 1 < count)(near_copy.wait_send)
+
+
+def ctx_scan(maps):
+    count = lax.axis_size("ctx")
+    if count == 1:
+        return jnp.zeros_like(maps[1])
+    spans, far = scan_spans(count)
+    side = maps.shape[1:]
+    return pl.pallas_call(
+        functools.partial(ctx_scan_kernel, count),
+        out_shape=jax.ShapeDtypeStruct(side, jnp.float32),
+        in_specs=[pl.BlockSpec(memory_space=pltpu.VMEM)],
+        out_specs=pl.BlockSpec(memory_space=pltpu.VMEM),
+        scratch_shapes=[
+            pltpu.VMEM((2,) + maps.shape, jnp.float32),
+            pltpu.VMEM((max(len(spans), 1),) + maps.shape, jnp.float32),
+            pltpu.VMEM(maps.shape, jnp.float32),
+            pltpu.VMEM(side, jnp.float32),
+            pltpu.SemaphoreType.DMA((len(spans) + 2,)),
+            pltpu.SemaphoreType.DMA((len(spans) + 2,)),
+        ],
+        compiler_params=pltpu.CompilerParams(collective_id=0, has_side_effects=True),
+    )(maps)
 
 
 def on_device(
@@ -306,22 +564,7 @@
     reach = query_decay - matmul("nhij,nhjd->nhid", within, key_part)
     carry_map = matmul("nhcd,nhde->nhce", reach, earlier_trans)
     total_trans, total_bias = trans[-1], bias[-1]
-    place = lax.axis_index("ctx")
-    count = lax.axis_size("ctx")
-    span = 1
-    while 2 * span < count:
-        arrived = passed_along(jnp.stack([total_trans, total_bias]), "ctx", span)
-        total_trans, total_bias = (
-            jnp.where(place >= span, compose_maps(total_trans, arrived[0]), total_trans),
-            compose_maps(total_trans, arrived[1]) + total_bias,
-        )
-        span *= 2
-    initial = jnp.zeros_like(total_bias)
-    if count > 1:
-        near = passed_along(jnp.stack([total_trans, total_bias]), "ctx", 1)
-        initial = near[1]
-        if span + 1 < count:
-            initial = compose_maps(near[0], passed_along(total_bias, "ctx", span + 1)) + initial
+    initial = ctx_scan(jnp.stack([total_trans, total_bias]))
     produced = local_result + matmul("nhcd,hde->nhce", carry_map, initial)
     outputs = produced.transpose(0, 2, 1, 3).reshape(count_rows, heads_here, DV)
     gate = local_gate.astype(jnp.float32).reshape(count_rows, heads_here, DV)

time: 267 us -> 263 us (0.985)
  the two profiles are of different devices: /device:TPU:57 before, /device:TPU:14 now
where the time goes in v3:
time: 263 us; the launch traced here: 259 us
  Pallas kernels  67.8 us (26%)
  matrix products  60.3 us (23%)
  waiting for transfers between devices  43.9 us (17%)
  starting transfers between devices  30.1 us (11%)
  blocking collectives  22.5 us (9%)
  local copies, waits for them, and re-layouts  19 us (7%)
  other arithmetic  14.1 us (5%)
    pallas_call x1, Pallas kernels, ctx_scan(): pl.pallas_call(functools.partial(ctx_scan_kernel, count), out_shape=jax.S...  67.8 us
    dot_general x29, matrix products, matmul(): return jnp.einsum(spec, left, right, precision=HIGHEST_PRECISION)  55.7 us
    all_to_all x1, blocking collectives, on_device(): lax.all_to_all(normed, 'head', split_axis=0, concat_axis=1, tiled=True)  22.5 us
    all_to_all x1, waiting for transfers between devices, on_device(): lax.all_to_all(value_rows, 'head', split_axis=1, concat_axis=0, tiled=True)  10.7 us
    all_to_all x1, starting transfers between devices, on_device(): lax.all_to_all(log_decay, 'head', split_axis=1, concat_axis=0, tiled=True)  10.4 us
    all_to_all x1, waiting for transfers between devices, on_device(): lax.all_to_all(key_rows, 'head', split_axis=1, concat_axis=0, tiled=True)  9.18 us
    unnamed x41, local copies, waits for them, and re-layouts  8.55 us
    all_to_all x1, waiting for transfers between devices, on_device(): lax.all_to_all(query_rows, 'head', split_axis=1, concat_axis=0, tiled=True)  8.41 us
  transfers between devices with their start and end apart: 7, of which 6 were waited for; matrix products, arithmetic and copies ran while one was open for 34% of the time, Pallas kernels for 26%

profile of v3, /device:TPU:14, one launch (start us, length us, event | category | flops | bytes accessed | tf_op | source)
XLA Modules:
  0.0 258.8 jit_solution(8295678948441448457)
XLA Ops:
  0.0 10.4 %all-to-all-start = ((bf16[128,8,2]{0,2,1:T(2,128)(2,1)}), bf16[128,8,2]{0,2,1:T(2,128)(2,1)S(1)}, u32[]{:S(2)}, u32[]{:S(2)}) async-start(bf16[128,8,2]{0,2,1:T(2,128)(2,1)} %bitcast.118), calls=%async_computation | async-start | bytes 8192 | tf_op jit(solution)/shard_map/all_to_all | solution.py:513
  10.8 7.3 %all-to-all-done = bf16[128,8,2]{0,2,1:T(2,128)(2,1)S(1)} async-done(((bf16[128,8,2]{0,2,1:T(2,128)(2,1)}), bf16[128,8,2]{0,2,1:T(2,128)(2,1)S(1)}, u32[]{:S(2)}, u32[]{:S(2)}) %all-to-all-start) | async-done | bytes 4128 | tf_op jit(solution)/shard_map/all_to_all | solution.py:513
  18.1 3.3 %all-to-all-start.4 = ((bf16[128,8,2]{0,2,1:T(2,128)(2,1)}), bf16[128,8,2]{0,2,1:T(2,128)(2,1)S(1)}, u32[]{:S(2)}, u32[]{:S(2)}) async-start(bf16[128,8,2]{0,2,1:T(2,128)(2,1)} %bitcast.119), calls=%async_computation.4 | async-start | bytes 8192 | tf_op jit(solution)/shard_map/all_to_all | solution.py:514
  21.4 1.9 copy.117
  23.3 5.6 %all-to-all-done.4 = bf16[128,8,2]{0,2,1:T(2,128)(2,1)S(1)} async-done(((bf16[128,8,2]{0,2,1:T(2,128)(2,1)}), bf16[128,8,2]{0,2,1:T(2,128)(2,1)S(1)}, u32[]{:S(2)}, u32[]{:S(2)}) %all-to-all-start.4) | async-done | bytes 4128 | tf_op jit(solution)/shard_map/all_to_all | solution.py:514
  28.9 3.4 %all-to-all-start.1 = ((bf16[128,8,128]{0,2,1:T(8,128)(2,1)}), bf16[128,8,128]{0,2,1:T(8,128)(2,1)S(1)}, u32[]{:S(2)}, u32[]{:S(2)}) async-start(bf16[128,8,128]{0,2,1:T(8,128)(2,1)} %bitcast.3), calls=%async_computation.1 | async-start | bytes 524288 | tf_op jit(solution)/shard_map/all_to_all | solution.py:509
  32.3 1.8 copy.119
  34.3 8.4 %all-to-all-done.1 = bf16[128,8,128]{0,2,1:T(8,128)(2,1)S(1)} async-done(((bf16[128,8,128]{0,2,1:T(8,128)(2,1)}), bf16[128,8,128]{0,2,1:T(8,128)(2,1)S(1)}, u32[]{:S(2)}, u32[]{:S(2)}) %all-to-all-start.1) | async-done | bytes 262176 | tf_op jit(solution)/shard_map/all_to_all | solution.py:509
  42.7 3.4 %all-to-all-start.2 = ((bf16[128,8,128]{0,2,1:T(8,128)(2,1)}), bf16[128,8,128]{0,2,1:T(8,128)(2,1)S(1)}, u32[]{:S(2)}, u32[]{:S(2)}) async-start(bf16[128,8,128]{0,2,1:T(8,128)(2,1)} %bitcast.6), calls=%async_computation.2 | async-start | bytes 524288 | tf_op jit(solution)/shard_map/all_to_all | solution.py:510
  46.2 1.0 copy.121
  47.3 9.2 %all-to-all-done.2 = bf16[128,8,128]{0,2,1:T(8,128)(2,1)S(1)} async-done(((bf16[128,8,128]{0,2,1:T(8,128)(2,1)}), bf16[128,8,128]{0,2,1:T(8,128)(2,1)S(1)}, u32[]{:S(2)}, u32[]{:S(2)}) %all-to-all-start.2) | async-done | bytes 262176 | tf_op jit(solution)/shard_map/all_to_all | solution.py:510
  56.5 3.5 %all-to-all-start.3 = ((bf16[128,8,256]{0,2,1:T(8,128)(2,1)}), bf16[128,8,256]{0,2,1:T(8,128)(2,1)S(1)}, u32[]{:S(2)}, u32[]{:S(2)}) async-start(bf16[128,8,256]{0,2,1:T(8,128)(2,1)} %bitcast.9), calls=%async_computation.3 | async-start | bytes 1048576 | tf_op jit(solution)/shard_map/all_to_all | solution.py:511
  60.3 1.0 copy.139
  62.6 10.7 %all-to-all-done.3 = bf16[128,8,256]{0,2,1:T(8,128)(2,1)S(1)} async-done(((bf16[128,8,256]{0,2,1:T(8,128)(2,1)}), bf16[128,8,256]{0,2,1:T(8,128)(2,1)S(1)}, u32[]{:S(2)}, u32[]{:S(2)}) %all-to-all-start.3) | async-done | bytes 524320 | tf_op jit(solution)/shard_map/all_to_all | solution.py:511
  73.2 4.1 %all-to-all-start.5 = ((bf16[128,8,256]{2,0,1:T(8,128)(2,1)}), bf16[128,8,256]{2,0,1:T(8,128)(2,1)}, u32[]{:S(2)}, u32[]{:S(2)}) async-start(bf16[128,8,256]{2,0,1:T(8,128)(2,1)} %copy.139), calls=%async_computation.5 | async-start | bytes 1048576 | tf_op jit(solution)/shard_map/all_to_all | solution.py:512
  77.6 1.7 pad_maximum_fusion.5
  79.3 1.9 collective-permute-start
  81.5 2.7 %collective-permute-done = bf16[3,512]{1,0:T(4,128)(2,1)S(1)} collective-permute-done((bf16[3,512]{1,0:T(4,128)(2,1)S(1)}, bf16[3,512]{1,0:T(4,128)(2,1)S(1)}, u32[]{:S(2)}, u32[]{:S(2)}) %collective-permute-start) | collective-permute-done | bytes 3104 | tf_op jit(solution)/shard_map/ppermute | solution.py:24
  84.2 5.2 %divide_multiply_fusion = f32[1024,512]{1,0:T(8,128)S(1)} fusion(f32[1024,512]{1,0:T(8,128)} %get-tuple-element.10, f32[3,512]{1,0:T(4,128)S(1)} %convert_element_type.63, f32[512]{0:T(512)S(1)} %bitcast.115, f32[512]{0:T(512)S(1)} %bitcast.116, f32[512]{0:T(512)S(1)} %bitcast.117, f32[512]{0:T(512)S(1)} %bitcast.114), kind=kLoop, calls=%fused_computation.42 | loop fusion | flops 7340032 | bytes 4208640 | tf_op jit(solution)/shard_map/jit(silu)/mul | solution.py:65
  89.8 1.2 divide_multiply_fusion.1
  90.9 1.8 fusion.74
  92.8 1.1 fusion.90
  93.8 1.0 fusion.108
  94.9 1.2 fusion.88
  96.1 1.3 fusion.97
  97.6 1.2 fusion.86
  98.8 1.2 fusion.157
  100.2 1.2 fusion.84
  101.4 1.4 fusion.158
  103.0 1.2 fusion.82
  104.2 1.2 fusion.159
  105.6 1.2 fusion.80
  106.8 2.2 fusion.160
  108.9 1.3 broadcast_multiply_fusion
  110.3 0.5 reshape_reshape.2
  111.2 0.9 copy-done.10
  112.4 1.9 fusion.10
  114.3 4.2 %fusion.52 = f32[16,2,128,128]{3,2,1,0:T(8,128)S(1)} fusion(f32[16,2,64,256]{3,2,1,0:T(8,128)S(1)} %fusion.10, f32[16,64,128]{2,1,0:T(8,128)S(1)} %bitcast.95, f32[16,2,64]{2,1,0:T(2,128)S(1)} %copy.124), kind=kOutput, calls=%fused_computation.51 | convolution fusion | flops 402915328 | bytes 3686400 | tf_op jit(solution)/shard_map/nhcd,nhce->nhde/dot_general | solution.py:28
  118.7 4.0 %multiply_subtract_fusion = f32[16,2,128,128]{3,2,1,0:T(8,128)S(1)} fusion(f32[128,128]{1,0:T(8,128)S(1)} %fusion.127, f32[16,2]{1,0:T(8,128)S(1)} %copy.123, f32[16,2,64,256]{3,2,1,0:T(8,128)S(1)} %fusion.10, f32[16,64,128]{2,1,0:T(8,128)S(1)} %bitcast.96, f32[16,2,64]{2,1,0:T(2,128)S(1)} %copy.124), kind=kOutput, calls=%fused_computation.41 | convolution fusion | flops 403963904 | bytes 3760128 | tf_op jit(solution)/shard_map/nhcd,nhce->nhde/dot_general | solution.py:28
  122.9 2.3 fusion.40
  125.4 2.3 fusion
  127.8 2.3 fusion.43
  130.3 2.4 fusion.15
  132.9 2.2 fusion.46
  135.3 2.2 fusion.19
  137.5 2.1 fusion.49
  139.7 1.7 slice.126
  141.8 2.3 fusion.23
  144.1 1.3 copy-done.4
  145.5 2.7 %convolution_multiply_fusion = f32[16,2,64,64]{3,2,1,0:T(8,128)} fusion(f32[16,2,64]{2,1,0:T(2,128)S(1)} %copy.127, f32[16,64,128]{2,1,0:T(8,128)S(1)} %bitcast.97, f32[16,64,128]{2,1,0:T(8,128)S(1)} %bitcast.98, pred[64,64]{1,0:T(8,128)(4,1)S(1)} %get-tuple-element.22), kind=kOutput, calls=%fused_computation.61 | convolution fusion | flops 201850880 | bytes 1585152 | tf_op jit(solution)/shard_map/nhid,nhjd->nhij/dot_general | solution.py:337
  148.3 0.7 pad_maximum_fusion.6.maps_ref
  149.0 67.8 %shard_map.100 = f32[2,128,128]{2,1,0:T(8,128)} custom-call(f32[2,2,128,128]{3,2,1,0:T(8,128)} %pad_maximum_fusion.6.maps_ref), custom_call_target="tpu_custom_call" | custom-call | tf_op jit(solution)/shard_map/pallas_call | solution.py:479
  216.8 2.6 %multiply_subtract_fusion.1 = f32[16,2,64,128]{3,2,1,0:T(8,128)S(1)} fusion(f32[16,2,64,64]{3,2,1,0:T(8,128)} %convolution_multiply_fusion, f32[16,2,64,256]{3,2,1,0:T(8,128)S(1)} %fusion.10, f32[16,64,128]{2,1,0:T(8,128)S(1)} %bitcast.99, f32[16,2,64]{2,1,0:T(2,128)S(1)} %copy.116), kind=kOutput, calls=%fused_computation.54 | convolution fusion | flops 201850880 | bytes 3162112 | tf_op jit(solution)/shard_map/nhij,nhjd->nhid/dot_general | solution.py:28
  219.5 2.1 fusion.1
  221.6 1.0 convolution_bitcast_fusion
  222.7 0.5 copy-done.2
  223.1 2.0 fusion.71
  225.2 1.2 fusion.161
  226.4 3.1 %multiply_reduce_fusion = (f32[16,64,2]{1,2,0:T(2,128)S(1)}, f32[16,64,2,128]{3,1,2,0:T(8,128)}) fusion(f32[16,64,2,128]{3,1,2,0:T(8,128)S(1)} %convolution_bitcast_fusion, f32[16,2,64,128]{3,2,1,0:T(8,128)S(1)} %fusion.161, f32[15,2,128,128]{3,2,1,0:T(8,128)S(1)} %copy-done.2, f32[16,64,128]{2,1,0:T(8,128)S(1)} %bitcast.100, f32[16,2,64]{2,1,0:T(2,128)S(1)} %copy.116), kind=kOutput, calls=%fused_computation.72 | convolution fusion | flops 403961856 | bytes 5652480 | tf_op jit(solution)/shard_map/nhcd,nhde->nhce/dot_general | solution.py:28
  230.3 2.0 copy.135
  232.4 0.8 reshape.775
  233.2 1.6 fusion.92
  234.8 22.5 %all_to_all.112 = bf16[8,128,256]{2,1,0:T(8,128)(2,1)S(1)} all-to-all(bf16[8,128,256]{2,1,0:T(8,128)(2,1)S(1)} %fusion.92), channel_id=1, replica_groups=mesh['ctx'=64,'head'=8] {'head'}, dimensions={0} | all-to-all | bytes 1048576 | tf_op jit(solution)/shard_map/all_to_all | solution.py:572
  257.6 1.0 copy.141
  (113 shorter events, 7.0 us)
Async XLA Ops:
  0.0 10.6 %copy-start = (f32[128]{0:T(128)S(1)}, f32[128]{0:T(128)}, u32[]{:S(2)}) copy-start(f32[128]{0:T(128)} %param.19) | copy-start | bytes 1540
  0.0 46.1 %copy-start.13 = (bf16[128,2048]{1,0:T(8,128)(2,1)S(1)}, bf16[128,2048]{1,0:T(8,128)(2,1)}, u32[]{:S(2)}) copy-start(bf16[128,2048]{1,0:T(8,128)(2,1)} %param.12) | copy-start | bytes 1572868
  0.0 18.1 %all-to-all-start = ((bf16[128,8,2]{0,2,1:T(2,128)(2,1)}), bf16[128,8,2]{0,2,1:T(2,128)(2,1)S(1)}, u32[]{:S(2)}, u32[]{:S(2)}) async-start(bf16[128,8,2]{0,2,1:T(2,128)(2,1)} %bitcast.118), calls=%async_computation | async-start | bytes 8192 | tf_op jit(solution)/shard_map/all_to_all | solution.py:513
  18.1 10.8 %all-to-all-start.4 = ((bf16[128,8,2]{0,2,1:T(2,128)(2,1)}), bf16[128,8,2]{0,2,1:T(2,128)(2,1)S(1)}, u32[]{:S(2)}, u32[]{:S(2)}) async-start(bf16[128,8,2]{0,2,1:T(2,128)(2,1)} %bitcast.119), calls=%async_computation.4 | async-start | bytes 8192 | tf_op jit(solution)/shard_map/all_to_all | solution.py:514
  21.4 38.6 %copy-start.15 = (bf16[4,256]{1,0:T(4,128)(2,1)S(1)}, bf16[4,256]{1,0:T(4,128)(2,1)}, u32[]{:S(2)}) copy-start(bf16[4,256]{1,0:T(4,128)(2,1)} %param.18) | copy-start | bytes 6148
  21.4 38.6 %copy-start.16 = (bf16[4,128]{1,0:T(4,128)(2,1)S(1)}, bf16[4,128]{1,0:T(4,128)(2,1)}, u32[]{:S(2)}) copy-start(bf16[4,128]{1,0:T(4,128)(2,1)} %param.17) | copy-start | bytes 3076
  21.4 38.6 %copy-start.17 = (bf16[4,128]{1,0:T(4,128)(2,1)S(1)}, bf16[4,128]{1,0:T(4,128)(2,1)}, u32[]{:S(2)}) copy-start(bf16[4,128]{1,0:T(4,128)(2,1)} %param.16) | copy-start | bytes 3076
  21.4 38.6 %copy-start.14 = (bf16[128,2048]{1,0:T(8,128)(2,1)S(1)}, bf16[128,2048]{1,0:T(8,128)(2,1)}, u32[]{:S(2)}) copy-start(bf16[128,2048]{1,0:T(8,128)(2,1)} %param.13) | copy-start | bytes 1572868
  28.9 13.8 %all-to-all-start.1 = ((bf16[128,8,128]{0,2,1:T(8,128)(2,1)}), bf16[128,8,128]{0,2,1:T(8,128)(2,1)S(1)}, u32[]{:S(2)}, u32[]{:S(2)}) async-start(bf16[128,8,128]{0,2,1:T(8,128)(2,1)} %bitcast.3), calls=%async_computation.1 | async-start | bytes 524288 | tf_op jit(solution)/shard_map/all_to_all | solution.py:509
  42.7 13.8 %all-to-all-start.2 = ((bf16[128,8,128]{0,2,1:T(8,128)(2,1)}), bf16[128,8,128]{0,2,1:T(8,128)(2,1)S(1)}, u32[]{:S(2)}, u32[]{:S(2)}) async-start(bf16[128,8,128]{0,2,1:T(8,128)(2,1)} %bitcast.6), calls=%async_computation.2 | async-start | bytes 524288 | tf_op jit(solution)/shard_map/all_to_all | solution.py:510
  56.5 16.7 %all-to-all-start.3 = ((bf16[128,8,256]{0,2,1:T(8,128)(2,1)}), bf16[128,8,256]{0,2,1:T(8,128)(2,1)S(1)}, u32[]{:S(2)}, u32[]{:S(2)}) async-start(bf16[128,8,256]{0,2,1:T(8,128)(2,1)} %bitcast.9), calls=%async_computation.3 | async-start | bytes 1048576 | tf_op jit(solution)/shard_map/all_to_all | solution.py:511
  73.2 160.0 %all-to-all-start.5 = ((bf16[128,8,256]{2,0,1:T(8,128)(2,1)}), bf16[128,8,256]{2,0,1:T(8,128)(2,1)}, u32[]{:S(2)}, u32[]{:S(2)}) async-start(bf16[128,8,256]{2,0,1:T(8,128)(2,1)} %copy.139), calls=%async_computation.5 | async-start | bytes 1048576 | tf_op jit(solution)/shard_map/all_to_all | solution.py:512
  79.3 4.9 %collective-permute-start = (bf16[3,512]{1,0:T(4,128)(2,1)S(1)}, bf16[3,512]{1,0:T(4,128)(2,1)S(1)}, u32[]{:S(2)}, u32[]{:S(2)}) collective-permute-start(bf16[3,512]{1,0:T(4,128)(2,1)S(1)} %slice.105), channel_id=1, source_target_pairs={{0,8},{8,16},{16,24},{24,32},{32,40},{40,48},{48,56},{56,64},{64,7... | collective-permute-start | bytes 9224 | tf_op jit(solution)/shard_map/ppermute | solution.py:24
  89.4 1.5 copy-start.3
  90.9 18.0 %copy-start.6 = (f32[1024,128]{1,0:T(8,128)}, f32[1024,128]{1,0:T(8,128)S(1)}, u32[]{:S(2)}) copy-start(f32[1024,128]{1,0:T(8,128)S(1)} %get-tuple-element.8) | copy-start | bytes 1572868
  106.8 3.5 %slice-start = ((f32[1024,512]{1,0:T(8,128)}), f32[1024,256]{1,0:T(8,128)S(1)}, s32[]{:S(2)}) async-start(f32[1024,512]{1,0:T(8,128)} %copy-done.3), calls=%async_computation.7 | async-start | bytes 2097152 | tf_op jit(solution)/shard_map/slice | solution.py:531
  110.8 1.2 copy-start.10
  110.8 1.5 copy-start.11
  112.4 1.9 copy-start.7
  139.7 2.0 copy-start.5
  144.1 1.4 copy-start.4
  144.1 1.4 copy-start.8
  145.5 2.8 %slice-start.3 = ((f32[16,2,128,128]{3,2,1,0:T(8,128)}), f32[1,2,128,128]{3,2,1,0:T(8,128)S(1)}, s32[]{:S(2)}) async-start(f32[16,2,128,128]{3,2,1,0:T(8,128)} %copy-done.5), calls=%async_computation.10 | async-start | bytes 262144 | tf_op jit(solution)/shard_map/slice | solution.py:566
  145.5 2.8 %slice-start.1 = ((f32[16,2,128,128]{3,2,1,0:T(8,128)}), f32[1,2,128,128]{3,2,1,0:T(8,128)S(1)}, s32[]{:S(2)}) async-start(f32[16,2,128,128]{3,2,1,0:T(8,128)} %copy-done.4), calls=%async_computation.8 | async-start | bytes 262144 | tf_op jit(solution)/shard_map/slice | solution.py:566
  216.8 2.6 %slice-start.2 = ((f32[16,2,128,128]{3,2,1,0:T(8,128)}), f32[15,2,128,128]{3,2,1,0:T(8,128)S(1)}, s32[]{:S(2)}) async-start(f32[16,2,128,128]{3,2,1,0:T(8,128)} %copy-done.4), calls=%async_computation.9 | async-start | bytes 3932160 | tf_op jit(solution)/shard_map/slice | solution.py:558
  219.5 2.1 copy-start.12
  221.6 1.5 copy-start.2
  223.1 2.0 copy-start.9
  233.2 25.4 %copy-start.1 = (f32[128]{0:T(128)S(1)}, f32[128]{0:T(128)}, u32[]{:S(2)}) copy-start(f32[128]{0:T(128)} %param.19) | copy-start | bytes 1540

commit v4 on v1

--- a/solution.py
+++ b/solution.py
@@ -1,6 +1,10 @@
+import functools
+
 import jax
 import jax.numpy as jnp
 from jax import lax
+from jax.experimental import pallas as pl
+from jax.experimental.pallas import tpu as pltpu
 from jax.sharding import PartitionSpec as P
 
 DK = 128
@@ -130,6 +134,227 @@
     return jnp.einsum("hij,hjk->hik", later_map, earlier_map, precision=HIGHEST_PRECISION)
 
 
+MESH_IDS = pl.DeviceIdType.MESH
+
+
+def scan_spans(count):
+    spans = []
+    span = 1
+    while 2 * span < count:
+        spans.append(span)
+        span *= 2
+    return spans, span + 1
+
+
+def kernel_dot(left, right):
+    return jnp.dot(left, right, preferred_element_type=jnp.float32, precision=HIGHEST_PRECISION)
+
+
+def ctx_scan_kernel(count, maps_ref, out_ref, current, slots, near_slot, far_slot, send_sems, recv_sems):
+    place = lax.axis_index("ctx")
+    group = lax.axis_index("head")
+    heads = maps_ref.shape[1]
+    spans, far = scan_spans(count)
+    offsets = sorted(set(spans + [1] + ([far] if far < count else [])))
+    barrier = pltpu.get_barrier_semaphore()
+    partners = jnp.int32(0)
+    for offset in offsets:
+        for target in (place + offset, place - offset):
+            valid = jnp.logical_and(target >= 0, target < count)
+
+            @pl.when(valid)
+            def _():
+                pl.semaphore_signal(barrier, inc=1, device_id=(target, group), device_id_type=MESH_IDS)
+
+            partners = partners + valid.astype(jnp.int32)
+    pl.semaphore_wait(barrier, partners)
+
+    source = maps_ref
+    for index, span in enumerate(spans):
+        sending = place + span < count
+        receiving = place >= span
+        copy_out = pltpu.make_async_remote_copy(
+            src_ref=source,
+            dst_ref=slots.at[index],
+            send_sem=send_sems.at[index],
+            recv_sem=recv_sems.at[index],
+            device_id=(place + span, group),
+            device_id_type=MESH_IDS,
+        )
+        pl.when(sending)(copy_out.start)
+        pl.when(receiving)(copy_out.wait_recv)
+        dest = current.at[index % 2]
+
+        def composed(source=source, dest=dest, index=index):
+            for head in range(heads):
+                trans_here = source[0, head]
+                dest[0, head] = kernel_dot(trans_here, slots[index, 0, head])
+                dest[1, head] = kernel_dot(trans_here, slots[index, 1, head]) + source[1, head]
+
+        def kept(source=source, dest=dest):
+            dest[...] = source[...]
+
+        pl.when(receiving)(composed)
+        pl.when(jnp.logical_not(receiving))(kept)
+        pl.when(sending)(copy_out.wait_send)
+        source = dest
+
+    last = len(spans)
+    near_copy = pltpu.make_async_remote_copy(
+        src_ref=source,
+        dst_ref=near_slot,
+        send_sem=send_sems.at[last],
+        recv_sem=recv_sems.at[last],
+        device_id=(place + 1, group),
+        device_id_type=MESH_IDS,
+    )
+    pl.when(place + 1 < count)(near_copy.start)
+    if far < count:
+        far_copy = pltpu.make_async_remote_copy(
+            src_ref=source.at[1],
+            dst_ref=far_slot,
+            send_sem=send_sems.at[last + 1],
+            recv_sem=recv_sems.at[last + 1],
+            device_id=(place + far, group),
+            device_id_type=MESH_IDS,
+        )
+        pl.when(place + far < count)(far_copy.start)
+    pl.when(place >= 1)(near_copy.wait_recv)
+    out_ref[...] = jnp.zeros_like(out_ref)
+
+    def from_near():
+        out_ref[...] = near_slot[1]
+
+    pl.when(place >= 1)(from_near)
+    if far < count:
+        pl.when(place >= far)(far_copy.wait_recv)
+
+        def from_far():
+            for head in range(heads):
+                out_ref[head] = out_ref[head] + kernel_dot(near_slot[0, head], far_slot[head])
+
+        pl.when(place >= far)(from_far)
+        pl.when(place + far < count)(far_copy.wait_send)
+    pl.when(place + 1 < count)(near_copy.wait_send)
+
+
+def ctx_scan(maps):
+    count = lax.axis_size("ctx")
+    if count == 1:
+        return jnp.zeros_like(maps[1])
+    spans, far = scan_spans(count)
+    side = maps.shape[1:]
+    return pl.pallas_call(
+        functools.partial(ctx_scan_kernel, count),
+        out_shape=jax.ShapeDtypeStruct(side, jnp.float32),
+        in_specs=[pl.BlockSpec(memory_space=pltpu.VMEM)],
+        out_specs=pl.BlockSpec(memory_space=pltpu.VMEM),
+        scratch_shapes=[
+            pltpu.VMEM((2,) + maps.shape, jnp.float32),
+            pltpu.VMEM((max(len(spans), 1),) + maps.shape, jnp.float32),
+            pltpu.VMEM(maps.shape, jnp.float32),
+            pltpu.VMEM(side, jnp.float32),
+            pltpu.SemaphoreType.DMA((len(spans) + 2,)),
+            pltpu.SemaphoreType.DMA((len(spans) + 2,)),
+        ],
+        compiler_params=pltpu.CompilerParams(collective_id=0, has_side_effects=True),
+    )(maps)
+
+
+def head_exchange_kernel(parts, count, source_view, target_view, *refs):
+    sources, targets = refs[:count], refs[count : 2 * count]
+    send_sems, recv_sems = refs[2 * count], refs[2 * count + 1]
+    me = lax.axis_index("head")
+    line = lax.axis_index("ctx")
+    barrier = pltpu.get_barrier_semaphore()
+    for peer in range(parts):
+
+        @pl.when(me != peer)
+        def _():
+            pl.semaphore_signal(barrier, inc=1, device_id=(line, peer), device_id_type=MESH_IDS)
+
+    pl.semaphore_wait(barrier, parts - 1)
+    outgoing, incoming, local = [], [], []
+    for index in range(count):
+        for peer in range(parts):
+            away = peer != me
+            sending = pltpu.make_async_remote_copy(
+                src_ref=source_view(sources[index], peer),
+                dst_ref=target_view(targets[index], me),
+                send_sem=send_sems.at[index, peer],
+                recv_sem=recv_sems.at[index, me],
+                device_id=(line, peer),
+                device_id_type=MESH_IDS,
+            )
+            pl.when(away)(sending.start)
+            staying = pltpu.make_async_copy(
+                source_view(sources[index], peer),
+                target_view(targets[index], peer),
+                send_sems.at[index, peer],
+            )
+            pl.when(jnp.logical_not(away))(staying.start)
+            arriving = pltpu.make_async_remote_copy(
+                src_ref=source_view(sources[index], peer),
+                dst_ref=target_view(targets[index], peer),
+                send_sem=send_sems.at[index, peer],
+                recv_sem=recv_sems.at[index, peer],
+                device_id=(line, peer),
+                device_id_type=MESH_IDS,
+            )
+            outgoing.append((away, sending))
+            incoming.append((away, arriving))
+            local.append((away, staying))
+    for (away, sending), (_, arriving), (_, staying) in zip(outgoing, incoming, local):
+        pl.when(away)(sending.wait_send)
+        pl.when(away)(arriving.wait_recv)
+        pl.when(jnp.logical_not(away))(staying.wait)
+
+
+def head_exchange(arrays, target_shapes, source_view, target_view, collective):
+    parts = lax.axis_size("head")
+    count = len(arrays)
+    return pl.pallas_call(
+        functools.partial(head_exchange_kernel, parts, count, source_view, target_view),
+        out_shape=[jax.ShapeDtypeStruct(shape, array.dtype) for shape, array in zip(target_shapes, arrays)],
+        in_specs=[pl.BlockSpec(memory_space=pl.ANY)] * count,
+        out_specs=[pl.BlockSpec(memory_space=pl.ANY)] * count,
+        scratch_shapes=[
+            pltpu.SemaphoreType.DMA((count, parts)),
+            pltpu.SemaphoreType.DMA((count, parts)),
+        ],
+        compiler_params=pltpu.CompilerParams(collective_id=collective, has_side_effects=True),
+    )(*arrays)
+
+
+def columns_of(ref, peer):
+    if len(ref.shape) == 3:
+        return ref.at[peer]
+    width = ref.shape[1] // lax.axis_size("head")
+    return ref.at[:, pl.ds(peer * width, width)]
+
+
+def rows_of(ref, peer):
+    if len(ref.shape) == 3:
+        return ref.at[peer]
+    height = ref.shape[0] // lax.axis_size("head")
+    return ref.at[pl.ds(peer * height, height), :]
+
+
+def spread_heads(arrays):
+    parts = lax.axis_size("head")
+    shapes = [
+        array.shape if array.ndim == 3 else (parts * array.shape[0], array.shape[1] // parts)
+        for array in arrays
+    ]
+    return head_exchange(arrays, shapes, columns_of, rows_of, 1)
+
+
+def gather_heads(array):
+    parts = lax.axis_size("head")
+    shape = (array.shape[0] // parts, array.shape[1] * parts)
+    return head_exchange([array], [shape], rows_of, columns_of, 2)[0]
+
+
 def on_device(
     query_rows,
     key_rows,
@@ -142,14 +367,21 @@
     conv_value,
     norm_gain,
 ):
-    device_query, local_key, local_value, local_gate, local_decay, local_strength = (
-        lax.all_to_all(query_rows, "head", split_axis=1, concat_axis=0, tiled=True),
-        lax.all_to_all(key_rows, "head", split_axis=1, concat_axis=0, tiled=True),
-        lax.all_to_all(value_rows, "head", split_axis=1, concat_axis=0, tiled=True),
-        lax.all_to_all(gate_rows, "head", split_axis=1, concat_axis=0, tiled=True),
-        lax.all_to_all(log_decay, "head", split_axis=1, concat_axis=0, tiled=True),
-        lax.all_to_all(write_strength, "head", split_axis=1, concat_axis=0, tiled=True),
-    )
+    parts = lax.axis_size("head")
+    scalars = jnp.concatenate(
+        [
+            log_decay.reshape(log_decay.shape[0], parts, -1),
+            write_strength.reshape(write_strength.shape[0], parts, -1),
+        ],
+        axis=2,
+    ).transpose(1, 0, 2)
+    device_query, local_key, local_value, moved_scalars = spread_heads(
+        [query_rows, key_rows, value_rows, scalars]
+    )
+    moved_scalars = moved_scalars.reshape(-1, moved_scalars.shape[-1])
+    split_at = log_decay.shape[1] // parts
+    local_decay, local_strength = moved_scalars[:, :split_at], moved_scalars[:, split_at:]
+    local_gate = lax.all_to_all(gate_rows, "head", split_axis=1, concat_axis=0, tiled=True)
     joined = jnp.concatenate([device_query, local_key, local_value], axis=1)
     kernel_width = conv_query.shape[0]
     count_rows = joined.shape[0]
@@ -192,32 +424,21 @@
             matmul("nhij,nhjk->nhik", trans, earlier_bias) + bias,
         )
         span *= 2
-    total_trans, total_bias = trans[-1], bias[-1]
-    place = lax.axis_index("ctx")
-    count = lax.axis_size("ctx")
-    span = 1
-    while span < count:
-        if 2 * span < count:
-            arrived = passed_along(jnp.stack([total_trans, total_bias]), "ctx", span)
-            total_trans, total_bias = (
-                jnp.where(place >= span, compose_maps(total_trans, arrived[0]), total_trans),
-                compose_maps(total_trans, arrived[1]) + total_bias,
-            )
-        else:
-            total_bias = compose_maps(total_trans, passed_along(total_bias, "ctx", span)) + total_bias
-        span *= 2
-    initial = passed_along(total_bias, "ctx", 1)
     earlier_trans = jnp.concatenate([identity_mat[None], trans[:-1]], axis=0)
     earlier_bias = jnp.concatenate([jnp.zeros_like(bias[:1]), bias[:-1]], axis=0)
-    starts = matmul("nhij,hjk->nhik", earlier_trans, initial) + earlier_bias
-    corrected = value_part - matmul("nhcd,nhde->nhce", key_part, starts)
-    produced = matmul("nhcd,nhde->nhce", query_decay, starts) + matmul(
+    corrected = value_part - matmul("nhcd,nhde->nhce", key_part, earlier_bias)
+    local_result = matmul("nhcd,nhde->nhce", query_decay, earlier_bias) + matmul(
         "nhij,nhje->nhie", within, corrected
     )
+    reach = query_decay - matmul("nhij,nhjd->nhid", within, key_part)
+    carry_map = matmul("nhcd,nhde->nhce", reach, earlier_trans)
+    total_trans, total_bias = trans[-1], bias[-1]
+    initial = ctx_scan(jnp.stack([total_trans, total_bias]))
+    produced = local_result + matmul("nhcd,hde->nhce", carry_map, initial)
     outputs = produced.transpose(0, 2, 1, 3).reshape(count_rows, heads_here, DV)
     gate = local_gate.astype(jnp.float32).reshape(count_rows, heads_here, DV)
     normed = gated_norm(outputs, gate, norm_gain)
-    return lax.all_to_all(normed, "head", split_axis=0, concat_axis=1, tiled=True)
+    return gather_heads(normed)
 
 
 def solution(mesh):

time: 278 us -> 227 us (0.82)
  the two profiles are of different devices: /device:TPU:21 before, /device:TPU:133 now
where the time goes in v4:
time: 227 us; the launch traced here: 223 us
  Pallas kernels  118 us (52%)
  matrix products  59.5 us (26%)
  local copies, waits for them, and re-layouts  18 us (8%)
  other arithmetic  15.7 us (7%)
  starting transfers between devices  10.9 us (5%)
    pallas_call x1, Pallas kernels, ctx_scan(): pl.pallas_call(functools.partial(ctx_scan_kernel, count), out_shape=jax.S...  61.7 us
    pallas_call x2, Pallas kernels, head_exchange(): pl.pallas_call(functools.partial(head_exchange_kernel, parts, count, sour...  56.5 us
    dot_general x29, matrix products, matmul(): return jnp.einsum(spec, left, right, precision=HIGHEST_PRECISION)  54.9 us
    unnamed x39, local copies, waits for them, and re-layouts  7.4 us
    all_to_all x1, starting transfers between devices, on_device(): lax.all_to_all(gate_rows, 'head', split_axis=1, concat_axis=0, tiled=True)  6.04 us
    mul x1, other arithmetic, causal_conv(): return jax.nn.silu(result)  5 us
    ppermute x1, starting transfers between devices, passed_along(): lax.ppermute(value, axis, [(source, source + steps) for source in range(l...  4.87 us
  transfers between devices with their start and end apart: 2, of which 0 were waited for; matrix products, arithmetic and copies ran while one was open for 35% of the time, Pallas kernels for 28%

profile of v4, /device:TPU:133, one launch (start us, length us, event | category | flops | bytes accessed | tf_op | source)
XLA Modules:
  0.0 223.3 jit_solution(10948856836708629783)
XLA Ops:
  0.0 0.9 copy.101
  0.9 0.9 copy.102
  1.8 0.9 maximum_bitcast_fusion.refs_3_
  2.7 37.4 %shard_map.100 = (bf16[1024,128]{1,0:T(8,128)(2,1)}, bf16[1024,128]{1,0:T(8,128)(2,1)}, bf16[1024,256]{1,0:T(8,128)(2,1)}, bf16[8,128,4]{2,1,0:T(8,128)(2,1)}) custom-call(bf16[128,1024]{1,0:T(8,128)(2,1)} %refs_0_.1, bf16[128,1024]{1,0:T(8,128)(2,1)} %refs_1_.1, bf16[128,2048]{1,0:T(8,128)(2,1)} %refs_2_.1, bf16[8,128,4]{2,1,0:T(8,128)(2,1)} %maximum_bitcast_fusion.refs_3_), custom_call_target="tpu_custom_call" | custom-call | tf_op jit(solution)/shard_map/pallas_call | solution.py:316
  40.1 1.0 constant_dynamic-update-slice_fusion.2
  41.2 1.0 constant_dynamic-update-slice_fusion.1
  42.2 1.1 constant_dynamic-update-slice_fusion
  43.3 4.9 %collective-permute-start = (bf16[3,512]{1,0:T(4,128)(2,1)S(1)}, bf16[3,512]{1,0:T(4,128)(2,1)S(1)}, u32[]{:S(2)}, u32[]{:S(2)}) collective-permute-start(bf16[3,512]{1,0:T(4,128)(2,1)S(1)} %slice.114), channel_id=1, source_target_pairs={{0,8},{8,16},{16,24},{24,32},{32,40},{40,48},{48,56},{56,64},{64,7... | collective-permute-start | bytes 9224 | tf_op jit(solution)/shard_map/ppermute | solution.py:24
  48.2 0.9 copy.144
  49.1 6.0 %all-to-all-start = ((bf16[128,8,256]{2,0,1:T(8,128)(2,1)}), bf16[128,8,256]{2,0,1:T(8,128)(2,1)}, u32[]{:S(2)}, u32[]{:S(2)}) async-start(bf16[128,8,256]{2,0,1:T(8,128)(2,1)} %bitcast.92), calls=%async_computation | async-start | bytes 1048576 | tf_op jit(solution)/shard_map/all_to_all | solution.py:384
  55.7 0.5 reduce_window_sum.11
  57.2 1.6 convert_element_type.46
  59.2 5.0 %divide_multiply_fusion = f32[1024,512]{1,0:T(8,128)S(1)} fusion(f32[1024,512]{1,0:T(8,128)} %convert_element_type.46, f32[3,512]{1,0:T(4,128)S(1)} %convert_element_type.48, f32[512]{0:T(512)S(1)} %bitcast.111, f32[512]{0:T(512)S(1)} %bitcast.112, f32[512]{0:T(512)S(1)} %bitcast.113, f32[512]{0:T(512)S(1)} %bitcast.110), kind=kLoop, calls=%fused_computation.42 | loop fusion | flops 7340032 | bytes 4208640 | tf_op jit(solution)/shard_map/jit(silu)/mul | solution.py:65
  64.2 0.3 multiply_reduce_fusion.2
  64.6 1.1 divide_multiply_fusion.1
  65.7 1.8 fusion.74
  67.6 1.1 fusion.92
  68.6 1.0 fusion.109
  69.7 1.2 fusion.90
  70.9 1.3 fusion.98
  72.2 0.2 subtract_subtract_fusion
  72.4 1.2 fusion.88
  73.6 1.2 fusion.157
  75.0 1.2 fusion.86
  76.2 1.4 fusion.158
  77.8 1.2 fusion.84
  79.0 1.2 fusion.159
  80.4 1.2 fusion.82
  81.6 2.1 fusion.160
  83.7 1.3 broadcast_multiply_fusion
  85.0 0.5 reshape_reshape.2
  85.6 0.3 bitcast_multiply_fusion.1
  85.9 0.9 copy-done.10
  86.8 0.3 copy-done.11
  87.1 1.9 fusion.10
  89.1 4.2 %fusion.52 = f32[16,2,128,128]{3,2,1,0:T(8,128)S(1)} fusion(f32[16,2,64,256]{3,2,1,0:T(8,128)S(1)} %fusion.10, f32[16,64,128]{2,1,0:T(8,128)S(1)} %bitcast.95, f32[16,2,64]{2,1,0:T(2,128)S(1)} %copy.106), kind=kOutput, calls=%fused_computation.51 | convolution fusion | flops 402915328 | bytes 3686400 | tf_op jit(solution)/shard_map/nhcd,nhce->nhde/dot_general | solution.py:28
  93.5 4.0 %multiply_subtract_fusion = f32[16,2,128,128]{3,2,1,0:T(8,128)S(1)} fusion(f32[128,128]{1,0:T(8,128)S(1)} %fusion.128, f32[16,2]{1,0:T(8,128)S(1)} %copy.105, f32[16,2,64,256]{3,2,1,0:T(8,128)S(1)} %fusion.10, f32[16,64,128]{2,1,0:T(8,128)S(1)} %bitcast.96, f32[16,2,64]{2,1,0:T(2,128)S(1)} %copy.106), kind=kOutput, calls=%fused_computation.41 | convolution fusion | flops 403963904 | bytes 3760128 | tf_op jit(solution)/shard_map/nhcd,nhce->nhde/dot_general | solution.py:28
  97.7 2.3 %fusion.40 = f32[16,2,128,128]{3,2,1,0:T(8,128)S(1)} fusion(f32[16,2,128,128]{3,2,1,0:T(8,128)S(1)} %fusion.52, f32[16,2,128,128]{3,2,1,0:T(8,128)S(1)} %multiply_subtract_fusion, f32[15,2,128,128]{3,2,1,0:T(8,128)S(1)} %slice.132), kind=kOutput, calls=%fused_computation.47 | convolution fusion | flops 805830656 | bytes 8257536 | tf_op jit(solution)/shard_map/nhij,nhjk->nhik/dot_general | solution.py:28
  100.2 2.3 %fusion = f32[16,2,128,128]{3,2,1,0:T(8,128)S(1)} fusion(f32[16,2,128,128]{3,2,1,0:T(8,128)S(1)} %multiply_subtract_fusion, f32[1,2,128,128]{3,2,1,0:T(8,128)S(1)} %broadcast_in_dim_broadcast_in_dim.15, f32[15,2,128,128]{3,2,1,0:T(8,128)S(1)} %slice.128), kind=kOutput, calls=%fused_computation.4 | convolution fusion | flops 805830656 | bytes 6291456 | tf_op jit(solution)/shard_map/nhij,nhjk->nhik/dot_general | solution.py:28
  102.6 2.3 %fusion.43 = f32[16,2,128,128]{3,2,1,0:T(8,128)S(1)} fusion(f32[16,2,128,128]{3,2,1,0:T(8,128)S(1)} %fusion.40, f32[16,2,128,128]{3,2,1,0:T(8,128)S(1)} %fusion, f32[14,2,128,128]{3,2,1,0:T(8,128)S(1)} %slice.133), kind=kOutput, calls=%fused_computation.48 | convolution fusion | flops 805830656 | bytes 8126464 | tf_op jit(solution)/shard_map/nhij,nhjk->nhik/dot_general | solution.py:28
  105.1 2.4 %fusion.15 = f32[16,2,128,128]{3,2,1,0:T(8,128)S(1)} fusion(f32[16,2,128,128]{3,2,1,0:T(8,128)S(1)} %fusion, f32[14,2,128,128]{3,2,1,0:T(8,128)S(1)} %slice.129, f32[2,2,128,128]{3,2,1,0:T(8,128)S(1)} %broadcast_in_dim_broadcast_in_dim.16), kind=kOutput, calls=%fused_computation.20 | convolution fusion | flops 805830656 | bytes 6291456 | tf_op jit(solution)/shard_map/nhij,nhjk->nhik/dot_general | solution.py:28
  107.7 2.2 fusion.46
  110.1 2.2 %fusion.19 = f32[16,2,128,128]{3,2,1,0:T(8,128)S(1)} fusion(f32[16,2,128,128]{3,2,1,0:T(8,128)S(1)} %fusion.15, f32[12,2,128,128]{3,2,1,0:T(8,128)S(1)} %slice.130, f32[4,2,128,128]{3,2,1,0:T(8,128)S(1)} %broadcast_in_dim_broadcast_in_dim.17), kind=kOutput, calls=%fused_computation.24 | convolution fusion | flops 805830656 | bytes 6291456 | tf_op jit(solution)/shard_map/nhij,nhjk->nhik/dot_general | solution.py:28
  112.3 2.1 fusion.49
  114.5 1.7 slice.136
  116.2 0.3 copy-done.5
  116.6 2.3 %fusion.23 = f32[16,2,128,128]{3,2,1,0:T(8,128)S(1)} fusion(f32[16,2,128,128]{3,2,1,0:T(8,128)S(1)} %fusion.19, f32[8,2,128,128]{3,2,1,0:T(8,128)S(1)} %slice.137, f32[8,2,128,128]{3,2,1,0:T(8,128)S(1)} %broadcast_in_dim_broadcast_in_dim.18), kind=kOutput, calls=%fused_computation.28 | convolution fusion | flops 805830656 | bytes 6291456 | tf_op jit(solution)/shard_map/nhij,nhjk->nhik/dot_general | solution.py:28
  118.9 1.3 copy-done.4
  120.3 2.7 %convolution_multiply_fusion = f32[16,2,64,64]{3,2,1,0:T(8,128)} fusion(f32[16,2,64]{2,1,0:T(2,128)S(1)} %copy.109, f32[16,64,128]{2,1,0:T(8,128)S(1)} %bitcast.97, f32[16,64,128]{2,1,0:T(8,128)S(1)} %bitcast.100, pred[64,64]{1,0:T(8,128)(4,1)S(1)} %get-tuple-element.30), kind=kOutput, calls=%fused_computation.61 | convolution fusion | flops 201850880 | bytes 1585152 | tf_op jit(solution)/shard_map/nhid,nhjd->nhij/dot_general | solution.py:105
  123.1 0.7 pad_maximum_fusion.5.maps_ref
  123.8 61.7 %shard_map.101 = f32[2,128,128]{2,1,0:T(8,128)} custom-call(f32[2,2,128,128]{3,2,1,0:T(8,128)} %pad_maximum_fusion.5.maps_ref), custom_call_target="tpu_custom_call" | custom-call | tf_op jit(solution)/shard_map/pallas_call | solution.py:247
  185.5 2.6 %multiply_subtract_fusion.1 = f32[16,2,64,128]{3,2,1,0:T(8,128)S(1)} fusion(f32[16,2,64,64]{3,2,1,0:T(8,128)} %convolution_multiply_fusion, f32[16,2,64,256]{3,2,1,0:T(8,128)S(1)} %fusion.10, f32[16,64,128]{2,1,0:T(8,128)S(1)} %bitcast.101, f32[16,2,64]{2,1,0:T(2,128)S(1)} %copy.104), kind=kOutput, calls=%fused_computation.54 | convolution fusion | flops 201850880 | bytes 3162112 | tf_op jit(solution)/shard_map/nhij,nhjd->nhid/dot_general | solution.py:28
  188.2 2.1 fusion.1
  190.3 1.0 convolution_bitcast_fusion
  191.4 0.5 copy-done.2
  191.8 2.0 fusion.71
  193.9 1.2 fusion.161
  195.1 2.2 %multiply_reduce_fusion = (f32[16,64,2]{1,2,0:T(2,128)S(1)}, f32[16,64,2,128]{3,1,2,0:T(8,128)S(1)}) fusion(f32[16,64,2,128]{3,1,2,0:T(8,128)S(1)} %convolution_bitcast_fusion, f32[16,2,64,128]{3,2,1,0:T(8,128)S(1)} %fusion.161, f32[15,2,128,128]{3,2,1,0:T(8,128)S(1)} %copy-done.2, f32[16,64,128]{2,1,0:T(8,128)S(1)} %bitcast.102, f32[16,2,64]{2,1,0:T(2,128)S(1)} %copy.104), kind=kOutput, calls=%fused_computation.74 | convolution fusion | flops 403961856 | bytes 5652480 | tf_op jit(solution)/shard_map/nhcd,nhde->nhce/dot_general | solution.py:28
  197.4 0.2 copy.124
  197.6 0.8 copy.117
  198.5 1.2 div.140
  199.7 2.4 %fusion.77.refs_0_ = bf16[1024,256]{1,0:T(8,128)(2,1)} fusion(f32[128,8,2,128]{3,2,1,0:T(2,128)S(1)} %bitcast.104, f32[128,8,2,128]{3,2,1,0:T(2,128)S(1)} %bitcast.103, bf16[128,8,256]{2,0,1:T(8,128)(2,1)} %all-to-all-done, f32[256]{0:T(256)S(1)} %broadcast_bitcast_fusion), kind=kLoop, calls=%fused_computation.67 | loop fusion | flops 2359296 | bytes 3146752 | tf_op jit(solution)/shard_map/convert_element_type | solution.py:130
  202.1 19.1 %shard_map.102 = bf16[128,2048]{1,0:T(8,128)(2,1)} custom-call(bf16[1024,256]{1,0:T(8,128)(2,1)} %fusion.77.refs_0_), custom_call_target="tpu_custom_call" | custom-call | tf_op jit(solution)/shard_map/pallas_call | solution.py:316
  221.2 1.9 copy.148
  (96 shorter events, 3.8 us)
Async XLA Ops:
  0.0 56.5 %copy-start = (f32[128]{0:T(128)S(1)}, f32[128]{0:T(128)}, u32[]{:S(2)}) copy-start(f32[128]{0:T(128)} %param.19) | copy-start | bytes 1540
  1.8 46.4 %copy-start.14 = (bf16[128,2048]{1,0:T(8,128)(2,1)S(1)}, bf16[128,2048]{1,0:T(8,128)(2,1)}, u32[]{:S(2)}) copy-start(bf16[128,2048]{1,0:T(8,128)(2,1)} %param.13) | copy-start | bytes 1572868
  40.1 15.2 %copy-start.15 = (bf16[4,256]{1,0:T(4,128)(2,1)S(1)}, bf16[4,256]{1,0:T(4,128)(2,1)}, u32[]{:S(2)}) copy-start(bf16[4,256]{1,0:T(4,128)(2,1)} %param.18) | copy-start | bytes 6148
  40.1 15.2 %copy-start.16 = (bf16[4,128]{1,0:T(4,128)(2,1)S(1)}, bf16[4,128]{1,0:T(4,128)(2,1)}, u32[]{:S(2)}) copy-start(bf16[4,128]{1,0:T(4,128)(2,1)} %param.17) | copy-start | bytes 3076
  40.1 15.2 %copy-start.17 = (bf16[4,128]{1,0:T(4,128)(2,1)S(1)}, bf16[4,128]{1,0:T(4,128)(2,1)}, u32[]{:S(2)}) copy-start(bf16[4,128]{1,0:T(4,128)(2,1)} %param.16) | copy-start | bytes 3076
  40.1 15.2 %copy-start.12 = (bf16[8,128,4]{2,1,0:T(8,128)(2,1)S(1)}, bf16[8,128,4]{2,1,0:T(8,128)(2,1)}, u32[]{:S(2)}) copy-start(bf16[8,128,4]{2,1,0:T(8,128)(2,1)} %get-tuple-element.9) | copy-start | bytes 24580
  43.3 15.9 %collective-permute-start = (bf16[3,512]{1,0:T(4,128)(2,1)S(1)}, bf16[3,512]{1,0:T(4,128)(2,1)S(1)}, u32[]{:S(2)}, u32[]{:S(2)}) collective-permute-start(bf16[3,512]{1,0:T(4,128)(2,1)S(1)} %slice.114), channel_id=1, source_target_pairs={{0,8},{8,16},{16,24},{24,32},{32,40},{40,48},{48,56},{56,64},{64,7... | collective-permute-start | bytes 9224 | tf_op jit(solution)/shard_map/ppermute | solution.py:24
  49.1 149.4 %all-to-all-start = ((bf16[128,8,256]{2,0,1:T(8,128)(2,1)}), bf16[128,8,256]{2,0,1:T(8,128)(2,1)}, u32[]{:S(2)}, u32[]{:S(2)}) async-start(bf16[128,8,256]{2,0,1:T(8,128)(2,1)} %bitcast.92), calls=%async_computation | async-start | bytes 1048576 | tf_op jit(solution)/shard_map/all_to_all | solution.py:384
  64.2 1.5 copy-start.3
  65.7 18.0 %copy-start.6 = (f32[1024,128]{1,0:T(8,128)}, f32[1024,128]{1,0:T(8,128)S(1)}, u32[]{:S(2)}) copy-start(f32[1024,128]{1,0:T(8,128)S(1)} %get-tuple-element.16) | copy-start | bytes 1572868
  81.6 3.5 %slice-start = ((f32[1024,512]{1,0:T(8,128)}), f32[1024,256]{1,0:T(8,128)S(1)}, s32[]{:S(2)}) async-start(f32[1024,512]{1,0:T(8,128)} %copy-done.3), calls=%async_computation.1 | async-start | bytes 2097152 | tf_op jit(solution)/shard_map/slice | solution.py:400
  85.6 1.2 copy-start.10
  85.6 1.5 copy-start.11
  87.1 1.9 copy-start.7
  114.5 2.0 copy-start.5
  118.9 1.3 copy-start.4
  118.9 1.4 copy-start.8
  120.3 2.8 %slice-start.3 = ((f32[16,2,128,128]{3,2,1,0:T(8,128)}), f32[1,2,128,128]{3,2,1,0:T(8,128)S(1)}, s32[]{:S(2)}) async-start(f32[16,2,128,128]{3,2,1,0:T(8,128)} %copy-done.5), calls=%async_computation.4 | async-start | bytes 262144 | tf_op jit(solution)/shard_map/slice | solution.py:435
  120.3 2.8 %slice-start.1 = ((f32[16,2,128,128]{3,2,1,0:T(8,128)}), f32[1,2,128,128]{3,2,1,0:T(8,128)S(1)}, s32[]{:S(2)}) async-start(f32[16,2,128,128]{3,2,1,0:T(8,128)} %copy-done.4), calls=%async_computation.2 | async-start | bytes 262144 | tf_op jit(solution)/shard_map/slice | solution.py:435
  185.5 2.6 %slice-start.2 = ((f32[16,2,128,128]{3,2,1,0:T(8,128)}), f32[15,2,128,128]{3,2,1,0:T(8,128)S(1)}, s32[]{:S(2)}) async-start(f32[16,2,128,128]{3,2,1,0:T(8,128)} %copy-done.4), calls=%async_computation.3 | async-start | bytes 3932160 | tf_op jit(solution)/shard_map/slice | solution.py:427
  188.2 2.1 copy-start.13
  190.3 1.5 copy-start.2
  191.8 2.0 copy-start.9
  199.7 23.4 %copy-start.1 = (f32[128]{0:T(128)S(1)}, f32[128]{0:T(128)}, u32[]{:S(2)}) copy-start(f32[128]{0:T(128)} %param.19) | copy-start | bytes 1540

commit v5 on v4

--- a/solution.py
+++ b/solution.py
@@ -16,6 +16,7 @@
 
 HIGHEST_PRECISION = lax.Precision.HIGHEST
 EPSILON = 1e-06
+MATMUL_PRECISION = lax.Precision.HIGH
 
 
 def passed_along(value, axis, steps):
@@ -25,7 +26,7 @@
 
 
 def matmul(spec, left, right):
-    return jnp.einsum(spec, left, right, precision=HIGHEST_PRECISION)
+    return jnp.einsum(spec, left, right, precision=MATMUL_PRECISION)
 
 
 def unit_lower_inverse(strict):
@@ -94,7 +95,7 @@
     strictly = rows_index > cols_index
     spread = jnp.where(causal, cumulative[..., :, None] - cumulative[..., None, :], 0.0)
     decays = jnp.where(causal, jnp.exp(spread), 0.0)
-    key_key = jnp.einsum("nhid,nhjd->nhij", keys, keys, precision=HIGHEST_PRECISION)
+    key_key = jnp.einsum("nhid,nhjd->nhij", keys, keys, precision=MATMUL_PRECISION)
     coupling = jnp.where(strictly, strength[..., None] * decays * key_key, 0.0)
     targets = jnp.concatenate(
         [(strength * jnp.exp(cumulative))[..., None] * keys, strength[..., None] * values], axis=-1
@@ -102,7 +103,7 @@
     solved = forward_substitution(coupling, targets)
     key_part = solved[..., :key_dim]
     value_part = solved[..., key_dim:]
-    query_key = jnp.einsum("nhid,nhjd->nhij", queries, keys, precision=HIGHEST_PRECISION)
+    query_key = jnp.einsum("nhid,nhjd->nhij", queries, keys, precision=MATMUL_PRECISION)
     within = query_key * decays
     query_decay = jnp.exp(cumulative)[..., None] * queries
     closing_logarithm = cumulative[..., -1:]

time: 227 us -> 202 us (0.89)
  matrix products: 59.5 us -> 33.9 us
    dot_general x31, matrix products: 59.5 us -> 33.9 us  [the longest x29 30.9 us: matmul(): return jnp.einsum(spec, left, right, precision=MATMUL_PRECISION)]
  transfers between devices with their start and end apart: 2 -> 2, of which waited for: 0 -> 0; matrix products, arithmetic and copies ran while one was open for 35% -> 27% of each run, Pallas kernels for 28% -> 31%
where the time goes in v5:
time: 202 us; the launch traced here: 198 us
  Pallas kernels  118 us (58%)
  matrix products  33.9 us (17%)
  local copies, waits for them, and re-layouts  18.6 us (9%)
  other arithmetic  15.7 us (8%)
  starting transfers between devices  10.9 us (5%)
    pallas_call x1, Pallas kernels, ctx_scan(): pl.pallas_call(functools.partial(ctx_scan_kernel, count), out_shape=jax.S...  61.5 us
    pallas_call x2, Pallas kernels, head_exchange(): pl.pallas_call(functools.partial(head_exchange_kernel, parts, count, sour...  56.5 us
    dot_general x29, matrix products, matmul(): return jnp.einsum(spec, left, right, precision=MATMUL_PRECISION)  30.9 us
    unnamed x39, local copies, waits for them, and re-layouts  8.05 us
    all_to_all x1, starting transfers between devices, on_device(): lax.all_to_all(gate_rows, 'head', split_axis=1, concat_axis=0, tiled=True)  6.04 us
    mul x1, other arithmetic, causal_conv(): return jax.nn.silu(result)  5 us
    ppermute x1, starting transfers between devices, passed_along(): lax.ppermute(value, axis, [(source, source + steps) for source in range(l...  4.87 us
  transfers between devices with their start and end apart: 2, of which 0 were waited for; matrix products, arithmetic and copies ran while one was open for 27% of the time, Pallas kernels for 31%

profile of v5, /device:TPU:133, one launch (start us, length us, event | category | flops | bytes accessed | tf_op | source)
XLA Modules:
  0.0 198.2 jit_solution(387775728361429602)
XLA Ops:
  0.0 0.9 copy.101
  0.9 0.9 copy.102
  1.8 0.9 maximum_bitcast_fusion.refs_3_
  2.7 37.4 %shard_map.100 = (bf16[1024,128]{1,0:T(8,128)(2,1)}, bf16[1024,128]{1,0:T(8,128)(2,1)}, bf16[1024,256]{1,0:T(8,128)(2,1)}, bf16[8,128,4]{2,1,0:T(8,128)(2,1)}) custom-call(bf16[128,1024]{1,0:T(8,128)(2,1)} %refs_0_.1, bf16[128,1024]{1,0:T(8,128)(2,1)} %refs_1_.1, bf16[128,2048]{1,0:T(8,128)(2,1)} %refs_2_.1, bf16[8,128,4]{2,1,0:T(8,128)(2,1)} %maximum_bitcast_fusion.refs_3_), custom_call_target="tpu_custom_call" | custom-call | tf_op jit(solution)/shard_map/pallas_call | solution.py:317
  40.1 1.0 constant_dynamic-update-slice_fusion.2
  41.2 1.0 constant_dynamic-update-slice_fusion.1
  42.2 1.1 constant_dynamic-update-slice_fusion
  43.3 4.9 %collective-permute-start = (bf16[3,512]{1,0:T(4,128)(2,1)S(1)}, bf16[3,512]{1,0:T(4,128)(2,1)S(1)}, u32[]{:S(2)}, u32[]{:S(2)}) collective-permute-start(bf16[3,512]{1,0:T(4,128)(2,1)S(1)} %slice.114), channel_id=1, source_target_pairs={{0,8},{8,16},{16,24},{24,32},{32,40},{40,48},{48,56},{56,64},{64,7... | collective-permute-start | bytes 9224 | tf_op jit(solution)/shard_map/ppermute | solution.py:25
  48.2 0.9 copy.144
  49.1 6.0 %all-to-all-start = ((bf16[128,8,256]{2,0,1:T(8,128)(2,1)}), bf16[128,8,256]{2,0,1:T(8,128)(2,1)}, u32[]{:S(2)}, u32[]{:S(2)}) async-start(bf16[128,8,256]{2,0,1:T(8,128)(2,1)} %bitcast.92), calls=%async_computation | async-start | bytes 1048576 | tf_op jit(solution)/shard_map/all_to_all | solution.py:385
  55.7 0.5 reduce_window_sum.11
  57.2 1.6 convert_element_type.46
  59.2 5.0 %divide_multiply_fusion = f32[1024,512]{1,0:T(8,128)S(1)} fusion(f32[1024,512]{1,0:T(8,128)} %convert_element_type.46, f32[3,512]{1,0:T(4,128)S(1)} %convert_element_type.48, f32[512]{0:T(512)S(1)} %bitcast.111, f32[512]{0:T(512)S(1)} %bitcast.112, f32[512]{0:T(512)S(1)} %bitcast.113, f32[512]{0:T(512)S(1)} %bitcast.110), kind=kLoop, calls=%fused_computation.42 | loop fusion | flops 7340032 | bytes 4208640 | tf_op jit(solution)/shard_map/jit(silu)/mul | solution.py:66
  64.2 0.3 multiply_reduce_fusion.2
  64.6 1.1 divide_multiply_fusion.1
  65.7 1.0 fusion.74
  66.8 0.6 fusion.92
  67.3 0.6 fusion.109
  67.9 0.6 fusion.90
  68.6 0.7 fusion.98
  69.3 0.2 subtract_subtract_fusion
  69.5 0.7 fusion.88
  70.2 0.6 fusion.157
  70.9 0.7 fusion.86
  71.6 0.7 fusion.158
  72.5 0.7 fusion.84
  73.1 0.6 fusion.159
  73.9 0.7 fusion.82
  74.6 1.6 fusion.160
  76.1 1.3 broadcast_multiply_fusion
  77.5 0.5 reshape_reshape.2
  78.0 0.3 bitcast_multiply_fusion.1
  78.4 0.9 copy-done.10
  79.2 0.3 copy-done.11
  79.5 1.1 fusion.10
  80.7 2.3 %fusion.52 = f32[16,2,128,128]{3,2,1,0:T(8,128)S(1)} fusion(f32[16,2,64,256]{3,2,1,0:T(8,128)S(1)} %fusion.10, f32[16,64,128]{2,1,0:T(8,128)S(1)} %bitcast.95, f32[16,2,64]{2,1,0:T(2,128)S(1)} %copy.106), kind=kOutput, calls=%fused_computation.51 | convolution fusion | flops 201588736 | bytes 3686400 | tf_op jit(solution)/shard_map/nhcd,nhce->nhde/dot_general | solution.py:29
  83.2 2.3 %multiply_subtract_fusion = f32[16,2,128,128]{3,2,1,0:T(8,128)S(1)} fusion(f32[128,128]{1,0:T(8,128)S(1)} %fusion.128, f32[16,2]{1,0:T(8,128)S(1)} %copy.105, f32[16,2,64,256]{3,2,1,0:T(8,128)S(1)} %fusion.10, f32[16,64,128]{2,1,0:T(8,128)S(1)} %bitcast.96, f32[16,2,64]{2,1,0:T(2,128)S(1)} %copy.106), kind=kOutput, calls=%fused_computation.41 | convolution fusion | flops 202637312 | bytes 3760128 | tf_op jit(solution)/shard_map/nhcd,nhce->nhde/dot_general | solution.py:29
  85.7 1.3 fusion.40
  87.2 1.2 fusion
  88.6 1.2 fusion.43
  90.0 1.2 fusion.15
  91.4 1.2 fusion.46
  92.8 1.2 fusion.19
  94.0 1.4 fusion.49
  95.4 1.7 slice.136
  97.1 0.3 copy-done.5
  97.6 1.2 fusion.23
  98.8 1.3 copy-done.4
  100.2 1.9 convolution_multiply_fusion
  102.2 0.7 pad_maximum_fusion.5.maps_ref
  102.9 61.5 %shard_map.101 = f32[2,128,128]{2,1,0:T(8,128)} custom-call(f32[2,2,128,128]{3,2,1,0:T(8,128)} %pad_maximum_fusion.5.maps_ref), custom_call_target="tpu_custom_call" | custom-call | tf_op jit(solution)/shard_map/pallas_call | solution.py:248
  164.4 2.0 %multiply_subtract_fusion.1 = f32[16,2,64,128]{3,2,1,0:T(8,128)S(1)} fusion(f32[16,2,64,64]{3,2,1,0:T(8,128)} %convolution_multiply_fusion, f32[16,2,64,256]{3,2,1,0:T(8,128)S(1)} %fusion.10, f32[16,64,128]{2,1,0:T(8,128)S(1)} %bitcast.101, f32[16,2,64]{2,1,0:T(2,128)S(1)} %copy.104), kind=kOutput, calls=%fused_computation.54 | convolution fusion | flops 101187584 | bytes 3162112 | tf_op jit(solution)/shard_map/nhij,nhjd->nhid/dot_general | solution.py:29
  166.4 1.1 fusion.1
  167.5 0.6 convolution_bitcast_fusion
  168.1 1.0 copy-done.2
  169.1 1.0 fusion.71
  170.3 0.7 fusion.161
  171.0 1.3 multiply_reduce_fusion
  172.3 0.2 copy.124
  172.5 0.8 copy.117
  173.4 1.2 div.140
  174.6 2.4 %fusion.77.refs_0_ = bf16[1024,256]{1,0:T(8,128)(2,1)} fusion(f32[128,8,2,128]{3,2,1,0:T(2,128)S(1)} %bitcast.104, f32[128,8,2,128]{3,2,1,0:T(2,128)S(1)} %bitcast.103, bf16[128,8,256]{2,0,1:T(8,128)(2,1)} %all-to-all-done, f32[256]{0:T(256)S(1)} %broadcast_bitcast_fusion), kind=kLoop, calls=%fused_computation.67 | loop fusion | flops 2359296 | bytes 3146752 | tf_op jit(solution)/shard_map/convert_element_type | solution.py:131
  177.0 19.1 %shard_map.102 = bf16[128,2048]{1,0:T(8,128)(2,1)} custom-call(bf16[1024,256]{1,0:T(8,128)(2,1)} %fusion.77.refs_0_), custom_call_target="tpu_custom_call" | custom-call | tf_op jit(solution)/shard_map/pallas_call | solution.py:317
  196.1 1.9 copy.148
  (96 shorter events, 4.0 us)
Async XLA Ops:
  0.0 56.5 %copy-start = (f32[128]{0:T(128)S(1)}, f32[128]{0:T(128)}, u32[]{:S(2)}) copy-start(f32[128]{0:T(128)} %param.19) | copy-start | bytes 1540
  1.8 46.4 %copy-start.14 = (bf16[128,2048]{1,0:T(8,128)(2,1)S(1)}, bf16[128,2048]{1,0:T(8,128)(2,1)}, u32[]{:S(2)}) copy-start(bf16[128,2048]{1,0:T(8,128)(2,1)} %param.13) | copy-start | bytes 1572868
  40.1 15.2 %copy-start.15 = (bf16[4,256]{1,0:T(4,128)(2,1)S(1)}, bf16[4,256]{1,0:T(4,128)(2,1)}, u32[]{:S(2)}) copy-start(bf16[4,256]{1,0:T(4,128)(2,1)} %param.18) | copy-start | bytes 6148
  40.1 15.2 %copy-start.16 = (bf16[4,128]{1,0:T(4,128)(2,1)S(1)}, bf16[4,128]{1,0:T(4,128)(2,1)}, u32[]{:S(2)}) copy-start(bf16[4,128]{1,0:T(4,128)(2,1)} %param.17) | copy-start | bytes 3076
  40.1 15.2 %copy-start.17 = (bf16[4,128]{1,0:T(4,128)(2,1)S(1)}, bf16[4,128]{1,0:T(4,128)(2,1)}, u32[]{:S(2)}) copy-start(bf16[4,128]{1,0:T(4,128)(2,1)} %param.16) | copy-start | bytes 3076
  40.1 15.2 %copy-start.12 = (bf16[8,128,4]{2,1,0:T(8,128)(2,1)S(1)}, bf16[8,128,4]{2,1,0:T(8,128)(2,1)}, u32[]{:S(2)}) copy-start(bf16[8,128,4]{2,1,0:T(8,128)(2,1)} %get-tuple-element.9) | copy-start | bytes 24580
  43.3 15.9 %collective-permute-start = (bf16[3,512]{1,0:T(4,128)(2,1)S(1)}, bf16[3,512]{1,0:T(4,128)(2,1)S(1)}, u32[]{:S(2)}, u32[]{:S(2)}) collective-permute-start(bf16[3,512]{1,0:T(4,128)(2,1)S(1)} %slice.114), channel_id=1, source_target_pairs={{0,8},{8,16},{16,24},{24,32},{32,40},{40,48},{48,56},{56,64},{64,7... | collective-permute-start | bytes 9224 | tf_op jit(solution)/shard_map/ppermute | solution.py:25
  49.1 124.3 %all-to-all-start = ((bf16[128,8,256]{2,0,1:T(8,128)(2,1)}), bf16[128,8,256]{2,0,1:T(8,128)(2,1)}, u32[]{:S(2)}, u32[]{:S(2)}) async-start(bf16[128,8,256]{2,0,1:T(8,128)(2,1)} %bitcast.92), calls=%async_computation | async-start | bytes 1048576 | tf_op jit(solution)/shard_map/all_to_all | solution.py:385
  64.2 1.5 copy-start.3
  65.7 10.4 %copy-start.6 = (f32[1024,128]{1,0:T(8,128)}, f32[1024,128]{1,0:T(8,128)S(1)}, u32[]{:S(2)}) copy-start(f32[1024,128]{1,0:T(8,128)S(1)} %get-tuple-element.16) | copy-start | bytes 1572868
  74.6 2.9 %slice-start = ((f32[1024,512]{1,0:T(8,128)}), f32[1024,256]{1,0:T(8,128)S(1)}, s32[]{:S(2)}) async-start(f32[1024,512]{1,0:T(8,128)} %copy-done.3), calls=%async_computation.1 | async-start | bytes 2097152 | tf_op jit(solution)/shard_map/slice | solution.py:401
  78.0 1.2 copy-start.10
  78.0 1.5 copy-start.11
  79.5 1.1 copy-start.7
  95.4 2.0 %copy-start.5 = (f32[16,2,128,128]{3,2,1,0:T(8,128)}, f32[16,2,128,128]{3,2,1,0:T(8,128)S(1)}, u32[]{:S(2)}) copy-start(f32[16,2,128,128]{3,2,1,0:T(8,128)S(1)} %fusion.49) | copy-start | bytes 6291460
  98.8 1.3 copy-start.4
  98.8 1.4 copy-start.8
  100.1 2.0 %slice-start.3 = ((f32[16,2,128,128]{3,2,1,0:T(8,128)}), f32[1,2,128,128]{3,2,1,0:T(8,128)S(1)}, s32[]{:S(2)}) async-start(f32[16,2,128,128]{3,2,1,0:T(8,128)} %copy-done.5), calls=%async_computation.4 | async-start | bytes 262144 | tf_op jit(solution)/shard_map/slice | solution.py:436
  100.1 2.0 %slice-start.1 = ((f32[16,2,128,128]{3,2,1,0:T(8,128)}), f32[1,2,128,128]{3,2,1,0:T(8,128)S(1)}, s32[]{:S(2)}) async-start(f32[16,2,128,128]{3,2,1,0:T(8,128)} %copy-done.4), calls=%async_computation.2 | async-start | bytes 262144 | tf_op jit(solution)/shard_map/slice | solution.py:436
  164.4 2.1 %slice-start.2 = ((f32[16,2,128,128]{3,2,1,0:T(8,128)}), f32[15,2,128,128]{3,2,1,0:T(8,128)S(1)}, s32[]{:S(2)}) async-start(f32[16,2,128,128]{3,2,1,0:T(8,128)} %copy-done.4), calls=%async_computation.3 | async-start | bytes 3932160 | tf_op jit(solution)/shard_map/slice | solution.py:428
  166.4 1.1 copy-start.13
  167.5 1.5 copy-start.2
  169.1 1.2 copy-start.9
  174.6 23.3 %copy-start.1 = (f32[128]{0:T(128)S(1)}, f32[128]{0:T(128)}, u32[]{:S(2)}) copy-start(f32[128]{0:T(128)} %param.19) | copy-start | bytes 1540

commit v6 on v5

--- a/solution.py
+++ b/solution.py
@@ -156,7 +156,9 @@
     group = lax.axis_index("head")
     heads = maps_ref.shape[1]
     spans, far = scan_spans(count)
-    offsets = sorted(set(spans + [1] + ([far] if far < count else [])))
+    rounds = len(spans)
+    has_far = far < count
+    offsets = sorted(set(spans + [1] + ([far] if has_far else [])))
     barrier = pltpu.get_barrier_semaphore()
     partners = jnp.int32(0)
     for offset in offsets:
@@ -170,73 +172,111 @@
             partners = partners + valid.astype(jnp.int32)
     pl.semaphore_wait(barrier, partners)
 
-    source = maps_ref
+    def result_of(index):
+        return maps_ref if index < 0 else current.at[index % 2]
+
+    def round_copy(index, kind, head):
+        return pltpu.make_async_remote_copy(
+            src_ref=result_of(index - 1).at[kind, head],
+            dst_ref=slots.at[index, kind, head],
+            send_sem=send_sems.at[index, kind * heads + head],
+            recv_sem=recv_sems.at[index, kind * heads + head],
+            device_id=(place + spans[index], group),
+            device_id_type=MESH_IDS,
+        )
+
+    def near_copy(kind, head):
+        return pltpu.make_async_remote_copy(
+            src_ref=result_of(rounds - 1).at[kind, head],
+            dst_ref=near_slot.at[kind, head],
+            send_sem=send_sems.at[rounds, kind * heads + head],
+            recv_sem=recv_sems.at[rounds, kind * heads + head],
+            device_id=(place + 1, group),
+            device_id_type=MESH_IDS,
+        )
+
+    def far_copy(head):
+        return pltpu.make_async_remote_copy(
+            src_ref=result_of(rounds - 1).at[1, head],
+            dst_ref=far_slot.at[head],
+            send_sem=send_sems.at[rounds + 1, head],
+            recv_sem=recv_sems.at[rounds + 1, head],
+            device_id=(place + far, group),
+            device_id_type=MESH_IDS,
+        )
+
+    def launch_after(index, kind, head):
+        following = index + 1
+        if following < rounds:
+            pl.when(place + spans[following] < count)(round_copy(following, kind, head).start)
+        else:
+            pl.when(place + 1 < count)(near_copy(kind, head).start)
+            if has_far and kind == 1:
+                pl.when(place + far < count)(far_copy(head).start)
+
+    for kind in range(2):
+        for head in range(heads):
+            launch_after(-1, kind, head)
+
     for index, span in enumerate(spans):
-        sending = place + span < count
+        source = result_of(index - 1)
+        dest = result_of(index)
         receiving = place >= span
-        copy_out = pltpu.make_async_remote_copy(
-            src_ref=source,
-            dst_ref=slots.at[index],
-            send_sem=send_sems.at[index],
-            recv_sem=recv_sems.at[index],
-            device_id=(place + span, group),
-            device_id_type=MESH_IDS,
-        )
-        pl.when(sending)(copy_out.start)
-        pl.when(receiving)(copy_out.wait_recv)
-        dest = current.at[index % 2]
-
-        def composed(source=source, dest=dest, index=index):
+
+        def composed(index=index, source=source, dest=dest):
             for head in range(heads):
-                trans_here = source[0, head]
-                dest[0, head] = kernel_dot(trans_here, slots[index, 0, head])
-                dest[1, head] = kernel_dot(trans_here, slots[index, 1, head]) + source[1, head]
-
-        def kept(source=source, dest=dest):
+                round_copy(index, 0, head).wait_recv()
+                dest[0, head] = kernel_dot(source[0, head], slots[index, 0, head])
+                launch_after(index, 0, head)
+                round_copy(index, 1, head).wait_recv()
+                dest[1, head] = kernel_dot(source[0, head], slots[index, 1, head]) + source[1, head]
+                launch_after(index, 1, head)
+
+        def kept(index=index, source=source, dest=dest):
             dest[...] = source[...]
+            for kind in range(2):
+                for head in range(heads):
+                    launch_after(index, kind, head)
 
         pl.when(receiving)(composed)
         pl.when(jnp.logical_not(receiving))(kept)
-        pl.when(sending)(copy_out.wait_send)
-        source = dest
-
-    last = len(spans)
-    near_copy = pltpu.make_async_remote_copy(
-        src_ref=source,
-        dst_ref=near_slot,
-        send_sem=send_sems.at[last],
-        recv_sem=recv_sems.at[last],
-        device_id=(place + 1, group),
-        device_id_type=MESH_IDS,
-    )
-    pl.when(place + 1 < count)(near_copy.start)
-    if far < count:
-        far_copy = pltpu.make_async_remote_copy(
-            src_ref=source.at[1],
-            dst_ref=far_slot,
-            send_sem=send_sems.at[last + 1],
-            recv_sem=recv_sems.at[last + 1],
-            device_id=(place + far, group),
-            device_id_type=MESH_IDS,
-        )
-        pl.when(place + far < count)(far_copy.start)
-    pl.when(place >= 1)(near_copy.wait_recv)
+
+        def sent(index=index):
+            for kind in range(2):
+                for head in range(heads):
+                    round_copy(index, kind, head).wait_send()
+
+        pl.when(place + span < count)(sent)
+
+    def near_arrived():
+        for kind in range(2):
+            for head in range(heads):
+                near_copy(kind, head).wait_recv()
+        out_ref[...] = near_slot[1]
+
     out_ref[...] = jnp.zeros_like(out_ref)
-
-    def from_near():
-        out_ref[...] = near_slot[1]
-
-    pl.when(place >= 1)(from_near)
-    if far < count:
-        pl.when(place >= far)(far_copy.wait_recv)
-
-        def from_far():
+    pl.when(place >= 1)(near_arrived)
+    if has_far:
+
+        def far_arrived():
             for head in range(heads):
+                far_copy(head).wait_recv()
                 out_ref[head] = out_ref[head] + kernel_dot(near_slot[0, head], far_slot[head])
 
-        pl.when(place >= far)(from_far)
-        pl.when(place + far < count)(far_copy.wait_send)
-    pl.when(place + 1 < count)(near_copy.wait_send)
+        pl.when(place >= far)(far_arrived)
+
+        def far_sent():
+            for head in range(heads):
+                far_copy(head).wait_send()
+
+        pl.when(place + far < count)(far_sent)
+
+    def near_sent():
+        for kind in range(2):
+            for head in range(heads):
+                near_copy(kind, head).wait_send()
+
+    pl.when(place + 1 < count)(near_sent)
 
 
 def ctx_scan(maps):
@@ -255,8 +295,8 @@
             pltpu.VMEM((max(len(spans), 1),) + maps.shape, jnp.float32),
             pltpu.VMEM(maps.shape, jnp.float32),
             pltpu.VMEM(side, jnp.float32),
-            pltpu.SemaphoreType.DMA((len(spans) + 2,)),
-            pltpu.SemaphoreType.DMA((len(spans) + 2,)),
+            pltpu.SemaphoreType.DMA((len(spans) + 2, 2 * maps.shape[1])),
+            pltpu.SemaphoreType.DMA((len(spans) + 2, 2 * maps.shape[1])),
         ],
         compiler_params=pltpu.CompilerParams(collective_id=0, has_side_effects=True),
     )(maps)

time: 202 us -> 195 us (0.965)
  the two profiles are of different devices: /device:TPU:133 before, /device:TPU:141 now
where the time goes in v6:
time: 195 us; the launch traced here: 191 us
  Pallas kernels  111 us (57%)
  matrix products  33.9 us (17%)
  local copies, waits for them, and re-layouts  18.6 us (10%)
  other arithmetic  15.7 us (8%)
  starting transfers between devices  10.9 us (6%)
    pallas_call x2, Pallas kernels, head_exchange(): pl.pallas_call(functools.partial(head_exchange_kernel, parts, count, sour...  57.2 us
    pallas_call x1, Pallas kernels, ctx_scan(): pl.pallas_call(functools.partial(ctx_scan_kernel, count), out_shape=jax.S...  53.7 us
    dot_general x29, matrix products, matmul(): return jnp.einsum(spec, left, right, precision=MATMUL_PRECISION)  30.9 us
    unnamed x39, local copies, waits for them, and re-layouts  8.04 us
    all_to_all x1, starting transfers between devices, on_device(): lax.all_to_all(gate_rows, 'head', split_axis=1, concat_axis=0, tiled=True)  6.04 us
    mul x1, other arithmetic, causal_conv(): return jax.nn.silu(result)  5 us
    ppermute x1, starting transfers between devices, passed_along(): lax.ppermute(value, axis, [(source, source + steps) for source in range(l...  4.87 us
  transfers between devices with their start and end apart: 2, of which 0 were waited for; matrix products, arithmetic and copies ran while one was open for 28% of the time, Pallas kernels for 28%

profile of v6, /device:TPU:141, one launch (start us, length us, event | category | flops | bytes accessed | tf_op | source)
XLA Modules:
  0.0 191.1 jit_solution(9000330845341581143)
XLA Ops:
  0.0 0.9 copy.101
  0.9 0.9 copy.102
  1.8 0.9 maximum_bitcast_fusion.refs_3_
  2.7 37.4 %shard_map.100 = (bf16[1024,128]{1,0:T(8,128)(2,1)}, bf16[1024,128]{1,0:T(8,128)(2,1)}, bf16[1024,256]{1,0:T(8,128)(2,1)}, bf16[8,128,4]{2,1,0:T(8,128)(2,1)}) custom-call(bf16[128,1024]{1,0:T(8,128)(2,1)} %refs_0_.1, bf16[128,1024]{1,0:T(8,128)(2,1)} %refs_1_.1, bf16[128,2048]{1,0:T(8,128)(2,1)} %refs_2_.1, bf16[8,128,4]{2,1,0:T(8,128)(2,1)} %maximum_bitcast_fusion.refs_3_), custom_call_target="tpu_custom_call" | custom-call | tf_op jit(solution)/shard_map/pallas_call | solution.py:357
  40.1 1.0 constant_dynamic-update-slice_fusion.2
  41.2 1.0 constant_dynamic-update-slice_fusion.1
  42.2 1.1 constant_dynamic-update-slice_fusion
  43.3 4.9 %collective-permute-start = (bf16[3,512]{1,0:T(4,128)(2,1)S(1)}, bf16[3,512]{1,0:T(4,128)(2,1)S(1)}, u32[]{:S(2)}, u32[]{:S(2)}) collective-permute-start(bf16[3,512]{1,0:T(4,128)(2,1)S(1)} %slice.114), channel_id=1, source_target_pairs={{0,8},{8,16},{16,24},{24,32},{32,40},{40,48},{48,56},{56,64},{64,7... | collective-permute-start | bytes 9224 | tf_op jit(solution)/shard_map/ppermute | solution.py:25
  48.2 0.9 copy.144
  49.1 6.0 %all-to-all-start = ((bf16[128,8,256]{2,0,1:T(8,128)(2,1)}), bf16[128,8,256]{2,0,1:T(8,128)(2,1)}, u32[]{:S(2)}, u32[]{:S(2)}) async-start(bf16[128,8,256]{2,0,1:T(8,128)(2,1)} %bitcast.92), calls=%async_computation | async-start | bytes 1048576 | tf_op jit(solution)/shard_map/all_to_all | solution.py:425
  55.7 0.5 reduce_window_sum.11
  57.2 1.6 convert_element_type.46
  59.2 5.0 %divide_multiply_fusion = f32[1024,512]{1,0:T(8,128)S(1)} fusion(f32[1024,512]{1,0:T(8,128)} %convert_element_type.46, f32[3,512]{1,0:T(4,128)S(1)} %convert_element_type.48, f32[512]{0:T(512)S(1)} %bitcast.111, f32[512]{0:T(512)S(1)} %bitcast.112, f32[512]{0:T(512)S(1)} %bitcast.113, f32[512]{0:T(512)S(1)} %bitcast.110), kind=kLoop, calls=%fused_computation.42 | loop fusion | flops 7340032 | bytes 4208640 | tf_op jit(solution)/shard_map/jit(silu)/mul | solution.py:66
  64.2 0.3 multiply_reduce_fusion.2
  64.6 1.1 divide_multiply_fusion.1
  65.7 1.0 fusion.74
  66.8 0.6 fusion.92
  67.3 0.6 fusion.109
  67.9 0.6 fusion.90
  68.6 0.7 fusion.98
  69.3 0.2 subtract_subtract_fusion
  69.5 0.7 fusion.88
  70.2 0.6 fusion.157
  70.9 0.7 fusion.86
  71.6 0.7 fusion.158
  72.5 0.7 fusion.84
  73.1 0.6 fusion.159
  73.9 0.7 fusion.82
  74.6 1.6 fusion.160
  76.1 1.3 broadcast_multiply_fusion
  77.5 0.5 reshape_reshape.2
  78.0 0.3 bitcast_multiply_fusion.1
  78.4 0.9 copy-done.10
  79.2 0.3 copy-done.11
  79.5 1.1 fusion.10
  80.7 2.3 %fusion.52 = f32[16,2,128,128]{3,2,1,0:T(8,128)S(1)} fusion(f32[16,2,64,256]{3,2,1,0:T(8,128)S(1)} %fusion.10, f32[16,64,128]{2,1,0:T(8,128)S(1)} %bitcast.95, f32[16,2,64]{2,1,0:T(2,128)S(1)} %copy.106), kind=kOutput, calls=%fused_computation.51 | convolution fusion | flops 201588736 | bytes 3686400 | tf_op jit(solution)/shard_map/nhcd,nhce->nhde/dot_general | solution.py:29
  83.2 2.3 %multiply_subtract_fusion = f32[16,2,128,128]{3,2,1,0:T(8,128)S(1)} fusion(f32[128,128]{1,0:T(8,128)S(1)} %fusion.128, f32[16,2]{1,0:T(8,128)S(1)} %copy.105, f32[16,2,64,256]{3,2,1,0:T(8,128)S(1)} %fusion.10, f32[16,64,128]{2,1,0:T(8,128)S(1)} %bitcast.96, f32[16,2,64]{2,1,0:T(2,128)S(1)} %copy.106), kind=kOutput, calls=%fused_computation.41 | convolution fusion | flops 202637312 | bytes 3760128 | tf_op jit(solution)/shard_map/nhcd,nhce->nhde/dot_general | solution.py:29
  85.7 1.3 fusion.40
  87.2 1.2 fusion
  88.6 1.2 fusion.43
  90.0 1.2 fusion.15
  91.4 1.2 fusion.46
  92.8 1.2 fusion.19
  94.0 1.4 fusion.49
  95.4 1.7 slice.136
  97.1 0.3 copy-done.5
  97.6 1.2 fusion.23
  98.8 1.3 copy-done.4
  100.2 1.9 %convolution_multiply_fusion = f32[16,2,64,64]{3,2,1,0:T(8,128)} fusion(f32[16,2,64]{2,1,0:T(2,128)S(1)} %copy.109, f32[16,64,128]{2,1,0:T(8,128)S(1)} %bitcast.97, f32[16,64,128]{2,1,0:T(8,128)S(1)} %bitcast.100, pred[64,64]{1,0:T(8,128)(4,1)S(1)} %get-tuple-element.30), kind=kOutput, calls=%fused_computation.61 | convolution fusion | flops 101187584 | bytes 1585152 | tf_op jit(solution)/shard_map/nhid,nhjd->nhij/dot_general | solution.py:106
  102.2 0.7 pad_maximum_fusion.5.maps_ref
  102.9 53.7 %shard_map.101 = f32[2,128,128]{2,1,0:T(8,128)} custom-call(f32[2,2,128,128]{3,2,1,0:T(8,128)} %pad_maximum_fusion.5.maps_ref), custom_call_target="tpu_custom_call" | custom-call | tf_op jit(solution)/shard_map/pallas_call | solution.py:288
  156.6 2.0 %multiply_subtract_fusion.1 = f32[16,2,64,128]{3,2,1,0:T(8,128)S(1)} fusion(f32[16,2,64,64]{3,2,1,0:T(8,128)} %convolution_multiply_fusion, f32[16,2,64,256]{3,2,1,0:T(8,128)S(1)} %fusion.10, f32[16,64,128]{2,1,0:T(8,128)S(1)} %bitcast.101, f32[16,2,64]{2,1,0:T(2,128)S(1)} %copy.104), kind=kOutput, calls=%fused_computation.54 | convolution fusion | flops 101187584 | bytes 3162112 | tf_op jit(solution)/shard_map/nhij,nhjd->nhid/dot_general | solution.py:29
  158.7 1.1 fusion.1
  159.8 0.6 convolution_bitcast_fusion
  160.3 0.9 copy-done.2
  161.3 1.0 fusion.71
  162.5 0.7 fusion.161
  163.2 1.3 multiply_reduce_fusion
  164.5 0.2 copy.124
  164.7 0.8 copy.117
  165.6 1.2 div.140
  166.8 2.4 %fusion.77.refs_0_ = bf16[1024,256]{1,0:T(8,128)(2,1)} fusion(f32[128,8,2,128]{3,2,1,0:T(2,128)S(1)} %bitcast.104, f32[128,8,2,128]{3,2,1,0:T(2,128)S(1)} %bitcast.103, bf16[128,8,256]{2,0,1:T(8,128)(2,1)} %all-to-all-done, f32[256]{0:T(256)S(1)} %broadcast_bitcast_fusion), kind=kLoop, calls=%fused_computation.67 | loop fusion | flops 2359296 | bytes 3146752 | tf_op jit(solution)/shard_map/convert_element_type | solution.py:131
  169.2 19.8 %shard_map.102 = bf16[128,2048]{1,0:T(8,128)(2,1)} custom-call(bf16[1024,256]{1,0:T(8,128)(2,1)} %fusion.77.refs_0_), custom_call_target="tpu_custom_call" | custom-call | tf_op jit(solution)/shard_map/pallas_call | solution.py:357
  189.0 1.9 copy.148
  (96 shorter events, 4.0 us)
Async XLA Ops:
  0.0 56.5 %copy-start = (f32[128]{0:T(128)S(1)}, f32[128]{0:T(128)}, u32[]{:S(2)}) copy-start(f32[128]{0:T(128)} %param.19) | copy-start | bytes 1540
  1.8 46.4 %copy-start.14 = (bf16[128,2048]{1,0:T(8,128)(2,1)S(1)}, bf16[128,2048]{1,0:T(8,128)(2,1)}, u32[]{:S(2)}) copy-start(bf16[128,2048]{1,0:T(8,128)(2,1)} %param.13) | copy-start | bytes 1572868
  40.1 15.2 %copy-start.15 = (bf16[4,256]{1,0:T(4,128)(2,1)S(1)}, bf16[4,256]{1,0:T(4,128)(2,1)}, u32[]{:S(2)}) copy-start(bf16[4,256]{1,0:T(4,128)(2,1)} %param.18) | copy-start | bytes 6148
  40.1 15.2 %copy-start.16 = (bf16[4,128]{1,0:T(4,128)(2,1)S(1)}, bf16[4,128]{1,0:T(4,128)(2,1)}, u32[]{:S(2)}) copy-start(bf16[4,128]{1,0:T(4,128)(2,1)} %param.17) | copy-start | bytes 3076
  40.1 15.2 %copy-start.17 = (bf16[4,128]{1,0:T(4,128)(2,1)S(1)}, bf16[4,128]{1,0:T(4,128)(2,1)}, u32[]{:S(2)}) copy-start(bf16[4,128]{1,0:T(4,128)(2,1)} %param.16) | copy-start | bytes 3076
  40.1 15.2 %copy-start.12 = (bf16[8,128,4]{2,1,0:T(8,128)(2,1)S(1)}, bf16[8,128,4]{2,1,0:T(8,128)(2,1)}, u32[]{:S(2)}) copy-start(bf16[8,128,4]{2,1,0:T(8,128)(2,1)} %get-tuple-element.9) | copy-start | bytes 24580
  43.3 15.9 %collective-permute-start = (bf16[3,512]{1,0:T(4,128)(2,1)S(1)}, bf16[3,512]{1,0:T(4,128)(2,1)S(1)}, u32[]{:S(2)}, u32[]{:S(2)}) collective-permute-start(bf16[3,512]{1,0:T(4,128)(2,1)S(1)} %slice.114), channel_id=1, source_target_pairs={{0,8},{8,16},{16,24},{24,32},{32,40},{40,48},{48,56},{56,64},{64,7... | collective-permute-start | bytes 9224 | tf_op jit(solution)/shard_map/ppermute | solution.py:25
  49.1 116.5 %all-to-all-start = ((bf16[128,8,256]{2,0,1:T(8,128)(2,1)}), bf16[128,8,256]{2,0,1:T(8,128)(2,1)}, u32[]{:S(2)}, u32[]{:S(2)}) async-start(bf16[128,8,256]{2,0,1:T(8,128)(2,1)} %bitcast.92), calls=%async_computation | async-start | bytes 1048576 | tf_op jit(solution)/shard_map/all_to_all | solution.py:425
  64.2 1.5 copy-start.3
  65.7 10.4 %copy-start.6 = (f32[1024,128]{1,0:T(8,128)}, f32[1024,128]{1,0:T(8,128)S(1)}, u32[]{:S(2)}) copy-start(f32[1024,128]{1,0:T(8,128)S(1)} %get-tuple-element.16) | copy-start | bytes 1572868
  74.6 2.9 %slice-start = ((f32[1024,512]{1,0:T(8,128)}), f32[1024,256]{1,0:T(8,128)S(1)}, s32[]{:S(2)}) async-start(f32[1024,512]{1,0:T(8,128)} %copy-done.3), calls=%async_computation.1 | async-start | bytes 2097152 | tf_op jit(solution)/shard_map/slice | solution.py:441
  78.0 1.2 copy-start.10
  78.0 1.5 copy-start.11
  79.5 1.1 copy-start.7
  95.4 2.0 %copy-start.5 = (f32[16,2,128,128]{3,2,1,0:T(8,128)}, f32[16,2,128,128]{3,2,1,0:T(8,128)S(1)}, u32[]{:S(2)}) copy-start(f32[16,2,128,128]{3,2,1,0:T(8,128)S(1)} %fusion.49) | copy-start | bytes 6291460
  98.8 1.3 copy-start.4
  98.8 1.4 copy-start.8
  100.1 2.0 %slice-start.3 = ((f32[16,2,128,128]{3,2,1,0:T(8,128)}), f32[1,2,128,128]{3,2,1,0:T(8,128)S(1)}, s32[]{:S(2)}) async-start(f32[16,2,128,128]{3,2,1,0:T(8,128)} %copy-done.5), calls=%async_computation.4 | async-start | bytes 262144 | tf_op jit(solution)/shard_map/slice | solution.py:476
  100.1 2.0 %slice-start.1 = ((f32[16,2,128,128]{3,2,1,0:T(8,128)}), f32[1,2,128,128]{3,2,1,0:T(8,128)S(1)}, s32[]{:S(2)}) async-start(f32[16,2,128,128]{3,2,1,0:T(8,128)} %copy-done.4), calls=%async_computation.2 | async-start | bytes 262144 | tf_op jit(solution)/shard_map/slice | solution.py:476
  156.6 2.1 %slice-start.2 = ((f32[16,2,128,128]{3,2,1,0:T(8,128)}), f32[15,2,128,128]{3,2,1,0:T(8,128)S(1)}, s32[]{:S(2)}) async-start(f32[16,2,128,128]{3,2,1,0:T(8,128)} %copy-done.4), calls=%async_computation.3 | async-start | bytes 3932160 | tf_op jit(solution)/shard_map/slice | solution.py:468
  158.7 1.1 copy-start.13
  159.7 1.5 copy-start.2
  161.3 1.2 copy-start.9
  166.8 24.1 %copy-start.1 = (f32[128]{0:T(128)S(1)}, f32[128]{0:T(128)}, u32[]{:S(2)}) copy-start(f32[128]{0:T(128)} %param.19) | copy-start | bytes 1540

commit v7 on v6

--- a/solution.py
+++ b/solution.py
@@ -42,14 +42,21 @@
             & ((cols_index // width) % 2 == 0)
         )
         lower = jnp.where(pick, strict, 0.0)
-        step = matmul("...ij,...jk->...ik", inverse, matmul("...ij,...jk->...ik", lower, inverse))
+        step = jnp.einsum(
+            "...ij,...jk->...ik",
+            inverse,
+            jnp.einsum("...ij,...jk->...ik", lower, inverse, precision=HIGHEST_PRECISION),
+            precision=HIGHEST_PRECISION,
+        )
         inverse = inverse - lax.optimization_barrier(step)
         width *= 2
     return inverse
 
 
 def forward_substitution(coupling, targets):
-    return matmul("...ij,...jf->...if", unit_lower_inverse(coupling), targets)
+    return jnp.einsum(
+        "...ij,...jf->...if", unit_lower_inverse(coupling), targets, precision=HIGHEST_PRECISION
+    )
 
 
 def causal_conv(inputs, earlier_rows, weights):
@@ -95,7 +102,7 @@
     strictly = rows_index > cols_index
     spread = jnp.where(causal, cumulative[..., :, None] - cumulative[..., None, :], 0.0)
     decays = jnp.where(causal, jnp.exp(spread), 0.0)
-    key_key = jnp.einsum("nhid,nhjd->nhij", keys, keys, precision=MATMUL_PRECISION)
+    key_key = jnp.einsum("nhid,nhjd->nhij", keys, keys, precision=HIGHEST_PRECISION)
     coupling = jnp.where(strictly, strength[..., None] * decays * key_key, 0.0)
     targets = jnp.concatenate(
         [(strength * jnp.exp(cumulative))[..., None] * keys, strength[..., None] * values], axis=-1

time: 195 us -> 203 us (1.041)
  matrix products: 33.9 us -> 42.4 us
    dot_general x1 -> x14, matrix products: 1.03 us -> 19.4 us  [the longest x6 8.46 us: unit_lower_inverse(): jnp.einsum('...ij,...jk->...ik', inverse, jnp.einsum('...ij,...jk->...ik'...]
    dot_general x29 -> x16, matrix products: 30.9 us -> 21.1 us  [matmul(): return jnp.einsum(spec, left, right, precision=MATMUL_PRECISION)]
  transfers between devices with their start and end apart: 2 -> 2, of which waited for: 0 -> 0; matrix products, arithmetic and copies ran while one was open for 28% -> 31% of each run, Pallas kernels for 28% -> 27%
where the time goes in v7:
time: 203 us; the launch traced here: 199 us
  Pallas kernels  111 us (55%)
  matrix products  42.4 us (21%)
  local copies, waits for them, and re-layouts  18.6 us (9%)
  other arithmetic  15.4 us (8%)
  starting transfers between devices  10.9 us (5%)
    pallas_call x2, Pallas kernels, head_exchange(): pl.pallas_call(functools.partial(head_exchange_kernel, parts, count, sour...  56.5 us
    pallas_call x1, Pallas kernels, ctx_scan(): pl.pallas_call(functools.partial(ctx_scan_kernel, count), out_shape=jax.S...  54.2 us
    dot_general x16, matrix products, matmul(): return jnp.einsum(spec, left, right, precision=MATMUL_PRECISION)  21.1 us
    dot_general x6, matrix products, unit_lower_inverse(): jnp.einsum('...ij,...jk->...ik', inverse, jnp.einsum('...ij,...jk->...ik'...  8.46 us
    unnamed x39, local copies, waits for them, and re-layouts  8.05 us
    dot_general x6, matrix products, unit_lower_inverse(): jnp.einsum('...ij,...jk->...ik', lower, inverse, precision=HIGHEST_PRECIS...  7.16 us
    all_to_all x1, starting transfers between devices, on_device(): lax.all_to_all(gate_rows, 'head', split_axis=1, concat_axis=0, tiled=True)  6.04 us
    ppermute x1, starting transfers between devices, passed_along(): lax.ppermute(value, axis, [(source, source + steps) for source in range(l...  4.87 us
  transfers between devices with their start and end apart: 2, of which 0 were waited for; matrix products, arithmetic and copies ran while one was open for 31% of the time, Pallas kernels for 27%

profile of v7, /device:TPU:141, one launch (start us, length us, event | category | flops | bytes accessed | tf_op | source)
XLA Modules:
  0.0 199.1 jit_solution(15660823483922179104)
XLA Ops:
  0.0 0.9 copy.101
  0.9 0.9 copy.102
  1.8 0.9 maximum_bitcast_fusion.refs_3_
  2.7 37.4 %shard_map.100 = (bf16[1024,128]{1,0:T(8,128)(2,1)}, bf16[1024,128]{1,0:T(8,128)(2,1)}, bf16[1024,256]{1,0:T(8,128)(2,1)}, bf16[8,128,4]{2,1,0:T(8,128)(2,1)}) custom-call(bf16[128,1024]{1,0:T(8,128)(2,1)} %refs_0_.1, bf16[128,1024]{1,0:T(8,128)(2,1)} %refs_1_.1, bf16[128,2048]{1,0:T(8,128)(2,1)} %refs_2_.1, bf16[8,128,4]{2,1,0:T(8,128)(2,1)} %maximum_bitcast_fusion.refs_3_), custom_call_target="tpu_custom_call" | custom-call | tf_op jit(solution)/shard_map/pallas_call | solution.py:364
  40.1 1.0 constant_dynamic-update-slice_fusion.2
  41.2 1.0 constant_dynamic-update-slice_fusion.1
  42.2 1.1 constant_dynamic-update-slice_fusion
  43.3 4.9 %collective-permute-start = (bf16[3,512]{1,0:T(4,128)(2,1)S(1)}, bf16[3,512]{1,0:T(4,128)(2,1)S(1)}, u32[]{:S(2)}, u32[]{:S(2)}) collective-permute-start(bf16[3,512]{1,0:T(4,128)(2,1)S(1)} %slice.114), channel_id=1, source_target_pairs={{0,8},{8,16},{16,24},{24,32},{32,40},{40,48},{48,56},{56,64},{64,7... | collective-permute-start | bytes 9224 | tf_op jit(solution)/shard_map/ppermute | solution.py:25
  48.2 0.9 copy.144
  49.1 6.0 %all-to-all-start = ((bf16[128,8,256]{2,0,1:T(8,128)(2,1)}), bf16[128,8,256]{2,0,1:T(8,128)(2,1)}, u32[]{:S(2)}, u32[]{:S(2)}) async-start(bf16[128,8,256]{2,0,1:T(8,128)(2,1)} %bitcast.92), calls=%async_computation | async-start | bytes 1048576 | tf_op jit(solution)/shard_map/all_to_all | solution.py:432
  55.7 0.5 reduce_window_sum.11
  57.2 1.6 convert_element_type.46
  59.2 4.7 %divide_multiply_fusion = f32[1024,512]{1,0:T(8,128)S(1)} fusion(f32[1024,512]{1,0:T(8,128)} %convert_element_type.46, f32[3,512]{1,0:T(4,128)S(1)} %convert_element_type.48, f32[512]{0:T(512)S(1)} %bitcast.111, f32[512]{0:T(512)S(1)} %bitcast.112, f32[512]{0:T(512)S(1)} %bitcast.113, f32[512]{0:T(512)S(1)} %bitcast.110), kind=kLoop, calls=%fused_computation.42 | loop fusion | flops 7340032 | bytes 4208640 | tf_op jit(solution)/shard_map/jit(silu)/mul | solution.py:73
  63.9 0.3 multiply_reduce_fusion.2
  64.3 1.2 divide_multiply_fusion.1
  65.5 1.8 fusion.74
  67.3 1.1 fusion.92
  68.4 1.0 fusion.109
  69.4 1.2 fusion.90
  70.7 1.3 fusion.98
  71.9 0.2 subtract_subtract_fusion
  72.1 1.2 fusion.88
  73.4 1.2 fusion.157
  74.7 1.2 fusion.86
  76.0 1.6 fusion.158
  77.7 1.2 fusion.84
  79.0 1.2 fusion.159
  80.3 1.2 fusion.82
  81.6 2.1 %fusion.160 = f32[16,2,64,64]{3,2,1,0:T(8,128)} fusion(f32[16,2,64,64]{3,2,1,0:T(8,128)S(1)} %sub.140, f32[16,2,64,64]{3,2,1,0:T(8,128)S(1)} %fusion.82), kind=kOutput, calls=%fused_computation.234 | convolution fusion | flops 100663296 | bytes 1572864 | tf_op jit(solution)/shard_map/...ij,...jk->...ik/dot_general | solution.py:45
  83.7 1.3 broadcast_multiply_fusion
  85.0 0.5 reshape_reshape.2
  85.6 0.3 bitcast_multiply_fusion.1
  85.9 0.9 copy-done.10
  86.8 0.3 copy-done.11
  87.1 1.9 fusion.10
  89.1 2.2 %fusion.52 = f32[16,2,128,128]{3,2,1,0:T(8,128)S(1)} fusion(f32[16,2,64,256]{3,2,1,0:T(8,128)S(1)} %fusion.10, f32[16,64,128]{2,1,0:T(8,128)S(1)} %bitcast.95, f32[16,2,64]{2,1,0:T(2,128)S(1)} %copy.106), kind=kOutput, calls=%fused_computation.51 | convolution fusion | flops 201588736 | bytes 3686400 | tf_op jit(solution)/shard_map/nhcd,nhce->nhde/dot_general | solution.py:29
  91.4 2.5 %multiply_subtract_fusion = f32[16,2,128,128]{3,2,1,0:T(8,128)S(1)} fusion(f32[128,128]{1,0:T(8,128)S(1)} %fusion.128, f32[16,2]{1,0:T(8,128)S(1)} %copy.105, f32[16,2,64,256]{3,2,1,0:T(8,128)S(1)} %fusion.10, f32[16,64,128]{2,1,0:T(8,128)S(1)} %bitcast.96, f32[16,2,64]{2,1,0:T(2,128)S(1)} %copy.106), kind=kOutput, calls=%fused_computation.41 | convolution fusion | flops 202637312 | bytes 3760128 | tf_op jit(solution)/shard_map/nhcd,nhce->nhde/dot_general | solution.py:29
  94.1 1.3 fusion.40
  95.6 1.2 fusion
  97.0 1.2 fusion.43
  98.4 1.2 fusion.15
  99.8 1.2 fusion.46
  101.2 1.2 fusion.19
  102.4 1.2 fusion.49
  103.6 1.7 slice.136
  105.3 0.3 copy-done.5
  105.8 1.2 fusion.23
  107.0 1.3 copy-done.4
  108.4 2.0 convolution_multiply_fusion
  110.4 0.7 pad_maximum_fusion.5.maps_ref
  111.1 54.2 %shard_map.101 = f32[2,128,128]{2,1,0:T(8,128)} custom-call(f32[2,2,128,128]{3,2,1,0:T(8,128)} %pad_maximum_fusion.5.maps_ref), custom_call_target="tpu_custom_call" | custom-call | tf_op jit(solution)/shard_map/pallas_call | solution.py:295
  165.3 2.0 %multiply_subtract_fusion.1 = f32[16,2,64,128]{3,2,1,0:T(8,128)S(1)} fusion(f32[16,2,64,64]{3,2,1,0:T(8,128)} %convolution_multiply_fusion, f32[16,2,64,256]{3,2,1,0:T(8,128)S(1)} %fusion.10, f32[16,64,128]{2,1,0:T(8,128)S(1)} %bitcast.101, f32[16,2,64]{2,1,0:T(2,128)S(1)} %copy.104), kind=kOutput, calls=%fused_computation.54 | convolution fusion | flops 101187584 | bytes 3162112 | tf_op jit(solution)/shard_map/nhij,nhjd->nhid/dot_general | solution.py:29
  167.4 1.1 fusion.1
  168.5 0.6 convolution_bitcast_fusion
  169.1 1.0 copy-done.2
  170.0 1.0 fusion.71
  171.3 0.7 fusion.161
  171.9 1.3 multiply_reduce_fusion
  173.2 0.2 copy.124
  173.5 0.8 copy.117
  174.3 1.2 div.140
  175.6 2.4 %fusion.77.refs_0_ = bf16[1024,256]{1,0:T(8,128)(2,1)} fusion(f32[128,8,2,128]{3,2,1,0:T(2,128)S(1)} %bitcast.104, f32[128,8,2,128]{3,2,1,0:T(2,128)S(1)} %bitcast.103, bf16[128,8,256]{2,0,1:T(8,128)(2,1)} %all-to-all-done, f32[256]{0:T(256)S(1)} %broadcast_bitcast_fusion), kind=kLoop, calls=%fused_computation.67 | loop fusion | flops 2359296 | bytes 3146752 | tf_op jit(solution)/shard_map/convert_element_type | solution.py:138
  178.0 19.0 %shard_map.102 = bf16[128,2048]{1,0:T(8,128)(2,1)} custom-call(bf16[1024,256]{1,0:T(8,128)(2,1)} %fusion.77.refs_0_), custom_call_target="tpu_custom_call" | custom-call | tf_op jit(solution)/shard_map/pallas_call | solution.py:364
  197.0 1.9 copy.148
  (96 shorter events, 4.0 us)
Async XLA Ops:
  0.0 56.5 %copy-start = (f32[128]{0:T(128)S(1)}, f32[128]{0:T(128)}, u32[]{:S(2)}) copy-start(f32[128]{0:T(128)} %param.19) | copy-start | bytes 1540
  1.8 46.4 %copy-start.14 = (bf16[128,2048]{1,0:T(8,128)(2,1)S(1)}, bf16[128,2048]{1,0:T(8,128)(2,1)}, u32[]{:S(2)}) copy-start(bf16[128,2048]{1,0:T(8,128)(2,1)} %param.13) | copy-start | bytes 1572868
  40.1 15.2 %copy-start.15 = (bf16[4,256]{1,0:T(4,128)(2,1)S(1)}, bf16[4,256]{1,0:T(4,128)(2,1)}, u32[]{:S(2)}) copy-start(bf16[4,256]{1,0:T(4,128)(2,1)} %param.18) | copy-start | bytes 6148
  40.1 15.2 %copy-start.16 = (bf16[4,128]{1,0:T(4,128)(2,1)S(1)}, bf16[4,128]{1,0:T(4,128)(2,1)}, u32[]{:S(2)}) copy-start(bf16[4,128]{1,0:T(4,128)(2,1)} %param.17) | copy-start | bytes 3076
  40.1 15.2 %copy-start.17 = (bf16[4,128]{1,0:T(4,128)(2,1)S(1)}, bf16[4,128]{1,0:T(4,128)(2,1)}, u32[]{:S(2)}) copy-start(bf16[4,128]{1,0:T(4,128)(2,1)} %param.16) | copy-start | bytes 3076
  40.1 15.2 %copy-start.12 = (bf16[8,128,4]{2,1,0:T(8,128)(2,1)S(1)}, bf16[8,128,4]{2,1,0:T(8,128)(2,1)}, u32[]{:S(2)}) copy-start(bf16[8,128,4]{2,1,0:T(8,128)(2,1)} %get-tuple-element.9) | copy-start | bytes 24580
  43.3 15.9 %collective-permute-start = (bf16[3,512]{1,0:T(4,128)(2,1)S(1)}, bf16[3,512]{1,0:T(4,128)(2,1)S(1)}, u32[]{:S(2)}, u32[]{:S(2)}) collective-permute-start(bf16[3,512]{1,0:T(4,128)(2,1)S(1)} %slice.114), channel_id=1, source_target_pairs={{0,8},{8,16},{16,24},{24,32},{32,40},{40,48},{48,56},{56,64},{64,7... | collective-permute-start | bytes 9224 | tf_op jit(solution)/shard_map/ppermute | solution.py:25
  49.1 125.3 %all-to-all-start = ((bf16[128,8,256]{2,0,1:T(8,128)(2,1)}), bf16[128,8,256]{2,0,1:T(8,128)(2,1)}, u32[]{:S(2)}, u32[]{:S(2)}) async-start(bf16[128,8,256]{2,0,1:T(8,128)(2,1)} %bitcast.92), calls=%async_computation | async-start | bytes 1048576 | tf_op jit(solution)/shard_map/all_to_all | solution.py:432
  63.9 1.5 copy-start.3
  65.5 18.2 %copy-start.6 = (f32[1024,128]{1,0:T(8,128)}, f32[1024,128]{1,0:T(8,128)S(1)}, u32[]{:S(2)}) copy-start(f32[1024,128]{1,0:T(8,128)S(1)} %get-tuple-element.16) | copy-start | bytes 1572868
  81.5 3.5 %slice-start = ((f32[1024,512]{1,0:T(8,128)}), f32[1024,256]{1,0:T(8,128)S(1)}, s32[]{:S(2)}) async-start(f32[1024,512]{1,0:T(8,128)} %copy-done.3), calls=%async_computation.1 | async-start | bytes 2097152 | tf_op jit(solution)/shard_map/slice | solution.py:448
  85.6 1.2 copy-start.10
  85.6 1.5 copy-start.11
  87.1 1.9 copy-start.7
  103.6 2.0 %copy-start.5 = (f32[16,2,128,128]{3,2,1,0:T(8,128)}, f32[16,2,128,128]{3,2,1,0:T(8,128)S(1)}, u32[]{:S(2)}) copy-start(f32[16,2,128,128]{3,2,1,0:T(8,128)S(1)} %fusion.49) | copy-start | bytes 6291460
  107.0 1.3 copy-start.4
  107.0 1.4 copy-start.8
  108.3 2.0 %slice-start.3 = ((f32[16,2,128,128]{3,2,1,0:T(8,128)}), f32[1,2,128,128]{3,2,1,0:T(8,128)S(1)}, s32[]{:S(2)}) async-start(f32[16,2,128,128]{3,2,1,0:T(8,128)} %copy-done.5), calls=%async_computation.4 | async-start | bytes 262144 | tf_op jit(solution)/shard_map/slice | solution.py:483
  108.3 2.0 %slice-start.1 = ((f32[16,2,128,128]{3,2,1,0:T(8,128)}), f32[1,2,128,128]{3,2,1,0:T(8,128)S(1)}, s32[]{:S(2)}) async-start(f32[16,2,128,128]{3,2,1,0:T(8,128)} %copy-done.4), calls=%async_computation.2 | async-start | bytes 262144 | tf_op jit(solution)/shard_map/slice | solution.py:483
  165.3 2.1 %slice-start.2 = ((f32[16,2,128,128]{3,2,1,0:T(8,128)}), f32[15,2,128,128]{3,2,1,0:T(8,128)S(1)}, s32[]{:S(2)}) async-start(f32[16,2,128,128]{3,2,1,0:T(8,128)} %copy-done.4), calls=%async_computation.3 | async-start | bytes 3932160 | tf_op jit(solution)/shard_map/slice | solution.py:475
  167.4 1.1 copy-start.13
  168.5 1.5 copy-start.2
  170.0 1.2 copy-start.9
  175.6 23.3 %copy-start.1 = (f32[128]{0:T(128)S(1)}, f32[128]{0:T(128)}, u32[]{:S(2)}) copy-start(f32[128]{0:T(128)} %param.19) | copy-start | bytes 1540

commit v8 on v6

--- a/solution.py
+++ b/solution.py
@@ -302,9 +302,9 @@
     )(maps)
 
 
-def head_exchange_kernel(parts, count, source_view, target_view, *refs):
-    sources, targets = refs[:count], refs[count : 2 * count]
-    send_sems, recv_sems = refs[2 * count], refs[2 * count + 1]
+def head_exchange_kernel(parts, plan, count, *refs):
+    sources, targets = refs[:count], refs[count:-2]
+    send_sems, recv_sems = refs[-2], refs[-1]
     me = lax.axis_index("head")
     line = lax.axis_index("ctx")
     barrier = pltpu.get_barrier_semaphore()
@@ -315,13 +315,13 @@
             pl.semaphore_signal(barrier, inc=1, device_id=(line, peer), device_id_type=MESH_IDS)
 
     pl.semaphore_wait(barrier, parts - 1)
-    outgoing, incoming, local = [], [], []
-    for index in range(count):
+    pending = []
+    for index, (source_at, target_at, source_view, target_view) in enumerate(plan):
         for peer in range(parts):
             away = peer != me
             sending = pltpu.make_async_remote_copy(
-                src_ref=source_view(sources[index], peer),
-                dst_ref=target_view(targets[index], me),
+                src_ref=source_view(sources[source_at], peer),
+                dst_ref=target_view(targets[target_at], me),
                 send_sem=send_sems.at[index, peer],
                 recv_sem=recv_sems.at[index, me],
                 device_id=(line, peer),
@@ -329,39 +329,37 @@
             )
             pl.when(away)(sending.start)
             staying = pltpu.make_async_copy(
-                source_view(sources[index], peer),
-                target_view(targets[index], peer),
+                source_view(sources[source_at], peer),
+                target_view(targets[target_at], peer),
                 send_sems.at[index, peer],
             )
             pl.when(jnp.logical_not(away))(staying.start)
             arriving = pltpu.make_async_remote_copy(
-                src_ref=source_view(sources[index], peer),
-                dst_ref=target_view(targets[index], peer),
+                src_ref=source_view(sources[source_at], peer),
+                dst_ref=target_view(targets[target_at], peer),
                 send_sem=send_sems.at[index, peer],
                 recv_sem=recv_sems.at[index, peer],
                 device_id=(line, peer),
                 device_id_type=MESH_IDS,
             )
-            outgoing.append((away, sending))
-            incoming.append((away, arriving))
-            local.append((away, staying))
-    for (away, sending), (_, arriving), (_, staying) in zip(outgoing, incoming, local):
+            pending.append((away, sending, arriving, staying))
+    for away, sending, arriving, staying in pending:
         pl.when(away)(sending.wait_send)
         pl.when(away)(arriving.wait_recv)
         pl.when(jnp.logical_not(away))(staying.wait)
 
 
-def head_exchange(arrays, target_shapes, source_view, target_view, collective):
+def head_exchange(arrays, target_specs, plan, collective):
     parts = lax.axis_size("head")
     count = len(arrays)
     return pl.pallas_call(
-        functools.partial(head_exchange_kernel, parts, count, source_view, target_view),
-        out_shape=[jax.ShapeDtypeStruct(shape, array.dtype) for shape, array in zip(target_shapes, arrays)],
+        functools.partial(head_exchange_kernel, parts, plan, count),
+        out_shape=[jax.ShapeDtypeStruct(shape, dtype) for shape, dtype in target_specs],
         in_specs=[pl.BlockSpec(memory_space=pl.ANY)] * count,
-        out_specs=[pl.BlockSpec(memory_space=pl.ANY)] * count,
+        out_specs=[pl.BlockSpec(memory_space=pl.ANY)] * len(target_specs),
         scratch_shapes=[
-            pltpu.SemaphoreType.DMA((count, parts)),
-            pltpu.SemaphoreType.DMA((count, parts)),
+            pltpu.SemaphoreType.DMA((len(plan), parts)),
+            pltpu.SemaphoreType.DMA((len(plan), parts)),
         ],
         compiler_params=pltpu.CompilerParams(collective_id=collective, has_side_effects=True),
     )(*arrays)
@@ -381,19 +379,31 @@
     return ref.at[pl.ds(peer * height, height), :]
 
 
-def spread_heads(arrays):
+def block_of(ref, peer):
+    return ref.at[peer]
+
+
+def spread_heads(joined_parts, scalars):
     parts = lax.axis_size("head")
-    shapes = [
-        array.shape if array.ndim == 3 else (parts * array.shape[0], array.shape[1] // parts)
-        for array in arrays
-    ]
-    return head_exchange(arrays, shapes, columns_of, rows_of, 1)
+    rows = joined_parts[0].shape[0]
+    widths = [array.shape[1] // parts for array in joined_parts]
+    plan = []
+    for index, width in enumerate(widths):
+        offset = sum(widths[:index])
+
+        def placed(ref, peer, offset=offset, width=width):
+            return ref.at[pl.ds(peer * rows, rows), pl.ds(offset, width)]
+
+        plan.append((index, 0, columns_of, placed))
+    plan.append((len(joined_parts), 1, block_of, block_of))
+    specs = [((parts * rows, sum(widths)), joined_parts[0].dtype), (scalars.shape, scalars.dtype)]
+    return head_exchange(list(joined_parts) + [scalars], specs, plan, 1)
 
 
 def gather_heads(array):
     parts = lax.axis_size("head")
     shape = (array.shape[0] // parts, array.shape[1] * parts)
-    return head_exchange([array], [shape], rows_of, columns_of, 2)[0]
+    return head_exchange([array], [(shape, array.dtype)], [(0, 0, rows_of, columns_of)], 2)[0]
 
 
 def on_device(
@@ -416,20 +426,17 @@
         ],
         axis=2,
     ).transpose(1, 0, 2)
-    device_query, local_key, local_value, moved_scalars = spread_heads(
-        [query_rows, key_rows, value_rows, scalars]
-    )
+    joined, moved_scalars = spread_heads([query_rows, key_rows, value_rows], scalars)
     moved_scalars = moved_scalars.reshape(-1, moved_scalars.shape[-1])
     split_at = log_decay.shape[1] // parts
     local_decay, local_strength = moved_scalars[:, :split_at], moved_scalars[:, split_at:]
     local_gate = lax.all_to_all(gate_rows, "head", split_axis=1, concat_axis=0, tiled=True)
-    joined = jnp.concatenate([device_query, local_key, local_value], axis=1)
     kernel_width = conv_query.shape[0]
     count_rows = joined.shape[0]
     tail_rows = passed_along(joined[count_rows - (kernel_width - 1) :], "ctx", 1)
     weights_all = jnp.concatenate([conv_query, conv_key, conv_value], axis=1).astype(jnp.float32)
     mixed = causal_conv(joined.astype(jnp.float32), tail_rows.astype(jnp.float32), weights_all)
-    key_width = device_query.shape[1]
+    key_width = query_rows.shape[1] // parts
     head_keys = key_width // DK
     per_key = HV // HK
     query_heads = jnp.repeat(

time: 195 us -> 194 us (level)
  local copies, waits for them, and re-layouts: 18.6 us -> 16.3 us
    unnamed x39 -> x37, local copies, waits for them, and re-layouts: 8.04 us -> 5.98 us
where the time goes in v8:
time: 194 us; the launch traced here: 190 us
  Pallas kernels  111 us (57%)
  matrix products  33.9 us (17%)
  other arithmetic  16.9 us (9%)
  local copies, waits for them, and re-layouts  16.3 us (8%)
  starting transfers between devices  10.9 us (6%)
    pallas_call x2, Pallas kernels, head_exchange(): pl.pallas_call(functools.partial(head_exchange_kernel, parts, plan, count...  57.2 us
    pallas_call x1, Pallas kernels, ctx_scan(): pl.pallas_call(functools.partial(ctx_scan_kernel, count), out_shape=jax.S...  53.7 us
    dot_general x29, matrix products, matmul(): return jnp.einsum(spec, left, right, precision=MATMUL_PRECISION)  30.9 us
    all_to_all x1, starting transfers between devices, on_device(): lax.all_to_all(gate_rows, 'head', split_axis=1, concat_axis=0, tiled=True)  6.04 us
    unnamed x37, local copies, waits for them, and re-layouts  5.98 us
    mul x1, other arithmetic, causal_conv(): return jax.nn.silu(result)  5 us
    ppermute x1, starting transfers between devices, passed_along(): lax.ppermute(value, axis, [(source, source + steps) for source in range(l...  4.86 us
  transfers between devices with their start and end apart: 2, of which 0 were waited for; matrix products, arithmetic and copies ran while one was open for 28% of the time, Pallas kernels for 28%

profile of v8, /device:TPU:141, one launch (start us, length us, event | category | flops | bytes accessed | tf_op | source)
XLA Modules:
  0.0 190.0 jit_solution(6869359374025826403)
XLA Ops:
  0.0 0.9 copy.101
  1.0 0.9 copy.102
  1.9 0.9 maximum_bitcast_fusion.refs_3_
  2.7 37.4 %shard_map.100 = (bf16[1024,512]{1,0:T(8,128)(2,1)}, bf16[8,128,4]{2,1,0:T(8,128)(2,1)}) custom-call(bf16[128,1024]{1,0:T(8,128)(2,1)} %refs_0_.1, bf16[128,1024]{1,0:T(8,128)(2,1)} %refs_1_.1, bf16[128,2048]{1,0:T(8,128)(2,1)} %refs_2_.1, bf16[8,128,4]{2,1,0:T(8,128)(2,1)} %maximum_bitcast_fusion.refs_3_), custom_call_target="tpu_custom_call" | custom-call | tf_op jit(solution)/shard_map/pallas_call | solution.py:355
  40.2 0.7 slice.86
  40.9 4.9 %collective-permute-start = (bf16[3,512]{1,0:T(4,128)(2,1)S(1)}, bf16[3,512]{1,0:T(4,128)(2,1)S(1)}, u32[]{:S(2)}, u32[]{:S(2)}) collective-permute-start(bf16[3,512]{1,0:T(4,128)(2,1)S(1)} %slice.86), channel_id=1, source_target_pairs={{0,8},{8,16},{16,24},{24,32},{32,40},{40,48},{48,56},{56,64},{64,7... | collective-permute-start | bytes 9224 | tf_op jit(solution)/shard_map/ppermute | solution.py:25
  45.8 0.9 copy.144
  46.7 6.0 %all-to-all-start = ((bf16[128,8,256]{2,0,1:T(8,128)(2,1)}), bf16[128,8,256]{2,0,1:T(8,128)(2,1)}, u32[]{:S(2)}, u32[]{:S(2)}) async-start(bf16[128,8,256]{2,0,1:T(8,128)(2,1)} %bitcast.92), calls=%async_computation | async-start | bytes 1048576 | tf_op jit(solution)/shard_map/all_to_all | solution.py:433
  53.3 0.5 reduce_window_sum.11
  53.9 0.2 copy.142
  54.8 2.9 %convert_element_type.46 = f32[1024,512]{1,0:T(8,128)} convert(bf16[1024,512]{1,0:T(8,128)(2,1)} %get-tuple-element.8) | non-fusion elementwise | flops 524288 | bytes 3145728 | tf_op jit(solution)/shard_map/convert_element_type | solution.py:438
  57.7 0.2 copy.108
  58.0 5.0 %divide_multiply_fusion = f32[1024,512]{1,0:T(8,128)S(1)} fusion(f32[1024,512]{1,0:T(8,128)} %convert_element_type.46, f32[3,512]{1,0:T(4,128)S(1)} %convert_element_type.48, f32[512]{0:T(512)S(1)} %bitcast.111, f32[512]{0:T(512)S(1)} %bitcast.112, f32[512]{0:T(512)S(1)} %bitcast.113, f32[512]{0:T(512)S(1)} %bitcast.110), kind=kLoop, calls=%fused_computation.42 | loop fusion | flops 7340032 | bytes 4208640 | tf_op jit(solution)/shard_map/jit(silu)/mul | solution.py:66
  63.1 0.3 multiply_reduce_fusion.2
  63.4 1.1 divide_multiply_fusion.1
  64.6 1.0 fusion.74
  65.6 0.6 fusion.92
  66.2 0.6 fusion.109
  66.8 0.6 fusion.90
  67.4 0.7 fusion.98
  68.1 0.2 subtract_subtract_fusion
  68.3 0.7 fusion.88
  69.0 0.6 fusion.157
  69.8 0.7 fusion.86
  70.4 0.7 fusion.158
  71.3 0.7 fusion.84
  72.0 0.6 fusion.159
  72.7 0.7 fusion.82
  73.4 1.6 fusion.160
  75.0 1.3 broadcast_multiply_fusion
  76.3 0.5 reshape_reshape.2
  76.9 0.3 bitcast_multiply_fusion.1
  77.2 0.9 copy-done.10
  78.1 0.3 copy-done.11
  78.4 1.1 fusion.10
  79.5 2.3 %fusion.52 = f32[16,2,128,128]{3,2,1,0:T(8,128)S(1)} fusion(f32[16,2,64,256]{3,2,1,0:T(8,128)S(1)} %fusion.10, f32[16,64,128]{2,1,0:T(8,128)S(1)} %bitcast.95, f32[16,2,64]{2,1,0:T(2,128)S(1)} %copy.106), kind=kOutput, calls=%fused_computation.51 | convolution fusion | flops 201588736 | bytes 3686400 | tf_op jit(solution)/shard_map/nhcd,nhce->nhde/dot_general | solution.py:29
  82.0 2.3 %multiply_subtract_fusion = f32[16,2,128,128]{3,2,1,0:T(8,128)S(1)} fusion(f32[128,128]{1,0:T(8,128)S(1)} %fusion.128, f32[16,2]{1,0:T(8,128)S(1)} %copy.105, f32[16,2,64,256]{3,2,1,0:T(8,128)S(1)} %fusion.10, f32[16,64,128]{2,1,0:T(8,128)S(1)} %bitcast.96, f32[16,2,64]{2,1,0:T(2,128)S(1)} %copy.106), kind=kOutput, calls=%fused_computation.41 | convolution fusion | flops 202637312 | bytes 3760128 | tf_op jit(solution)/shard_map/nhcd,nhce->nhde/dot_general | solution.py:29
  84.6 1.3 fusion.40
  86.1 1.2 fusion
  87.5 1.2 fusion.43
  88.9 1.2 fusion.15
  90.3 1.2 fusion.46
  91.6 1.2 fusion.19
  92.8 1.4 fusion.49
  94.2 1.7 slice.135
  95.9 0.3 copy-done.5
  96.4 1.2 fusion.23
  97.6 1.3 copy-done.4
  99.1 1.9 %convolution_multiply_fusion = f32[16,2,64,64]{3,2,1,0:T(8,128)} fusion(f32[16,2,64]{2,1,0:T(2,128)S(1)} %copy.109, f32[16,64,128]{2,1,0:T(8,128)S(1)} %bitcast.97, f32[16,64,128]{2,1,0:T(8,128)S(1)} %bitcast.100, pred[64,64]{1,0:T(8,128)(4,1)S(1)} %get-tuple-element.26), kind=kOutput, calls=%fused_computation.61 | convolution fusion | flops 101187584 | bytes 1585152 | tf_op jit(solution)/shard_map/nhid,nhjd->nhij/dot_general | solution.py:106
  101.0 0.7 pad_maximum_fusion.5.maps_ref
  101.7 53.7 %shard_map.101 = f32[2,128,128]{2,1,0:T(8,128)} custom-call(f32[2,2,128,128]{3,2,1,0:T(8,128)} %pad_maximum_fusion.5.maps_ref), custom_call_target="tpu_custom_call" | custom-call | tf_op jit(solution)/shard_map/pallas_call | solution.py:288
  155.4 2.0 %multiply_subtract_fusion.1 = f32[16,2,64,128]{3,2,1,0:T(8,128)S(1)} fusion(f32[16,2,64,64]{3,2,1,0:T(8,128)} %convolution_multiply_fusion, f32[16,2,64,256]{3,2,1,0:T(8,128)S(1)} %fusion.10, f32[16,64,128]{2,1,0:T(8,128)S(1)} %bitcast.101, f32[16,2,64]{2,1,0:T(2,128)S(1)} %copy.104), kind=kOutput, calls=%fused_computation.54 | convolution fusion | flops 101187584 | bytes 3162112 | tf_op jit(solution)/shard_map/nhij,nhjd->nhid/dot_general | solution.py:29
  157.5 1.1 fusion.1
  158.6 0.6 convolution_bitcast_fusion
  159.2 0.9 copy-done.2
  160.1 1.0 fusion.71
  161.4 0.7 fusion.161
  162.0 1.3 multiply_reduce_fusion
  163.3 0.2 copy.124
  163.6 0.8 copy.117
  164.4 1.2 div.140
  165.7 2.4 %fusion.77.refs_0_ = bf16[1024,256]{1,0:T(8,128)(2,1)} fusion(f32[128,8,2,128]{3,2,1,0:T(2,128)S(1)} %bitcast.104, f32[128,8,2,128]{3,2,1,0:T(2,128)S(1)} %bitcast.103, bf16[128,8,256]{2,0,1:T(8,128)(2,1)} %all-to-all-done, f32[256]{0:T(256)S(1)} %broadcast_bitcast_fusion), kind=kLoop, calls=%fused_computation.67 | loop fusion | flops 2359296 | bytes 3146752 | tf_op jit(solution)/shard_map/convert_element_type | solution.py:131
  168.1 19.8 %shard_map.102 = bf16[128,2048]{1,0:T(8,128)(2,1)} custom-call(bf16[1024,256]{1,0:T(8,128)(2,1)} %fusion.77.refs_0_), custom_call_target="tpu_custom_call" | custom-call | tf_op jit(solution)/shard_map/pallas_call | solution.py:355
  187.9 1.9 copy.146
  (93 shorter events, 3.6 us)
Async XLA Ops:
  0.0 54.1 %copy-start = (f32[128]{0:T(128)S(1)}, f32[128]{0:T(128)}, u32[]{:S(2)}) copy-start(f32[128]{0:T(128)} %param.19) | copy-start | bytes 1540
  0.0 45.8 %copy-start.14 = (bf16[128,2048]{1,0:T(8,128)(2,1)S(1)}, bf16[128,2048]{1,0:T(8,128)(2,1)}, u32[]{:S(2)}) copy-start(bf16[128,2048]{1,0:T(8,128)(2,1)} %param.13) | copy-start | bytes 1572868
  1.9 51.0 %copy-start.15 = (bf16[4,256]{1,0:T(4,128)(2,1)S(1)}, bf16[4,256]{1,0:T(4,128)(2,1)}, u32[]{:S(2)}) copy-start(bf16[4,256]{1,0:T(4,128)(2,1)} %param.18) | copy-start | bytes 6148
  1.9 51.0 %copy-start.16 = (bf16[4,128]{1,0:T(4,128)(2,1)S(1)}, bf16[4,128]{1,0:T(4,128)(2,1)}, u32[]{:S(2)}) copy-start(bf16[4,128]{1,0:T(4,128)(2,1)} %param.17) | copy-start | bytes 3076
  1.9 51.0 %copy-start.17 = (bf16[4,128]{1,0:T(4,128)(2,1)S(1)}, bf16[4,128]{1,0:T(4,128)(2,1)}, u32[]{:S(2)}) copy-start(bf16[4,128]{1,0:T(4,128)(2,1)} %param.16) | copy-start | bytes 3076
  40.2 12.8 %copy-start.12 = (bf16[8,128,4]{2,1,0:T(8,128)(2,1)S(1)}, bf16[8,128,4]{2,1,0:T(8,128)(2,1)}, u32[]{:S(2)}) copy-start(bf16[8,128,4]{2,1,0:T(8,128)(2,1)} %get-tuple-element.7) | copy-start | bytes 24580
  40.9 17.1 %collective-permute-start = (bf16[3,512]{1,0:T(4,128)(2,1)S(1)}, bf16[3,512]{1,0:T(4,128)(2,1)S(1)}, u32[]{:S(2)}, u32[]{:S(2)}) collective-permute-start(bf16[3,512]{1,0:T(4,128)(2,1)S(1)} %slice.86), channel_id=1, source_target_pairs={{0,8},{8,16},{16,24},{24,32},{32,40},{40,48},{48,56},{56,64},{64,7... | collective-permute-start | bytes 9224 | tf_op jit(solution)/shard_map/ppermute | solution.py:25
  46.7 117.7 %all-to-all-start = ((bf16[128,8,256]{2,0,1:T(8,128)(2,1)}), bf16[128,8,256]{2,0,1:T(8,128)(2,1)}, u32[]{:S(2)}, u32[]{:S(2)}) async-start(bf16[128,8,256]{2,0,1:T(8,128)(2,1)} %bitcast.92), calls=%async_computation | async-start | bytes 1048576 | tf_op jit(solution)/shard_map/all_to_all | solution.py:433
  63.1 1.5 copy-start.3
  64.6 10.4 %copy-start.6 = (f32[1024,128]{1,0:T(8,128)}, f32[1024,128]{1,0:T(8,128)S(1)}, u32[]{:S(2)}) copy-start(f32[1024,128]{1,0:T(8,128)S(1)} %get-tuple-element.12) | copy-start | bytes 1572868
  73.4 2.9 %slice-start = ((f32[1024,512]{1,0:T(8,128)}), f32[1024,256]{1,0:T(8,128)S(1)}, s32[]{:S(2)}) async-start(f32[1024,512]{1,0:T(8,128)} %copy-done.3), calls=%async_computation.1 | async-start | bytes 2097152 | tf_op jit(solution)/shard_map/slice | solution.py:448
  76.8 1.2 copy-start.10
  76.8 1.5 copy-start.11
  78.4 1.1 copy-start.7
  94.2 2.0 %copy-start.5 = (f32[16,2,128,128]{3,2,1,0:T(8,128)}, f32[16,2,128,128]{3,2,1,0:T(8,128)S(1)}, u32[]{:S(2)}) copy-start(f32[16,2,128,128]{3,2,1,0:T(8,128)S(1)} %fusion.49) | copy-start | bytes 6291460
  97.6 1.3 copy-start.4
  97.6 1.4 copy-start.8
  99.0 2.0 %slice-start.3 = ((f32[16,2,128,128]{3,2,1,0:T(8,128)}), f32[1,2,128,128]{3,2,1,0:T(8,128)S(1)}, s32[]{:S(2)}) async-start(f32[16,2,128,128]{3,2,1,0:T(8,128)} %copy-done.5), calls=%async_computation.4 | async-start | bytes 262144 | tf_op jit(solution)/shard_map/slice | solution.py:483
  99.0 2.0 %slice-start.1 = ((f32[16,2,128,128]{3,2,1,0:T(8,128)}), f32[1,2,128,128]{3,2,1,0:T(8,128)S(1)}, s32[]{:S(2)}) async-start(f32[16,2,128,128]{3,2,1,0:T(8,128)} %copy-done.4), calls=%async_computation.2 | async-start | bytes 262144 | tf_op jit(solution)/shard_map/slice | solution.py:483
  155.4 2.1 %slice-start.2 = ((f32[16,2,128,128]{3,2,1,0:T(8,128)}), f32[15,2,128,128]{3,2,1,0:T(8,128)S(1)}, s32[]{:S(2)}) async-start(f32[16,2,128,128]{3,2,1,0:T(8,128)} %copy-done.4), calls=%async_computation.3 | async-start | bytes 3932160 | tf_op jit(solution)/shard_map/slice | solution.py:475
  157.5 1.1 copy-start.13
  158.6 1.5 copy-start.2
  160.1 1.2 copy-start.9
  165.7 24.1 %copy-start.1 = (f32[128]{0:T(128)S(1)}, f32[128]{0:T(128)}, u32[]{:S(2)}) copy-start(f32[128]{0:T(128)} %param.19) | copy-start | bytes 1540

commit v9 on v8

--- a/solution.py
+++ b/solution.py
@@ -33,19 +33,21 @@
     size = strict.shape[-1]
     rows_index = jnp.arange(size)[:, None]
     cols_index = jnp.arange(size)[None, :]
-    inverse = jnp.broadcast_to(jnp.eye(size, dtype=strict.dtype), strict.shape)
-    width = 1
-    while width < size:
+    levels = max(size - 1, 1).bit_length()
+
+    def level(step, inverse):
+        width = jnp.left_shift(jnp.int32(1), step)
         pick = (
             (rows_index // (2 * width) == cols_index // (2 * width))
             & ((rows_index // width) % 2 == 1)
             & ((cols_index // width) % 2 == 0)
         )
         lower = jnp.where(pick, strict, 0.0)
-        step = matmul("...ij,...jk->...ik", inverse, matmul("...ij,...jk->...ik", lower, inverse))
-        inverse = inverse - lax.optimization_barrier(step)
-        width *= 2
-    return inverse
+        update = matmul("...ij,...jk->...ik", inverse, matmul("...ij,...jk->...ik", lower, inverse))
+        return inverse - lax.optimization_barrier(update)
+
+    start = jnp.broadcast_to(jnp.eye(size, dtype=strict.dtype), strict.shape)
+    return lax.fori_loop(0, levels, level, start)
 
 
 def forward_substitution(coupling, targets):

time: 194 us -> 189 us (0.974); the launches traced: 190 us -> 188 us
  other arithmetic: 16.9 us -> 14.3 us
    mul x1, other arithmetic: 5 us -> 1.3 us  [causal_conv(): return jax.nn.silu(result)]
    unnamed x37 -> x35, local copies, waits for them, and re-layouts: 5.98 us -> 5.68 us
  transfers between devices with their start and end apart: 2 -> 2, of which waited for: 0 -> 0; matrix products, arithmetic and copies ran while one was open for 28% -> 28% of each run, Pallas kernels for 28% -> 29%
where the time goes in v9:
time: 189 us; the launch traced here: 188 us
  Pallas kernels  111 us (59%)
  matrix products  34.5 us (18%)
  local copies, waits for them, and re-layouts  16.1 us (9%)
  other arithmetic  14.3 us (8%)
  starting transfers between devices  10.9 us (6%)
    pallas_call x2, Pallas kernels, head_exchange(): pl.pallas_call(functools.partial(head_exchange_kernel, parts, plan, count...  56.3 us
    pallas_call x1, Pallas kernels, ctx_scan(): pl.pallas_call(functools.partial(ctx_scan_kernel, count), out_shape=jax.S...  54.7 us
    dot_general x29, matrix products, matmul(): return jnp.einsum(spec, left, right, precision=MATMUL_PRECISION)  31.5 us
    all_to_all x1, starting transfers between devices, on_device(): lax.all_to_all(gate_rows, 'head', split_axis=1, concat_axis=0, tiled=True)  6.04 us
    unnamed x35, local copies, waits for them, and re-layouts  5.68 us
    ppermute x1, starting transfers between devices, passed_along(): lax.ppermute(value, axis, [(source, source + steps) for source in range(l...  4.86 us
  transfers between devices with their start and end apart: 2, of which 0 were waited for; matrix products, arithmetic and copies ran while one was open for 28% of the time, Pallas kernels for 29%

profile of v9, /device:TPU:141, one launch (start us, length us, event | category | flops | bytes accessed | tf_op | source)
XLA Modules:
  0.0 188.0 jit_solution(8937213212905204779)
XLA Ops:
  0.0 0.9 copy.120
  1.0 0.9 copy.121
  1.9 0.9 maximum_bitcast_fusion.refs_3_
  2.7 37.4 %shard_map.100 = (bf16[1024,512]{1,0:T(8,128)(2,1)}, bf16[8,128,4]{2,1,0:T(8,128)(2,1)}) custom-call(bf16[128,1024]{1,0:T(8,128)(2,1)} %refs_0_.1, bf16[128,1024]{1,0:T(8,128)(2,1)} %refs_1_.1, bf16[128,2048]{1,0:T(8,128)(2,1)} %refs_2_.1, bf16[8,128,4]{2,1,0:T(8,128)(2,1)} %maximum_bitcast_fusion.refs_3_), custom_call_target="tpu_custom_call" | custom-call | tf_op jit(solution)/shard_map/pallas_call | solution.py:357
  40.2 0.7 slice.86
  40.9 4.9 %collective-permute-start = (bf16[3,512]{1,0:T(4,128)(2,1)S(1)}, bf16[3,512]{1,0:T(4,128)(2,1)S(1)}, u32[]{:S(2)}, u32[]{:S(2)}) collective-permute-start(bf16[3,512]{1,0:T(4,128)(2,1)S(1)} %slice.86), channel_id=1, source_target_pairs={{0,8},{8,16},{16,24},{24,32},{32,40},{40,48},{48,56},{56,64},{64,7... | collective-permute-start | bytes 9224 | tf_op jit(solution)/shard_map/ppermute | solution.py:25
  45.8 0.9 copy.168
  46.7 6.0 %all-to-all-start = ((bf16[128,8,256]{2,0,1:T(8,128)(2,1)}), bf16[128,8,256]{2,0,1:T(8,128)(2,1)}, u32[]{:S(2)}, u32[]{:S(2)}) async-start(bf16[128,8,256]{2,0,1:T(8,128)(2,1)} %bitcast.124), calls=%async_computation | async-start | bytes 1048576 | tf_op jit(solution)/shard_map/all_to_all | solution.py:435
  53.1 0.5 reduce_window_sum.11
  54.1 1.5 convert_element_type.42
  56.0 1.3 divide_multiply_fusion
  57.3 0.3 multiply_reduce_fusion.2
  57.7 1.1 divide_multiply_fusion.1
  58.8 1.3 broadcast_multiply_fusion
  60.2 1.0 fusion.95
  61.3 13.4 %while.18 = (s32[]{:T(128)}, f32[16,2,64,64]{2,3,1,0:T(8,128)S(1)}, f32[16,2,64,64]{3,2,1,0:T(8,128)S(1)}, s32[]{:T(128)}, s32[]{:T(128)}) while((s32[]{:T(128)}, f32[16,2,64,64]{2,3,1,0:T(8,128)S(1)}, f32[16,2,64,64]{3,2,1,0:T(8,128)S(1)}, s32[]{:T(128)}, s32[]{:T(128)}) %tuple.62), condition=%wide.region_4.5_spmd.clone.clone, body=%wide.region_3.4_spmd.clone.clone.sunk | while | flops 100941312 | bytes 4728181 | solution.py:50
  61.7 0.9 fusion.162
  62.6 0.6 convolution_bitcast_fusion.3
  63.2 0.3 sub.126
  63.9 0.9 fusion.162
  64.8 0.6 convolution_bitcast_fusion.3
  65.4 0.3 sub.126
  66.1 0.9 fusion.162
  67.1 0.6 convolution_bitcast_fusion.3
  67.7 0.3 sub.126
  68.3 0.9 fusion.162
  69.3 0.6 convolution_bitcast_fusion.3
  69.9 0.3 sub.126
  70.5 0.9 fusion.162
  71.5 0.6 convolution_bitcast_fusion.3
  72.7 0.9 fusion.162
  73.7 0.6 convolution_bitcast_fusion.3
  74.8 0.5 reshape_reshape.2
  75.3 0.3 bitcast_multiply_fusion.1
  75.7 0.9 copy-done.10
  76.5 1.1 fusion.31
  77.7 2.2 %fusion.73 = f32[16,2,128,128]{3,2,1,0:T(8,128)S(1)} fusion(f32[16,2,64,256]{3,2,1,0:T(8,128)S(1)} %fusion.31, f32[16,64,128]{2,1,0:T(8,128)S(1)} %bitcast.143, f32[16,2,64]{2,1,0:T(2,128)S(1)} %copy.125), kind=kOutput, calls=%fused_computation.90 | convolution fusion | flops 201588736 | bytes 3686400 | tf_op jit(solution)/shard_map/nhcd,nhce->nhde/dot_general | solution.py:29
  80.1 2.3 %multiply_subtract_fusion = f32[16,2,128,128]{3,2,1,0:T(8,128)S(1)} fusion(f32[128,128]{1,0:T(8,128)S(1)} %fusion.116, f32[16,2]{1,0:T(8,128)S(1)} %copy.124, f32[16,2,64,256]{3,2,1,0:T(8,128)S(1)} %fusion.31, f32[16,64,128]{2,1,0:T(8,128)S(1)} %bitcast.144, f32[16,2,64]{2,1,0:T(2,128)S(1)} %copy.125), kind=kOutput, calls=%fused_computation.80 | convolution fusion | flops 202637312 | bytes 3760128 | tf_op jit(solution)/shard_map/nhcd,nhce->nhde/dot_general | solution.py:29
  82.6 1.3 fusion.61
  84.1 1.2 fusion.21
  85.5 1.2 fusion.64
  86.9 1.2 fusion.36
  88.3 1.5 fusion.67
  89.9 1.2 fusion.40
  91.1 1.2 fusion.70
  92.3 1.7 slice.135
  94.0 0.3 copy-done.5
  94.5 1.2 fusion.44
  95.7 1.3 copy-done.4
  97.1 2.0 %convolution_multiply_fusion = f32[16,2,64,64]{3,2,1,0:T(8,128)} fusion(f32[16,2,64]{2,1,0:T(2,128)S(1)} %copy.128, f32[16,64,128]{2,1,0:T(8,128)S(1)} %bitcast.145, f32[16,64,128]{2,1,0:T(8,128)S(1)} %bitcast.148, pred[64,64]{1,0:T(8,128)(4,1)S(1)} %get-tuple-element.281), kind=kOutput, calls=%fused_computation.100 | convolution fusion | flops 101187584 | bytes 1585152 | tf_op jit(solution)/shard_map/nhid,nhjd->nhij/dot_general | solution.py:108
  99.1 0.7 pad_maximum_fusion.5.maps_ref
  99.8 54.7 %shard_map.101 = f32[2,128,128]{2,1,0:T(8,128)} custom-call(f32[2,2,128,128]{3,2,1,0:T(8,128)} %pad_maximum_fusion.5.maps_ref), custom_call_target="tpu_custom_call" | custom-call | tf_op jit(solution)/shard_map/pallas_call | solution.py:290
  154.6 2.0 %multiply_subtract_fusion.1 = f32[16,2,64,128]{3,2,1,0:T(8,128)S(1)} fusion(f32[16,2,64,64]{3,2,1,0:T(8,128)} %convolution_multiply_fusion, f32[16,2,64,256]{3,2,1,0:T(8,128)S(1)} %fusion.31, f32[16,64,128]{2,1,0:T(8,128)S(1)} %bitcast.149, f32[16,2,64]{2,1,0:T(2,128)S(1)} %copy.123), kind=kOutput, calls=%fused_computation.93 | convolution fusion | flops 101187584 | bytes 3162112 | tf_op jit(solution)/shard_map/nhij,nhjd->nhid/dot_general | solution.py:29
  156.6 1.1 fusion.22
  157.7 0.6 convolution_bitcast_fusion.1
  158.3 1.0 copy-done.2
  159.3 1.0 fusion.92
  160.5 0.7 fusion.133
  161.1 1.3 multiply_reduce_fusion
  162.7 0.8 copy.137
  163.5 1.2 div.135
  164.8 2.4 %fusion.98.refs_0_ = bf16[1024,256]{1,0:T(8,128)(2,1)} fusion(f32[128,8,2,128]{3,2,1,0:T(2,128)S(1)} %bitcast.152, f32[128,8,2,128]{3,2,1,0:T(2,128)S(1)} %bitcast.151, bf16[128,8,256]{2,0,1:T(8,128)(2,1)} %all-to-all-done, f32[256]{0:T(256)S(1)} %broadcast_bitcast_fusion), kind=kLoop, calls=%fused_computation.106 | loop fusion | flops 2359296 | bytes 3146752 | tf_op jit(solution)/shard_map/convert_element_type | solution.py:133
  167.2 18.9 %shard_map.102 = bf16[128,2048]{1,0:T(8,128)(2,1)} custom-call(bf16[1024,256]{1,0:T(8,128)(2,1)} %fusion.98.refs_0_), custom_call_target="tpu_custom_call" | custom-call | tf_op jit(solution)/shard_map/pallas_call | solution.py:357
  186.1 1.9 %copy.178 = bf16[128,2048]{1,0:T(8,128)(2,1)} copy(bf16[128,2048]{1,0:T(8,128)(2,1)} %shard_map.102) | data formatting | bytes 1048576
  (95 shorter events, 5.9 us)
Async XLA Ops:
  0.0 54.0 %copy-start = (f32[128]{0:T(128)S(1)}, f32[128]{0:T(128)}, u32[]{:S(2)}) copy-start(f32[128]{0:T(128)} %param.21) | copy-start | bytes 1540
  0.0 45.8 %copy-start.13 = (bf16[128,2048]{1,0:T(8,128)(2,1)S(1)}, bf16[128,2048]{1,0:T(8,128)(2,1)}, u32[]{:S(2)}) copy-start(bf16[128,2048]{1,0:T(8,128)(2,1)} %param.15) | copy-start | bytes 1572868
  1.9 50.9 %copy-start.14 = (bf16[4,256]{1,0:T(4,128)(2,1)S(1)}, bf16[4,256]{1,0:T(4,128)(2,1)}, u32[]{:S(2)}) copy-start(bf16[4,256]{1,0:T(4,128)(2,1)} %param.20) | copy-start | bytes 6148
  1.9 50.9 %copy-start.15 = (bf16[4,128]{1,0:T(4,128)(2,1)S(1)}, bf16[4,128]{1,0:T(4,128)(2,1)}, u32[]{:S(2)}) copy-start(bf16[4,128]{1,0:T(4,128)(2,1)} %param.19) | copy-start | bytes 3076
  1.9 50.9 %copy-start.16 = (bf16[4,128]{1,0:T(4,128)(2,1)S(1)}, bf16[4,128]{1,0:T(4,128)(2,1)}, u32[]{:S(2)}) copy-start(bf16[4,128]{1,0:T(4,128)(2,1)} %param.18) | copy-start | bytes 3076
  40.2 12.6 %copy-start.11 = (bf16[8,128,4]{2,1,0:T(8,128)(2,1)S(1)}, bf16[8,128,4]{2,1,0:T(8,128)(2,1)}, u32[]{:S(2)}) copy-start(bf16[8,128,4]{2,1,0:T(8,128)(2,1)} %get-tuple-element.209) | copy-start | bytes 24580
  40.9 15.1 %collective-permute-start = (bf16[3,512]{1,0:T(4,128)(2,1)S(1)}, bf16[3,512]{1,0:T(4,128)(2,1)S(1)}, u32[]{:S(2)}, u32[]{:S(2)}) collective-permute-start(bf16[3,512]{1,0:T(4,128)(2,1)S(1)} %slice.86), channel_id=1, source_target_pairs={{0,8},{8,16},{16,24},{24,32},{32,40},{40,48},{48,56},{56,64},{64,7... | collective-permute-start | bytes 9224 | tf_op jit(solution)/shard_map/ppermute | solution.py:25
  46.7 116.9 %all-to-all-start = ((bf16[128,8,256]{2,0,1:T(8,128)(2,1)}), bf16[128,8,256]{2,0,1:T(8,128)(2,1)}, u32[]{:S(2)}, u32[]{:S(2)}) async-start(bf16[128,8,256]{2,0,1:T(8,128)(2,1)} %bitcast.124), calls=%async_computation | async-start | bytes 1048576 | tf_op jit(solution)/shard_map/all_to_all | solution.py:435
  57.3 1.5 copy-start.3
  58.8 2.3 %copy-start.6 = (f32[1024,128]{1,0:T(8,128)}, f32[1024,128]{1,0:T(8,128)S(1)}, u32[]{:S(2)}) copy-start(f32[1024,128]{1,0:T(8,128)S(1)} %get-tuple-element.267) | copy-start | bytes 1572868
  61.3 13.5 %slice-start = ((f32[1024,512]{1,0:T(8,128)}), f32[1024,256]{1,0:T(8,128)S(1)}, s32[]{:S(2)}) async-start(f32[1024,512]{1,0:T(8,128)} %copy-done.3), calls=%async_computation.1 | async-start | bytes 2097152 | tf_op jit(solution)/shard_map/slice | solution.py:450
  75.3 1.2 copy-start.10
  76.5 1.1 copy-start.7
  92.3 2.0 %copy-start.5 = (f32[16,2,128,128]{3,2,1,0:T(8,128)}, f32[16,2,128,128]{3,2,1,0:T(8,128)S(1)}, u32[]{:S(2)}) copy-start(f32[16,2,128,128]{3,2,1,0:T(8,128)S(1)} %fusion.70) | copy-start | bytes 6291460
  95.7 1.3 copy-start.4
  95.7 1.4 copy-start.8
  97.0 2.1 %slice-start.3 = ((f32[16,2,128,128]{3,2,1,0:T(8,128)}), f32[1,2,128,128]{3,2,1,0:T(8,128)S(1)}, s32[]{:S(2)}) async-start(f32[16,2,128,128]{3,2,1,0:T(8,128)} %copy-done.5), calls=%async_computation.4 | async-start | bytes 262144 | tf_op jit(solution)/shard_map/slice | solution.py:485
  97.0 2.1 %slice-start.1 = ((f32[16,2,128,128]{3,2,1,0:T(8,128)}), f32[1,2,128,128]{3,2,1,0:T(8,128)S(1)}, s32[]{:S(2)}) async-start(f32[16,2,128,128]{3,2,1,0:T(8,128)} %copy-done.4), calls=%async_computation.2 | async-start | bytes 262144 | tf_op jit(solution)/shard_map/slice | solution.py:485
  154.5 2.1 %slice-start.2 = ((f32[16,2,128,128]{3,2,1,0:T(8,128)}), f32[15,2,128,128]{3,2,1,0:T(8,128)S(1)}, s32[]{:S(2)}) async-start(f32[16,2,128,128]{3,2,1,0:T(8,128)} %copy-done.4), calls=%async_computation.3 | async-start | bytes 3932160 | tf_op jit(solution)/shard_map/slice | solution.py:477
  156.6 1.1 copy-start.12
  157.7 1.5 copy-start.2
  159.3 1.2 copy-start.9
  164.8 23.2 %copy-start.1 = (f32[128]{0:T(128)S(1)}, f32[128]{0:T(128)}, u32[]{:S(2)}) copy-start(f32[128]{0:T(128)} %param.21) | copy-start | bytes 1540

commit v10 on v9

--- a/solution.py
+++ b/solution.py
@@ -437,7 +437,7 @@
     count_rows = joined.shape[0]
     tail_rows = passed_along(joined[count_rows - (kernel_width - 1) :], "ctx", 1)
     weights_all = jnp.concatenate([conv_query, conv_key, conv_value], axis=1).astype(jnp.float32)
-    mixed = causal_conv(joined.astype(jnp.float32), tail_rows.astype(jnp.float32), weights_all)
+    mixed = causal_conv(joined, tail_rows, weights_all)
     key_width = query_rows.shape[1] // parts
     head_keys = key_width // DK
     per_key = HV // HK

time: 189 us -> 187 us (0.989)
    unnamed x35 -> x37, local copies, waits for them, and re-layouts: 5.68 us -> 5.69 us
  transfers between devices with their start and end apart: 2 -> 2, of which waited for: 0 -> 0; matrix products, arithmetic and copies ran while one was open for 28% -> 27% of each run, Pallas kernels for 29% -> 29%
where the time goes in v10:
time: 187 us
  Pallas kernels  111 us (59%)
  matrix products  34.5 us (18%)
  local copies, waits for them, and re-layouts  16.1 us (9%)
  other arithmetic  13 us (7%)
  starting transfers between devices  11 us (6%)
    pallas_call x2, Pallas kernels, head_exchange(): pl.pallas_call(functools.partial(head_exchange_kernel, parts, plan, count...  57.2 us
    pallas_call x1, Pallas kernels, ctx_scan(): pl.pallas_call(functools.partial(ctx_scan_kernel, count), out_shape=jax.S...  53.8 us
    dot_general x29, matrix products, matmul(): return jnp.einsum(spec, left, right, precision=MATMUL_PRECISION)  31.5 us
    all_to_all x1, starting transfers between devices, on_device(): lax.all_to_all(gate_rows, 'head', split_axis=1, concat_axis=0, tiled=True)  6.17 us
    unnamed x37, local copies, waits for them, and re-layouts  5.69 us
    ppermute x1, starting transfers between devices, passed_along(): lax.ppermute(value, axis, [(source, source + steps) for source in range(l...  4.86 us
  transfers between devices with their start and end apart: 2, of which 0 were waited for; matrix products, arithmetic and copies ran while one was open for 27% of the time, Pallas kernels for 29%

profile of v10, /device:TPU:141, one launch (start us, length us, event | category | flops | bytes accessed | tf_op | source)
XLA Modules:
  0.0 186.7 jit_solution(14286303021664543397)
XLA Ops:
  0.0 0.9 copy.120
  1.0 0.9 copy.121
  1.9 0.9 maximum_bitcast_fusion.refs_3_
  2.7 37.4 %shard_map.100 = (bf16[1024,512]{1,0:T(8,128)(2,1)}, bf16[8,128,4]{2,1,0:T(8,128)(2,1)}) custom-call(bf16[128,1024]{1,0:T(8,128)(2,1)} %refs_0_.1, bf16[128,1024]{1,0:T(8,128)(2,1)} %refs_1_.1, bf16[128,2048]{1,0:T(8,128)(2,1)} %refs_2_.1, bf16[8,128,4]{2,1,0:T(8,128)(2,1)} %maximum_bitcast_fusion.refs_3_), custom_call_target="tpu_custom_call" | custom-call | tf_op jit(solution)/shard_map/pallas_call | solution.py:357
  40.2 0.7 slice.86
  40.9 4.9 %collective-permute-start = (bf16[3,512]{1,0:T(4,128)(2,1)S(1)}, bf16[3,512]{1,0:T(4,128)(2,1)S(1)}, u32[]{:S(2)}, u32[]{:S(2)}) collective-permute-start(bf16[3,512]{1,0:T(4,128)(2,1)S(1)} %slice.86), channel_id=1, source_target_pairs={{0,8},{8,16},{16,24},{24,32},{32,40},{40,48},{48,56},{56,64},{64,7... | collective-permute-start | bytes 9224 | tf_op jit(solution)/shard_map/ppermute | solution.py:25
  45.8 0.9 copy.168
  46.7 6.2 %all-to-all-start = ((bf16[128,8,256]{2,0,1:T(8,128)(2,1)}), bf16[128,8,256]{2,0,1:T(8,128)(2,1)}, u32[]{:S(2)}, u32[]{:S(2)}) async-start(bf16[128,8,256]{2,0,1:T(8,128)(2,1)} %bitcast.124), calls=%async_computation | async-start | bytes 1048576 | tf_op jit(solution)/shard_map/all_to_all | solution.py:435
  53.3 0.5 reduce_window_sum.11
  54.6 1.4 divide_multiply_fusion
  56.1 0.3 multiply_reduce_fusion.2
  56.5 1.1 divide_multiply_fusion.1
  57.6 1.3 broadcast_multiply_fusion
  58.9 1.0 fusion.87
  60.0 13.4 %while.18 = (s32[]{:T(128)}, f32[16,2,64,64]{2,3,1,0:T(8,128)S(1)}, f32[16,2,64,64]{3,2,1,0:T(8,128)S(1)}, s32[]{:T(128)}, s32[]{:T(128)}) while((s32[]{:T(128)}, f32[16,2,64,64]{2,3,1,0:T(8,128)S(1)}, f32[16,2,64,64]{3,2,1,0:T(8,128)S(1)}, s32[]{:T(128)}, s32[]{:T(128)}) %tuple.62), condition=%wide.region_4.5_spmd.clone.clone, body=%wide.region_3.4_spmd.clone.clone.sunk | while | flops 100941312 | bytes 4728181 | solution.py:50
  60.4 0.9 fusion.156
  61.4 0.6 convolution_bitcast_fusion.3
  62.0 0.3 sub.126
  62.6 0.9 fusion.156
  63.6 0.6 convolution_bitcast_fusion.3
  64.2 0.3 sub.126
  64.8 0.9 fusion.156
  65.8 0.6 convolution_bitcast_fusion.3
  66.4 0.3 sub.126
  67.0 0.9 fusion.156
  68.0 0.6 convolution_bitcast_fusion.3
  68.6 0.3 sub.126
  69.3 0.9 fusion.156
  70.2 0.6 convolution_bitcast_fusion.3
  70.8 0.3 sub.126
  71.5 0.9 fusion.156
  72.4 0.6 convolution_bitcast_fusion.3
  73.5 0.5 reshape_reshape.2
  74.1 0.3 bitcast_multiply_fusion.1
  74.4 0.9 copy-done.10
  75.3 1.1 fusion.23
  76.4 2.2 %fusion.65 = f32[16,2,128,128]{3,2,1,0:T(8,128)S(1)} fusion(f32[16,2,64,256]{3,2,1,0:T(8,128)S(1)} %fusion.23, f32[16,64,128]{2,1,0:T(8,128)S(1)} %bitcast.143, f32[16,2,64]{2,1,0:T(2,128)S(1)} %copy.125), kind=kOutput, calls=%fused_computation.79 | convolution fusion | flops 201588736 | bytes 3686400 | tf_op jit(solution)/shard_map/nhcd,nhce->nhde/dot_general | solution.py:29
  78.8 2.3 %multiply_subtract_fusion = f32[16,2,128,128]{3,2,1,0:T(8,128)S(1)} fusion(f32[128,128]{1,0:T(8,128)S(1)} %fusion.110, f32[16,2]{1,0:T(8,128)S(1)} %copy.124, f32[16,2,64,256]{3,2,1,0:T(8,128)S(1)} %fusion.23, f32[16,64,128]{2,1,0:T(8,128)S(1)} %bitcast.144, f32[16,2,64]{2,1,0:T(2,128)S(1)} %copy.125), kind=kOutput, calls=%fused_computation.69 | convolution fusion | flops 202637312 | bytes 3760128 | tf_op jit(solution)/shard_map/nhcd,nhce->nhde/dot_general | solution.py:29
  81.3 1.3 fusion.53
  82.8 1.2 fusion.21
  84.2 1.2 fusion.56
  85.6 1.2 fusion.28
  87.0 1.5 fusion.59
  88.6 1.2 fusion.32
  89.9 1.2 fusion.62
  91.0 1.7 slice.135
  92.7 0.3 copy-done.5
  93.2 1.2 fusion.36
  94.4 1.3 copy-done.4
  95.9 2.0 %convolution_multiply_fusion = f32[16,2,64,64]{3,2,1,0:T(8,128)} fusion(f32[16,2,64]{2,1,0:T(2,128)S(1)} %copy.128, f32[16,64,128]{2,1,0:T(8,128)S(1)} %bitcast.145, f32[16,64,128]{2,1,0:T(8,128)S(1)} %bitcast.148, pred[64,64]{1,0:T(8,128)(4,1)S(1)} %get-tuple-element.281), kind=kOutput, calls=%fused_computation.91 | convolution fusion | flops 101187584 | bytes 1585152 | tf_op jit(solution)/shard_map/nhid,nhjd->nhij/dot_general | solution.py:108
  97.8 0.7 pad_maximum_fusion.5.maps_ref
  98.5 53.8 %shard_map.101 = f32[2,128,128]{2,1,0:T(8,128)} custom-call(f32[2,2,128,128]{3,2,1,0:T(8,128)} %pad_maximum_fusion.5.maps_ref), custom_call_target="tpu_custom_call" | custom-call | tf_op jit(solution)/shard_map/pallas_call | solution.py:290
  152.4 2.0 %multiply_subtract_fusion.1 = f32[16,2,64,128]{3,2,1,0:T(8,128)S(1)} fusion(f32[16,2,64,64]{3,2,1,0:T(8,128)} %convolution_multiply_fusion, f32[16,2,64,256]{3,2,1,0:T(8,128)S(1)} %fusion.23, f32[16,64,128]{2,1,0:T(8,128)S(1)} %bitcast.149, f32[16,2,64]{2,1,0:T(2,128)S(1)} %copy.123), kind=kOutput, calls=%fused_computation.82 | convolution fusion | flops 101187584 | bytes 3162112 | tf_op jit(solution)/shard_map/nhij,nhjd->nhid/dot_general | solution.py:29
  154.4 1.1 fusion.22
  155.5 0.6 convolution_bitcast_fusion.1
  156.1 1.0 copy-done.2
  157.1 1.0 fusion.84
  158.3 0.7 fusion.127
  159.0 1.3 multiply_reduce_fusion
  160.5 0.8 copy.137
  161.4 1.2 div.135
  162.6 2.4 %fusion.92.refs_0_ = bf16[1024,256]{1,0:T(8,128)(2,1)} fusion(f32[128,8,2,128]{3,2,1,0:T(2,128)S(1)} %bitcast.152, f32[128,8,2,128]{3,2,1,0:T(2,128)S(1)} %bitcast.151, bf16[128,8,256]{2,0,1:T(8,128)(2,1)} %all-to-all-done, f32[256]{0:T(256)S(1)} %broadcast_bitcast_fusion), kind=kLoop, calls=%fused_computation.99 | loop fusion | flops 2359296 | bytes 3146752 | tf_op jit(solution)/shard_map/convert_element_type | solution.py:133
  165.0 19.8 %shard_map.102 = bf16[128,2048]{1,0:T(8,128)(2,1)} custom-call(bf16[1024,256]{1,0:T(8,128)(2,1)} %fusion.92.refs_0_), custom_call_target="tpu_custom_call" | custom-call | tf_op jit(solution)/shard_map/pallas_call | solution.py:357
  184.8 1.9 %copy.178 = bf16[128,2048]{1,0:T(8,128)(2,1)} copy(bf16[128,2048]{1,0:T(8,128)(2,1)} %shard_map.102) | data formatting | bytes 1048576
  (95 shorter events, 5.7 us)
Async XLA Ops:
  0.0 54.1 %copy-start = (f32[128]{0:T(128)S(1)}, f32[128]{0:T(128)}, u32[]{:S(2)}) copy-start(f32[128]{0:T(128)} %param.21) | copy-start | bytes 1540
  0.0 45.8 %copy-start.14 = (bf16[128,2048]{1,0:T(8,128)(2,1)S(1)}, bf16[128,2048]{1,0:T(8,128)(2,1)}, u32[]{:S(2)}) copy-start(bf16[128,2048]{1,0:T(8,128)(2,1)} %param.15) | copy-start | bytes 1572868
  1.9 51.0 %copy-start.15 = (bf16[4,256]{1,0:T(4,128)(2,1)S(1)}, bf16[4,256]{1,0:T(4,128)(2,1)}, u32[]{:S(2)}) copy-start(bf16[4,256]{1,0:T(4,128)(2,1)} %param.20) | copy-start | bytes 6148
  1.9 51.0 %copy-start.16 = (bf16[4,128]{1,0:T(4,128)(2,1)S(1)}, bf16[4,128]{1,0:T(4,128)(2,1)}, u32[]{:S(2)}) copy-start(bf16[4,128]{1,0:T(4,128)(2,1)} %param.19) | copy-start | bytes 3076
  1.9 51.0 %copy-start.17 = (bf16[4,128]{1,0:T(4,128)(2,1)S(1)}, bf16[4,128]{1,0:T(4,128)(2,1)}, u32[]{:S(2)}) copy-start(bf16[4,128]{1,0:T(4,128)(2,1)} %param.18) | copy-start | bytes 3076
  40.2 12.8 %copy-start.12 = (bf16[8,128,4]{2,1,0:T(8,128)(2,1)S(1)}, bf16[8,128,4]{2,1,0:T(8,128)(2,1)}, u32[]{:S(2)}) copy-start(bf16[8,128,4]{2,1,0:T(8,128)(2,1)} %get-tuple-element.209) | copy-start | bytes 24580
  40.9 13.7 %collective-permute-start = (bf16[3,512]{1,0:T(4,128)(2,1)S(1)}, bf16[3,512]{1,0:T(4,128)(2,1)S(1)}, u32[]{:S(2)}, u32[]{:S(2)}) collective-permute-start(bf16[3,512]{1,0:T(4,128)(2,1)S(1)} %slice.86), channel_id=1, source_target_pairs={{0,8},{8,16},{16,24},{24,32},{32,40},{40,48},{48,56},{56,64},{64,7... | collective-permute-start | bytes 9224 | tf_op jit(solution)/shard_map/ppermute | solution.py:25
  46.7 8.0 %copy-start.11 = (bf16[1024,512]{1,0:T(8,128)(2,1)S(1)}, bf16[1024,512]{1,0:T(8,128)(2,1)}, u32[]{:S(2)}) copy-start(bf16[1024,512]{1,0:T(8,128)(2,1)} %get-tuple-element.210) | copy-start | bytes 3145732
  46.7 114.7 %all-to-all-start = ((bf16[128,8,256]{2,0,1:T(8,128)(2,1)}), bf16[128,8,256]{2,0,1:T(8,128)(2,1)}, u32[]{:S(2)}, u32[]{:S(2)}) async-start(bf16[128,8,256]{2,0,1:T(8,128)(2,1)} %bitcast.124), calls=%async_computation | async-start | bytes 1048576 | tf_op jit(solution)/shard_map/all_to_all | solution.py:435
  56.1 1.5 copy-start.3
  57.6 2.3 %copy-start.6 = (f32[1024,128]{1,0:T(8,128)}, f32[1024,128]{1,0:T(8,128)S(1)}, u32[]{:S(2)}) copy-start(f32[1024,128]{1,0:T(8,128)S(1)} %get-tuple-element.267) | copy-start | bytes 1572868
  60.0 13.5 %slice-start = ((f32[1024,512]{1,0:T(8,128)}), f32[1024,256]{1,0:T(8,128)S(1)}, s32[]{:S(2)}) async-start(f32[1024,512]{1,0:T(8,128)} %copy-done.3), calls=%async_computation.1 | async-start | bytes 2097152 | tf_op jit(solution)/shard_map/slice | solution.py:450
  74.0 1.2 copy-start.10
  75.3 1.1 copy-start.7
  91.0 2.0 %copy-start.5 = (f32[16,2,128,128]{3,2,1,0:T(8,128)}, f32[16,2,128,128]{3,2,1,0:T(8,128)S(1)}, u32[]{:S(2)}) copy-start(f32[16,2,128,128]{3,2,1,0:T(8,128)S(1)} %fusion.62) | copy-start | bytes 6291460
  94.4 1.3 copy-start.4
  94.4 1.4 copy-start.8
  95.8 2.1 %slice-start.3 = ((f32[16,2,128,128]{3,2,1,0:T(8,128)}), f32[1,2,128,128]{3,2,1,0:T(8,128)S(1)}, s32[]{:S(2)}) async-start(f32[16,2,128,128]{3,2,1,0:T(8,128)} %copy-done.5), calls=%async_computation.4 | async-start | bytes 262144 | tf_op jit(solution)/shard_map/slice | solution.py:485
  95.8 2.1 %slice-start.1 = ((f32[16,2,128,128]{3,2,1,0:T(8,128)}), f32[1,2,128,128]{3,2,1,0:T(8,128)S(1)}, s32[]{:S(2)}) async-start(f32[16,2,128,128]{3,2,1,0:T(8,128)} %copy-done.4), calls=%async_computation.2 | async-start | bytes 262144 | tf_op jit(solution)/shard_map/slice | solution.py:485
  152.4 2.1 %slice-start.2 = ((f32[16,2,128,128]{3,2,1,0:T(8,128)}), f32[15,2,128,128]{3,2,1,0:T(8,128)S(1)}, s32[]{:S(2)}) async-start(f32[16,2,128,128]{3,2,1,0:T(8,128)} %copy-done.4), calls=%async_computation.3 | async-start | bytes 3932160 | tf_op jit(solution)/shard_map/slice | solution.py:477
  154.4 1.1 copy-start.13
  155.5 1.5 copy-start.2
  157.1 1.2 copy-start.9
  162.6 24.1 %copy-start.1 = (f32[128]{0:T(128)S(1)}, f32[128]{0:T(128)}, u32[]{:S(2)}) copy-start(f32[128]{0:T(128)} %param.21) | copy-start | bytes 1540

commit v11 on v10

--- a/solution.py
+++ b/solution.py
@@ -44,7 +44,7 @@
         )
         lower = jnp.where(pick, strict, 0.0)
         update = matmul("...ij,...jk->...ik", inverse, matmul("...ij,...jk->...ik", lower, inverse))
-        return inverse - lax.optimization_barrier(update)
+        return inverse - update
 
     start = jnp.broadcast_to(jnp.eye(size, dtype=strict.dtype), strict.shape)
     return lax.fori_loop(0, levels, level, start)

time: 187 us -> 187 us (level)
  no operation moved by 1% of the time
where the time goes in v11:
time: 187 us; the launch traced here: 186 us
  Pallas kernels  111 us (59%)
  matrix products  35 us (19%)
  local copies, waits for them, and re-layouts  16.5 us (9%)
  other arithmetic  11.3 us (6%)
  starting transfers between devices  11 us (6%)
    pallas_call x2, Pallas kernels, head_exchange(): pl.pallas_call(functools.partial(head_exchange_kernel, parts, plan, count...  57 us
    pallas_call x1, Pallas kernels, ctx_scan(): pl.pallas_call(functools.partial(ctx_scan_kernel, count), out_shape=jax.S...  54 us
    dot_general x29, matrix products, matmul(): return jnp.einsum(spec, left, right, precision=MATMUL_PRECISION)  32.1 us
    all_to_all x1, starting transfers between devices, on_device(): lax.all_to_all(gate_rows, 'head', split_axis=1, concat_axis=0, tiled=True)  6.17 us
    unnamed x37, local copies, waits for them, and re-layouts  5.68 us
    ppermute x1, starting transfers between devices, passed_along(): lax.ppermute(value, axis, [(source, source + steps) for source in range(l...  4.86 us
  transfers between devices with their start and end apart: 2, of which 0 were waited for; matrix products, arithmetic and copies ran while one was open for 27% of the time, Pallas kernels for 29%

profile of v11, /device:TPU:141, one launch (start us, length us, event | category | flops | bytes accessed | tf_op | source)
XLA Modules:
  0.0 186.0 jit_solution(1404436381590595970)
XLA Ops:
  0.0 0.9 copy.120
  1.0 0.9 copy.121
  1.9 0.9 maximum_bitcast_fusion.refs_3_
  2.7 37.4 %shard_map.100 = (bf16[1024,512]{1,0:T(8,128)(2,1)}, bf16[8,128,4]{2,1,0:T(8,128)(2,1)}) custom-call(bf16[128,1024]{1,0:T(8,128)(2,1)} %refs_0_.1, bf16[128,1024]{1,0:T(8,128)(2,1)} %refs_1_.1, bf16[128,2048]{1,0:T(8,128)(2,1)} %refs_2_.1, bf16[8,128,4]{2,1,0:T(8,128)(2,1)} %maximum_bitcast_fusion.refs_3_), custom_call_target="tpu_custom_call" | custom-call | tf_op jit(solution)/shard_map/pallas_call | solution.py:357
  40.2 0.7 slice.86
  40.9 4.9 %collective-permute-start = (bf16[3,512]{1,0:T(4,128)(2,1)S(1)}, bf16[3,512]{1,0:T(4,128)(2,1)S(1)}, u32[]{:S(2)}, u32[]{:S(2)}) collective-permute-start(bf16[3,512]{1,0:T(4,128)(2,1)S(1)} %slice.86), channel_id=1, source_target_pairs={{0,8},{8,16},{16,24},{24,32},{32,40},{40,48},{48,56},{56,64},{64,7... | collective-permute-start | bytes 9224 | tf_op jit(solution)/shard_map/ppermute | solution.py:25
  45.8 0.9 copy.168
  46.7 6.2 %all-to-all-start = ((bf16[128,8,256]{2,0,1:T(8,128)(2,1)}), bf16[128,8,256]{2,0,1:T(8,128)(2,1)}, u32[]{:S(2)}, u32[]{:S(2)}) async-start(bf16[128,8,256]{2,0,1:T(8,128)(2,1)} %bitcast.126), calls=%async_computation | async-start | bytes 1048576 | tf_op jit(solution)/shard_map/all_to_all | solution.py:435
  53.1 0.2 copy.165
  53.3 0.5 reduce_window_sum.11
  53.9 0.2 copy.166
  54.3 0.2 copy.127
  54.6 1.4 divide_multiply_fusion
  56.1 0.3 multiply_reduce_fusion.2
  56.5 1.1 divide_multiply_fusion.1
  57.6 1.3 broadcast_multiply_fusion
  58.9 1.0 fusion.88
  60.0 12.8 %while.18 = (s32[]{:T(128)}, f32[16,2,64,64]{2,3,1,0:T(8,128)S(1)}, f32[16,2,64,64]{3,2,1,0:T(8,128)S(1)}, s32[]{:T(128)}, s32[]{:T(128)}) while((s32[]{:T(128)}, f32[16,2,64,64]{2,3,1,0:T(8,128)S(1)}, f32[16,2,64,64]{3,2,1,0:T(8,128)S(1)}, s32[]{:T(128)}, s32[]{:T(128)}) %tuple.62), condition=%wide.region_4.5_spmd.clone.clone, body=%wide.region_3.4_spmd.clone.clone.sunk | while | flops 100941312 | bytes 4203893 | solution.py:50
  60.5 1.0 fusion.158
  61.5 0.7 fusion.159
  62.6 1.0 fusion.158
  63.6 0.7 fusion.159
  64.7 1.0 fusion.158
  65.7 0.7 fusion.159
  66.8 1.0 fusion.158
  67.8 0.7 fusion.159
  68.9 1.0 fusion.158
  69.8 0.7 fusion.159
  71.0 1.0 fusion.158
  71.9 0.7 fusion.159
  72.8 0.5 reshape_reshape.2
  73.4 0.3 bitcast_multiply_fusion.1
  73.7 0.9 copy-done.10
  74.6 1.1 fusion.24
  75.7 2.2 %fusion.66 = f32[16,2,128,128]{3,2,1,0:T(8,128)S(1)} fusion(f32[16,2,64,256]{3,2,1,0:T(8,128)S(1)} %fusion.24, f32[16,64,128]{2,1,0:T(8,128)S(1)} %bitcast.145, f32[16,2,64]{2,1,0:T(2,128)S(1)} %copy.125), kind=kOutput, calls=%fused_computation.80 | convolution fusion | flops 201588736 | bytes 3686400 | tf_op jit(solution)/shard_map/nhcd,nhce->nhde/dot_general | solution.py:29
  77.9 0.2 slice.131
  78.1 2.3 %multiply_subtract_fusion = f32[16,2,128,128]{3,2,1,0:T(8,128)S(1)} fusion(f32[128,128]{1,0:T(8,128)S(1)} %fusion.111, f32[16,2]{1,0:T(8,128)S(1)} %copy.124, f32[16,2,64,256]{3,2,1,0:T(8,128)S(1)} %fusion.24, f32[16,64,128]{2,1,0:T(8,128)S(1)} %bitcast.146, f32[16,2,64]{2,1,0:T(2,128)S(1)} %copy.125), kind=kOutput, calls=%fused_computation.70 | convolution fusion | flops 202637312 | bytes 3760128 | tf_op jit(solution)/shard_map/nhcd,nhce->nhde/dot_general | solution.py:29
  80.6 1.3 fusion.54
  82.1 1.2 fusion.22
  83.6 1.2 fusion.57
  85.0 1.2 fusion.29
  86.3 1.5 fusion.60
  88.0 1.2 fusion.33
  89.2 1.2 fusion.63
  90.4 1.7 slice.135
  92.0 0.3 copy-done.5
  92.5 1.2 fusion.37
  93.8 1.3 copy-done.4
  95.2 2.0 %convolution_multiply_fusion = f32[16,2,64,64]{3,2,1,0:T(8,128)} fusion(f32[16,2,64]{2,1,0:T(2,128)S(1)} %copy.128, f32[16,64,128]{2,1,0:T(8,128)S(1)} %bitcast.147, f32[16,64,128]{2,1,0:T(8,128)S(1)} %bitcast.150, pred[64,64]{1,0:T(8,128)(4,1)S(1)} %get-tuple-element.281), kind=kOutput, calls=%fused_computation.92 | convolution fusion | flops 101187584 | bytes 1585152 | tf_op jit(solution)/shard_map/nhid,nhjd->nhij/dot_general | solution.py:108
  97.1 0.7 pad_maximum_fusion.5.maps_ref
  97.9 54.0 %shard_map.101 = f32[2,128,128]{2,1,0:T(8,128)} custom-call(f32[2,2,128,128]{3,2,1,0:T(8,128)} %pad_maximum_fusion.5.maps_ref), custom_call_target="tpu_custom_call" | custom-call | tf_op jit(solution)/shard_map/pallas_call | solution.py:290
  151.9 2.0 %multiply_subtract_fusion.1 = f32[16,2,64,128]{3,2,1,0:T(8,128)S(1)} fusion(f32[16,2,64,64]{3,2,1,0:T(8,128)} %convolution_multiply_fusion, f32[16,2,64,256]{3,2,1,0:T(8,128)S(1)} %fusion.24, f32[16,64,128]{2,1,0:T(8,128)S(1)} %bitcast.151, f32[16,2,64]{2,1,0:T(2,128)S(1)} %copy.123), kind=kOutput, calls=%fused_computation.83 | convolution fusion | flops 101187584 | bytes 3162112 | tf_op jit(solution)/shard_map/nhij,nhjd->nhid/dot_general | solution.py:29
  154.0 1.1 fusion.23
  155.1 0.6 convolution_bitcast_fusion.1
  155.7 0.9 copy-done.2
  156.6 1.0 fusion.85
  157.8 0.7 fusion.128
  158.5 1.3 multiply_reduce_fusion
  159.8 0.2 copy.148
  160.1 0.8 copy.137
  160.9 1.2 div.135
  162.2 2.4 %fusion.93.refs_0_ = bf16[1024,256]{1,0:T(8,128)(2,1)} fusion(f32[128,8,2,128]{3,2,1,0:T(2,128)S(1)} %bitcast.154, f32[128,8,2,128]{3,2,1,0:T(2,128)S(1)} %bitcast.153, bf16[128,8,256]{2,0,1:T(8,128)(2,1)} %all-to-all-done, f32[256]{0:T(256)S(1)} %broadcast_bitcast_fusion), kind=kLoop, calls=%fused_computation.100 | loop fusion | flops 2359296 | bytes 3146752 | tf_op jit(solution)/shard_map/convert_element_type | solution.py:133
  164.5 19.6 %shard_map.102 = bf16[128,2048]{1,0:T(8,128)(2,1)} custom-call(bf16[1024,256]{1,0:T(8,128)(2,1)} %fusion.93.refs_0_), custom_call_target="tpu_custom_call" | custom-call | tf_op jit(solution)/shard_map/pallas_call | solution.py:357
  184.1 1.9 %copy.180 = bf16[128,2048]{1,0:T(8,128)(2,1)} copy(bf16[128,2048]{1,0:T(8,128)(2,1)} %shard_map.102) | data formatting | bytes 1048576
  (95 shorter events, 4.8 us)
Async XLA Ops:
  0.0 54.1 %copy-start = (f32[128]{0:T(128)S(1)}, f32[128]{0:T(128)}, u32[]{:S(2)}) copy-start(f32[128]{0:T(128)} %param.21) | copy-start | bytes 1540
  0.0 45.8 %copy-start.14 = (bf16[128,2048]{1,0:T(8,128)(2,1)S(1)}, bf16[128,2048]{1,0:T(8,128)(2,1)}, u32[]{:S(2)}) copy-start(bf16[128,2048]{1,0:T(8,128)(2,1)} %param.15) | copy-start | bytes 1572868
  1.9 51.0 %copy-start.15 = (bf16[4,256]{1,0:T(4,128)(2,1)S(1)}, bf16[4,256]{1,0:T(4,128)(2,1)}, u32[]{:S(2)}) copy-start(bf16[4,256]{1,0:T(4,128)(2,1)} %param.20) | copy-start | bytes 6148
  1.9 51.0 %copy-start.16 = (bf16[4,128]{1,0:T(4,128)(2,1)S(1)}, bf16[4,128]{1,0:T(4,128)(2,1)}, u32[]{:S(2)}) copy-start(bf16[4,128]{1,0:T(4,128)(2,1)} %param.19) | copy-start | bytes 3076
  1.9 51.0 %copy-start.17 = (bf16[4,128]{1,0:T(4,128)(2,1)S(1)}, bf16[4,128]{1,0:T(4,128)(2,1)}, u32[]{:S(2)}) copy-start(bf16[4,128]{1,0:T(4,128)(2,1)} %param.18) | copy-start | bytes 3076
  40.2 12.8 %copy-start.12 = (bf16[8,128,4]{2,1,0:T(8,128)(2,1)S(1)}, bf16[8,128,4]{2,1,0:T(8,128)(2,1)}, u32[]{:S(2)}) copy-start(bf16[8,128,4]{2,1,0:T(8,128)(2,1)} %get-tuple-element.209) | copy-start | bytes 24580
  40.9 13.7 %collective-permute-start = (bf16[3,512]{1,0:T(4,128)(2,1)S(1)}, bf16[3,512]{1,0:T(4,128)(2,1)S(1)}, u32[]{:S(2)}, u32[]{:S(2)}) collective-permute-start(bf16[3,512]{1,0:T(4,128)(2,1)S(1)} %slice.86), channel_id=1, source_target_pairs={{0,8},{8,16},{16,24},{24,32},{32,40},{40,48},{48,56},{56,64},{64,7... | collective-permute-start | bytes 9224 | tf_op jit(solution)/shard_map/ppermute | solution.py:25
  46.7 8.0 %copy-start.11 = (bf16[1024,512]{1,0:T(8,128)(2,1)S(1)}, bf16[1024,512]{1,0:T(8,128)(2,1)}, u32[]{:S(2)}) copy-start(bf16[1024,512]{1,0:T(8,128)(2,1)} %get-tuple-element.210) | copy-start | bytes 3145732
  46.7 114.2 %all-to-all-start = ((bf16[128,8,256]{2,0,1:T(8,128)(2,1)}), bf16[128,8,256]{2,0,1:T(8,128)(2,1)}, u32[]{:S(2)}, u32[]{:S(2)}) async-start(bf16[128,8,256]{2,0,1:T(8,128)(2,1)} %bitcast.126), calls=%async_computation | async-start | bytes 1048576 | tf_op jit(solution)/shard_map/all_to_all | solution.py:435
  56.1 1.5 copy-start.3
  57.6 2.3 %copy-start.6 = (f32[1024,128]{1,0:T(8,128)}, f32[1024,128]{1,0:T(8,128)S(1)}, u32[]{:S(2)}) copy-start(f32[1024,128]{1,0:T(8,128)S(1)} %get-tuple-element.267) | copy-start | bytes 1572868
  60.0 12.8 %slice-start = ((f32[1024,512]{1,0:T(8,128)}), f32[1024,256]{1,0:T(8,128)S(1)}, s32[]{:S(2)}) async-start(f32[1024,512]{1,0:T(8,128)} %copy-done.3), calls=%async_computation.1 | async-start | bytes 2097152 | tf_op jit(solution)/shard_map/slice | solution.py:450
  73.4 1.2 copy-start.10
  74.6 1.1 copy-start.7
  90.4 2.0 %copy-start.5 = (f32[16,2,128,128]{3,2,1,0:T(8,128)}, f32[16,2,128,128]{3,2,1,0:T(8,128)S(1)}, u32[]{:S(2)}) copy-start(f32[16,2,128,128]{3,2,1,0:T(8,128)S(1)} %fusion.63) | copy-start | bytes 6291460
  93.7 1.3 copy-start.4
  93.8 1.4 copy-start.8
  95.1 2.1 %slice-start.3 = ((f32[16,2,128,128]{3,2,1,0:T(8,128)}), f32[1,2,128,128]{3,2,1,0:T(8,128)S(1)}, s32[]{:S(2)}) async-start(f32[16,2,128,128]{3,2,1,0:T(8,128)} %copy-done.5), calls=%async_computation.4 | async-start | bytes 262144 | tf_op jit(solution)/shard_map/slice | solution.py:485
  95.1 2.1 %slice-start.1 = ((f32[16,2,128,128]{3,2,1,0:T(8,128)}), f32[1,2,128,128]{3,2,1,0:T(8,128)S(1)}, s32[]{:S(2)}) async-start(f32[16,2,128,128]{3,2,1,0:T(8,128)} %copy-done.4), calls=%async_computation.2 | async-start | bytes 262144 | tf_op jit(solution)/shard_map/slice | solution.py:485
  151.9 2.1 %slice-start.2 = ((f32[16,2,128,128]{3,2,1,0:T(8,128)}), f32[15,2,128,128]{3,2,1,0:T(8,128)S(1)}, s32[]{:S(2)}) async-start(f32[16,2,128,128]{3,2,1,0:T(8,128)} %copy-done.4), calls=%async_computation.3 | async-start | bytes 3932160 | tf_op jit(solution)/shard_map/slice | solution.py:477
  154.0 1.1 copy-start.13
  155.1 1.5 copy-start.2
  156.6 1.2 copy-start.9
  162.1 23.9 %copy-start.1 = (f32[128]{0:T(128)S(1)}, f32[128]{0:T(128)}, u32[]{:S(2)}) copy-start(f32[128]{0:T(128)} %param.21) | copy-start | bytes 1540

commit v12 on v10

--- a/solution.py
+++ b/solution.py
@@ -421,17 +421,14 @@
     norm_gain,
 ):
     parts = lax.axis_size("head")
-    scalars = jnp.concatenate(
-        [
-            log_decay.reshape(log_decay.shape[0], parts, -1),
-            write_strength.reshape(write_strength.shape[0], parts, -1),
-        ],
-        axis=2,
-    ).transpose(1, 0, 2)
+    scalars = (
+        jnp.stack([log_decay, write_strength], axis=-1)
+        .reshape(log_decay.shape[0], parts, -1)
+        .transpose(1, 0, 2)
+    )
     joined, moved_scalars = spread_heads([query_rows, key_rows, value_rows], scalars)
-    moved_scalars = moved_scalars.reshape(-1, moved_scalars.shape[-1])
-    split_at = log_decay.shape[1] // parts
-    local_decay, local_strength = moved_scalars[:, :split_at], moved_scalars[:, split_at:]
+    moved_scalars = moved_scalars.reshape(-1, moved_scalars.shape[-1] // 2, 2)
+    local_decay, local_strength = moved_scalars[..., 0], moved_scalars[..., 1]
     local_gate = lax.all_to_all(gate_rows, "head", split_axis=1, concat_axis=0, tiled=True)
     kernel_width = conv_query.shape[0]
     count_rows = joined.shape[0]

time: 187 us -> 187 us (level)
    unnamed x37 -> x35, local copies, waits for them, and re-layouts: 5.69 us -> 5.69 us
  transfers between devices with their start and end apart: 2 -> 2, of which waited for: 0 -> 0; matrix products, arithmetic and copies ran while one was open for 27% -> 28% of each run, Pallas kernels for 29% -> 29%
where the time goes in v12:
time: 187 us; the launch traced here: 186 us
  Pallas kernels  111 us (59%)
  matrix products  34.5 us (18%)
  local copies, waits for them, and re-layouts  15.9 us (9%)
  other arithmetic  12.7 us (7%)
  starting transfers between devices  10.9 us (6%)
    pallas_call x2, Pallas kernels, head_exchange(): pl.pallas_call(functools.partial(head_exchange_kernel, parts, plan, count...  56.2 us
    pallas_call x1, Pallas kernels, ctx_scan(): pl.pallas_call(functools.partial(ctx_scan_kernel, count), out_shape=jax.S...  54.7 us
    dot_general x29, matrix products, matmul(): return jnp.einsum(spec, left, right, precision=MATMUL_PRECISION)  31.5 us
    all_to_all x1, starting transfers between devices, on_device(): lax.all_to_all(gate_rows, 'head', split_axis=1, concat_axis=0, tiled=True)  6.04 us
    unnamed x35, local copies, waits for them, and re-layouts  5.69 us
    ppermute x1, starting transfers between devices, passed_along(): lax.ppermute(value, axis, [(source, source + steps) for source in range(l...  4.86 us
  transfers between devices with their start and end apart: 2, of which 0 were waited for; matrix products, arithmetic and copies ran while one was open for 28% of the time, Pallas kernels for 29%

profile of v12, /device:TPU:141, one launch (start us, length us, event | category | flops | bytes accessed | tf_op | source)
XLA Modules:
  0.0 186.1 jit_solution(4032031523006156112)
XLA Ops:
  0.0 0.7 pad_maximum_fusion.6
  0.8 0.9 copy.92
  1.7 37.4 %shard_map.100 = (bf16[1024,512]{1,0:T(8,128)(2,1)}, bf16[8,128,4]{2,1,0:T(8,128)(2,1)}) custom-call(bf16[128,1024]{1,0:T(8,128)(2,1)} %refs_0_.1, bf16[128,1024]{1,0:T(8,128)(2,1)} %refs_1_.1, bf16[128,2048]{1,0:T(8,128)(2,1)} %refs_2_.1, bf16[8,128,4]{2,1,0:T(8,128)(2,1)} %bitcast.151), custom_call_target="tpu_custom_call" | custom-call | tf_op jit(solution)/shard_map/pallas_call | solution.py:357
  39.1 0.8 slice.86
  39.9 4.9 %collective-permute-start = (bf16[3,512]{1,0:T(4,128)(2,1)S(1)}, bf16[3,512]{1,0:T(4,128)(2,1)S(1)}, u32[]{:S(2)}, u32[]{:S(2)}) collective-permute-start(bf16[3,512]{1,0:T(4,128)(2,1)S(1)} %slice.86), channel_id=1, source_target_pairs={{0,8},{8,16},{16,24},{24,32},{32,40},{40,48},{48,56},{56,64},{64,7... | collective-permute-start | bytes 9224 | tf_op jit(solution)/shard_map/ppermute | solution.py:25
  44.8 1.9 %copy.131 = bf16[16,8,8,256]{3,2,0,1:T(8,128)(2,1)} copy(bf16[16,8,8,256]{3,2,1,0:T(8,128)(2,1)} %bitcast.152) | data formatting | bytes 1048576 | tf_op jit(solution)/shard_map/all_to_all | solution.py:432
  46.7 6.0 %all-to-all-start = ((bf16[128,8,256]{2,0,1:T(8,128)(2,1)}), bf16[128,8,256]{2,0,1:T(8,128)(2,1)}, u32[]{:S(2)}, u32[]{:S(2)}) async-start(bf16[128,8,256]{2,0,1:T(8,128)(2,1)} %bitcast.123), calls=%async_computation | async-start | bytes 1048576 | tf_op jit(solution)/shard_map/all_to_all | solution.py:432
  53.1 0.4 reduce_window_sum.11
  54.1 1.4 divide_multiply_fusion
  55.6 0.3 multiply_reduce_fusion.2
  56.0 1.1 divide_multiply_fusion.1
  57.1 1.3 broadcast_multiply_fusion
  58.4 1.0 fusion.87
  59.5 13.4 %while.18 = (s32[]{:T(128)}, f32[16,2,64,64]{2,3,1,0:T(8,128)S(1)}, f32[16,2,64,64]{3,2,1,0:T(8,128)S(1)}, s32[]{:T(128)}, s32[]{:T(128)}) while((s32[]{:T(128)}, f32[16,2,64,64]{2,3,1,0:T(8,128)S(1)}, f32[16,2,64,64]{3,2,1,0:T(8,128)S(1)}, s32[]{:T(128)}, s32[]{:T(128)}) %tuple.62), condition=%wide.region_4.5_spmd.clone.clone, body=%wide.region_3.4_spmd.clone.clone.sunk | while | flops 100941312 | bytes 4728181 | solution.py:50
  59.9 0.9 fusion.158
  60.9 0.6 convolution_bitcast_fusion.3
  61.5 0.3 sub.126
  62.1 0.9 fusion.158
  63.1 0.6 convolution_bitcast_fusion.3
  63.7 0.3 sub.126
  64.3 0.9 fusion.158
  65.3 0.6 convolution_bitcast_fusion.3
  65.9 0.3 sub.126
  66.5 0.9 fusion.158
  67.5 0.6 convolution_bitcast_fusion.3
  68.1 0.3 sub.126
  68.7 0.9 fusion.158
  69.7 0.6 convolution_bitcast_fusion.3
  70.3 0.3 sub.126
  71.0 0.9 fusion.158
  71.9 0.6 convolution_bitcast_fusion.3
  72.5 0.3 sub.126
  73.0 0.5 reshape_reshape.2
  73.5 0.3 bitcast_multiply_fusion.1
  73.9 0.9 copy-done.10
  74.8 1.1 fusion.23
  75.9 2.2 %fusion.65 = f32[16,2,128,128]{3,2,1,0:T(8,128)S(1)} fusion(f32[16,2,64,256]{3,2,1,0:T(8,128)S(1)} %fusion.23, f32[16,64,128]{2,1,0:T(8,128)S(1)} %bitcast.142, f32[16,2,64]{2,1,0:T(2,128)S(1)} %copy.96), kind=kOutput, calls=%fused_computation.79 | convolution fusion | flops 201588736 | bytes 3686400 | tf_op jit(solution)/shard_map/nhcd,nhce->nhde/dot_general | solution.py:29
  78.3 2.3 %multiply_subtract_fusion = f32[16,2,128,128]{3,2,1,0:T(8,128)S(1)} fusion(f32[128,128]{1,0:T(8,128)S(1)} %fusion.110, f32[16,2]{1,0:T(8,128)S(1)} %copy.95, f32[16,2,64,256]{3,2,1,0:T(8,128)S(1)} %fusion.23, f32[16,64,128]{2,1,0:T(8,128)S(1)} %bitcast.143, f32[16,2,64]{2,1,0:T(2,128)S(1)} %copy.96), kind=kOutput, calls=%fused_computation.69 | convolution fusion | flops 202637312 | bytes 3760128 | tf_op jit(solution)/shard_map/nhcd,nhce->nhde/dot_general | solution.py:29
  80.8 1.3 fusion.53
  82.3 1.2 fusion.21
  83.7 1.2 fusion.56
  85.1 1.2 fusion.28
  86.5 1.5 fusion.59
  88.1 1.2 fusion.32
  89.4 1.2 fusion.62
  90.5 1.7 slice.135
  92.2 0.3 copy-done.5
  92.7 1.2 fusion.36
  93.9 1.3 copy-done.4
  95.4 2.0 %convolution_multiply_fusion = f32[16,2,64,64]{3,2,1,0:T(8,128)} fusion(f32[16,2,64]{2,1,0:T(2,128)S(1)} %copy.98, f32[16,64,128]{2,1,0:T(8,128)S(1)} %bitcast.144, f32[16,64,128]{2,1,0:T(8,128)S(1)} %bitcast.145, pred[64,64]{1,0:T(8,128)(4,1)S(1)} %get-tuple-element.281), kind=kOutput, calls=%fused_computation.91 | convolution fusion | flops 101187584 | bytes 1585152 | tf_op jit(solution)/shard_map/nhid,nhjd->nhij/dot_general | solution.py:108
  97.3 0.7 pad_maximum_fusion.5.maps_ref
  98.0 54.7 %shard_map.101 = f32[2,128,128]{2,1,0:T(8,128)} custom-call(f32[2,2,128,128]{3,2,1,0:T(8,128)} %pad_maximum_fusion.5.maps_ref), custom_call_target="tpu_custom_call" | custom-call | tf_op jit(solution)/shard_map/pallas_call | solution.py:290
  152.8 2.0 %multiply_subtract_fusion.1 = f32[16,2,64,128]{3,2,1,0:T(8,128)S(1)} fusion(f32[16,2,64,64]{3,2,1,0:T(8,128)} %convolution_multiply_fusion, f32[16,2,64,256]{3,2,1,0:T(8,128)S(1)} %fusion.23, f32[16,64,128]{2,1,0:T(8,128)S(1)} %bitcast.146, f32[16,2,64]{2,1,0:T(2,128)S(1)} %copy.94), kind=kOutput, calls=%fused_computation.82 | convolution fusion | flops 101187584 | bytes 3162112 | tf_op jit(solution)/shard_map/nhij,nhjd->nhid/dot_general | solution.py:29
  154.8 1.1 fusion.22
  155.9 0.6 convolution_bitcast_fusion.1
  156.5 1.0 copy-done.2
  157.5 1.0 fusion.84
  158.7 0.7 fusion.129
  159.3 1.3 multiply_reduce_fusion
  160.9 0.8 copy.107
  161.7 1.2 div.135
  163.0 2.4 %fusion.92.refs_0_ = bf16[1024,256]{1,0:T(8,128)(2,1)} fusion(f32[128,8,2,128]{3,2,1,0:T(2,128)S(1)} %bitcast.149, f32[128,8,2,128]{3,2,1,0:T(2,128)S(1)} %bitcast.148, bf16[128,8,256]{2,0,1:T(8,128)(2,1)} %all-to-all-done, f32[256]{0:T(256)S(1)} %broadcast_bitcast_fusion), kind=kLoop, calls=%fused_computation.99 | loop fusion | flops 2359296 | bytes 3146752 | tf_op jit(solution)/shard_map/convert_element_type | solution.py:133
  165.4 18.8 %shard_map.102 = bf16[128,2048]{1,0:T(8,128)(2,1)} custom-call(bf16[1024,256]{1,0:T(8,128)(2,1)} %fusion.92.refs_0_), custom_call_target="tpu_custom_call" | custom-call | tf_op jit(solution)/shard_map/pallas_call | solution.py:357
  184.2 1.9 %copy.141 = bf16[128,2048]{1,0:T(8,128)(2,1)} copy(bf16[128,2048]{1,0:T(8,128)(2,1)} %shard_map.102) | data formatting | bytes 1048576
  (95 shorter events, 5.0 us)
Async XLA Ops:
  0.0 53.8 %copy-start = (f32[128]{0:T(128)S(1)}, f32[128]{0:T(128)}, u32[]{:S(2)}) copy-start(f32[128]{0:T(128)} %param.21) | copy-start | bytes 1540
  0.0 52.8 %copy-start.16 = (bf16[4,128]{1,0:T(4,128)(2,1)S(1)}, bf16[4,128]{1,0:T(4,128)(2,1)}, u32[]{:S(2)}) copy-start(bf16[4,128]{1,0:T(4,128)(2,1)} %param.18) | copy-start | bytes 3076
  0.0 52.8 %copy-start.15 = (bf16[4,128]{1,0:T(4,128)(2,1)S(1)}, bf16[4,128]{1,0:T(4,128)(2,1)}, u32[]{:S(2)}) copy-start(bf16[4,128]{1,0:T(4,128)(2,1)} %param.19) | copy-start | bytes 3076
  0.0 52.8 %copy-start.14 = (bf16[4,256]{1,0:T(4,128)(2,1)S(1)}, bf16[4,256]{1,0:T(4,128)(2,1)}, u32[]{:S(2)}) copy-start(bf16[4,256]{1,0:T(4,128)(2,1)} %param.20) | copy-start | bytes 6148
  39.1 13.7 %copy-start.13 = (bf16[8,128,4]{2,1,0:T(8,128)(2,1)S(1)}, bf16[8,128,4]{2,1,0:T(8,128)(2,1)}, u32[]{:S(2)}) copy-start(bf16[8,128,4]{2,1,0:T(8,128)(2,1)} %get-tuple-element.209) | copy-start | bytes 24580
  39.1 15.0 %copy-start.11 = (bf16[1024,512]{1,0:T(8,128)(2,1)S(1)}, bf16[1024,512]{1,0:T(8,128)(2,1)}, u32[]{:S(2)}) copy-start(bf16[1024,512]{1,0:T(8,128)(2,1)} %get-tuple-element.210) | copy-start | bytes 3145732
  39.9 14.2 %collective-permute-start = (bf16[3,512]{1,0:T(4,128)(2,1)S(1)}, bf16[3,512]{1,0:T(4,128)(2,1)S(1)}, u32[]{:S(2)}, u32[]{:S(2)}) collective-permute-start(bf16[3,512]{1,0:T(4,128)(2,1)S(1)} %slice.86), channel_id=1, source_target_pairs={{0,8},{8,16},{16,24},{24,32},{32,40},{40,48},{48,56},{56,64},{64,7... | collective-permute-start | bytes 9224 | tf_op jit(solution)/shard_map/ppermute | solution.py:25
  46.7 115.0 %all-to-all-start = ((bf16[128,8,256]{2,0,1:T(8,128)(2,1)}), bf16[128,8,256]{2,0,1:T(8,128)(2,1)}, u32[]{:S(2)}, u32[]{:S(2)}) async-start(bf16[128,8,256]{2,0,1:T(8,128)(2,1)} %bitcast.123), calls=%async_computation | async-start | bytes 1048576 | tf_op jit(solution)/shard_map/all_to_all | solution.py:432
  55.6 1.5 copy-start.3
  57.1 2.3 %copy-start.6 = (f32[1024,128]{1,0:T(8,128)}, f32[1024,128]{1,0:T(8,128)S(1)}, u32[]{:S(2)}) copy-start(f32[1024,128]{1,0:T(8,128)S(1)} %get-tuple-element.269) | copy-start | bytes 1572868
  59.5 13.5 %slice-start = ((f32[1024,512]{1,0:T(8,128)}), f32[1024,256]{1,0:T(8,128)S(1)}, s32[]{:S(2)}) async-start(f32[1024,512]{1,0:T(8,128)} %copy-done.3), calls=%async_computation.1 | async-start | bytes 2097152 | tf_op jit(solution)/shard_map/slice | solution.py:447
  73.5 1.2 copy-start.10
  74.8 1.1 copy-start.7
  90.5 2.0 %copy-start.5 = (f32[16,2,128,128]{3,2,1,0:T(8,128)}, f32[16,2,128,128]{3,2,1,0:T(8,128)S(1)}, u32[]{:S(2)}) copy-start(f32[16,2,128,128]{3,2,1,0:T(8,128)S(1)} %fusion.62) | copy-start | bytes 6291460
  93.9 1.3 copy-start.4
  93.9 1.4 copy-start.8
  95.3 2.1 %slice-start.3 = ((f32[16,2,128,128]{3,2,1,0:T(8,128)}), f32[1,2,128,128]{3,2,1,0:T(8,128)S(1)}, s32[]{:S(2)}) async-start(f32[16,2,128,128]{3,2,1,0:T(8,128)} %copy-done.5), calls=%async_computation.4 | async-start | bytes 262144 | tf_op jit(solution)/shard_map/slice | solution.py:482
  95.3 2.1 %slice-start.1 = ((f32[16,2,128,128]{3,2,1,0:T(8,128)}), f32[1,2,128,128]{3,2,1,0:T(8,128)S(1)}, s32[]{:S(2)}) async-start(f32[16,2,128,128]{3,2,1,0:T(8,128)} %copy-done.4), calls=%async_computation.2 | async-start | bytes 262144 | tf_op jit(solution)/shard_map/slice | solution.py:482
  152.7 2.1 %slice-start.2 = ((f32[16,2,128,128]{3,2,1,0:T(8,128)}), f32[15,2,128,128]{3,2,1,0:T(8,128)S(1)}, s32[]{:S(2)}) async-start(f32[16,2,128,128]{3,2,1,0:T(8,128)} %copy-done.4), calls=%async_computation.3 | async-start | bytes 3932160 | tf_op jit(solution)/shard_map/slice | solution.py:474
  154.8 1.1 copy-start.12
  155.9 1.5 copy-start.2
  157.5 1.2 copy-start.9
  163.0 23.1 %copy-start.1 = (f32[128]{0:T(128)S(1)}, f32[128]{0:T(128)}, u32[]{:S(2)}) copy-start(f32[128]{0:T(128)} %param.21) | copy-start | bytes 1540
